TPU v7x, 32 devices: a whole 2x2x4 slice. The times are simulated.
32 devices in a mesh: dp: 8 (over z, y), tensor: 4 (over x, core).
Axes of the slice: x: 2, y: 2, z: 4, core: 2. Of those that a mesh axis runs over, the one named last changes fastest.
Arguments:
- layer_in: bfloat16 [8192, 1024], P(('dp', 'tensor')), may hold values from -6 to 6
- norm_gain: float32 [6, 1024], replicated, may hold values from 0.25 to 1.75
- norm_shift: float32 [6, 1024], replicated, may hold values from -2.5 to 2.5
- early_up: bfloat16 [1024, 4096], P('dp', 'tensor'), may hold values from -0.1875 to 0.1875
- early_down: bfloat16 [4096, 1024], P('tensor', 'dp'), may hold values from -0.09375 to 0.09375
- attend_in: bfloat16 [3, 1024, 1024], P(None, 'dp', 'tensor'), may hold values from -0.1875 to 0.1875
- attend_out: bfloat16 [1024, 1024], P('tensor', 'dp'), may hold values from -0.75 to 0.75
- position_table: bfloat16 [73, 64], replicated, may hold values from -4 to 4
- pointwise_in: bfloat16 [1024, 2, 1024], P('dp', None, 'tensor'), may hold values from -0.1875 to 0.1875
- depthwise: bfloat16 [31, 1024], P(None, 'tensor'), may hold values from -1 to 1
- pointwise_out: bfloat16 [1024, 1024], P('tensor', 'dp'), may hold values from -0.1875 to 0.1875
- late_up: bfloat16 [1024, 4096], P('dp', 'tensor'), may hold values from -0.1875 to 0.1875
- late_down: bfloat16 [4096, 1024], P('tensor', 'dp'), may hold values from -0.09375 to 0.09375
- output_grad: bfloat16 [8192, 1024], P(('dp', 'tensor')), may hold values from -6 to 6
- clip_lengths: int32 [16], replicated, may hold values from 128 to 512, as said below
- clip_slots: int32 [16], replicated, may hold values from 0 to 15, each once
- position_rows: int32 [73], replicated, may hold values from 0 to 72, each once
Outputs:
- layer_out: bfloat16 [8192, 1024], P(('dp', 'tensor'))
- input_grad: float32 [8192, 1024], P(('dp', 'tensor'))
- grad_norm_gain: float32 [6, 1024], replicated
- grad_norm_shift: float32 [6, 1024], replicated
- grad_early_up: float32 [1024, 4096], P('dp', 'tensor')
- grad_early_down: float32 [4096, 1024], P('tensor', 'dp')
- grad_attend_in: float32 [3, 1024, 1024], P(None, 'dp', 'tensor')
- grad_attend_out: float32 [1024, 1024], P('tensor', 'dp')
- grad_position_table: float32 [73, 64], replicated
- grad_pointwise_in: float32 [1024, 2, 1024], P('dp', None, 'tensor')
- grad_depthwise: float32 [31, 1024], replicated
- grad_pointwise_out: float32 [1024, 1024], P('tensor', 'dp')
- grad_late_up: float32 [1024, 4096], P('dp', 'tensor')
- grad_late_down: float32 [4096, 1024], P('tensor', 'dp')
Inputs may be any that keep to these rules, and one draw needn't show every extreme that they name: `clip_lengths`: some clip has exactly 512 frames and some exactly 128. `clip_slots`: each slot number once. `position_rows`: each row of position_table once.
All inputs are finite; a program needn't handle non-finite values.
Results may differ from a plain program's by a relative error of at most 0.029.
Values may be sent and summed in bfloat16 or wider, within the bound.
No kernel may reach another device: no remote copies, remote signals or barrier semaphores. Data moves between devices by JAX's collectives and lax.ppermute only.
A program may use at most 192 MiB of HBM per device.

v0:
```python
import jax
import jax.numpy as jnp
from jax import lax
from jax.sharding import PartitionSpec as P

D = 1024
HEAD_DIM = 64
KERNEL = 31
REL_LEFT = 64
REL_RIGHT = 8
CLIP_DEV = 2
L = 512
RELS = 73


norm_eps = 1e-05
masked_score = -1e30
highest = lax.Precision.HIGHEST


def matmul(left_op, right_op):
    return jnp.dot(left_op, right_op, preferred_element_type=jnp.float32)


def matmul_tn(left_op, right_op):
    return lax.dot_general(
        left_op, right_op, (((0,), (0,)), ((), ())), preferred_element_type=jnp.float32
    )


def matmul_nt(left_op, right_op):
    return lax.dot_general(
        left_op, right_op, (((1,), (1,)), ((), ())), preferred_element_type=jnp.float32
    )


def swish(operand):
    return operand * jax.nn.sigmoid(operand)


def swish_grad(operand):
    logistic = jax.nn.sigmoid(operand)
    return logistic * (1.0 + operand * (1.0 - logistic))


def norm_forward(operand, gain_vec, shift_vec):
    centre = operand - jnp.mean(operand, axis=-1, keepdims=True)
    spread = jnp.mean(centre * centre, axis=-1, keepdims=True)
    scale_inv = lax.rsqrt(spread + norm_eps)
    standard = centre * scale_inv
    return (standard * gain_vec + shift_vec, standard, scale_inv)


def norm_backward(upstream, standard, scale_inv, gain_vec):
    scaled = upstream * gain_vec
    bracket = (
        scaled
        - jnp.mean(scaled, axis=-1, keepdims=True)
        - standard * jnp.mean(scaled * standard, axis=-1, keepdims=True)
    )
    return (scale_inv * bracket, jnp.sum(upstream * standard, axis=0), jnp.sum(upstream, axis=0))


def frames_gather(normed):
    return lax.all_gather(normed.astype(jnp.bfloat16), "tensor", axis=0, tiled=True)


def frames_reduce(row_term, rows_here):
    return lax.psum_scatter(
        row_term(jnp.int32(0), rows_here * lax.axis_size("tensor")).astype(jnp.bfloat16),
        "tensor",
        scatter_dimension=0,
        tiled=True,
    ).astype(jnp.float32)


def grads_gather(upstream):
    return lax.all_gather(upstream.astype(jnp.bfloat16), "tensor", axis=0, tiled=True)


def grads_reduce(row_term, rows_here):
    return lax.psum_scatter(
        row_term(jnp.int32(0), rows_here * lax.axis_size("tensor")).astype(jnp.bfloat16),
        "tensor",
        scatter_dimension=0,
        tiled=True,
    ).astype(jnp.float32)


def ffn_forward(stream, gain_vec, shift_vec, weight_up, weight_down):
    normed, standard, scale_inv = norm_forward(stream, gain_vec, shift_vec)
    gathered = frames_gather(normed)
    hidden = matmul(gathered, weight_up)
    active = swish(hidden).astype(jnp.bfloat16)

    def down_rows(row_start, row_count):
        return matmul(active, weight_down)

    branch = frames_reduce(down_rows, stream.shape[0])
    return (stream + 0.5 * branch, (standard, scale_inv, gathered, hidden, active))


def ffn_backward(upstream, gain_vec, weight_up, weight_down, saved):
    standard, scale_inv, gathered, hidden, active = saved
    incoming = grads_gather(upstream)
    grad_down = 0.5 * matmul_tn(active, incoming)
    grad_hidden = (0.5 * matmul_nt(incoming, weight_down) * swish_grad(hidden)).astype(jnp.bfloat16)
    grad_up = matmul_tn(gathered, grad_hidden)

    def up_rows(row_start, row_count):
        return matmul_nt(grad_hidden, weight_up)

    grad_normed = grads_reduce(up_rows, upstream.shape[0])
    grad_stream, grad_gain, grad_shift = norm_backward(grad_normed, standard, scale_inv, gain_vec)
    return (upstream + grad_stream, grad_up, grad_down, grad_gain, grad_shift)


def block_scores(query_blk, key_rows, table_dist, clip_len, offset):
    direct = jnp.einsum("cihd,cjhd->chij", query_blk, key_rows, preferred_element_type=jnp.float32)
    by_dist = jnp.einsum("cihd,rd->chir", query_blk, table_dist, preferred_element_type=jnp.float32)
    query_pos = offset + jnp.arange(query_blk.shape[1], dtype=jnp.int32)
    key_pos = jnp.arange(key_rows.shape[1], dtype=jnp.int32)
    distance = jnp.clip(key_pos[None, :] - query_pos[:, None], -REL_LEFT, REL_RIGHT) + REL_LEFT
    band_table = (distance[None, :, :] == jnp.arange(RELS, dtype=jnp.int32)[:, None, None]).astype(
        jnp.float32
    )
    relative = jnp.einsum("chir,rij->chij", by_dist, band_table, precision=highest)
    live_keys = key_pos[None, :] < clip_len[:, None]
    scores = (direct + relative) * HEAD_DIM ** (-0.5)
    scores = jnp.where(live_keys[:, None, None, :], scores, masked_score)
    return (scores, band_table)


def attention_forward(stream, gain_vec, shift_vec, weight_in, weight_out, table_dist, clip_len):
    normed, standard, scale_inv = norm_forward(stream, gain_vec, shift_vec)
    gathered = frames_gather(normed)
    heads_here = weight_in.shape[2] // HEAD_DIM
    packed = jnp.einsum(
        "td,gdc->gtc", gathered, weight_in, preferred_element_type=jnp.float32
    ).astype(jnp.bfloat16)
    shaped = packed.reshape(3, CLIP_DEV, L, heads_here, HEAD_DIM)
    block_rows = min(L, 256)
    outputs = []
    log_totals = []
    for offset in range(0, L, block_rows):
        scores, band_table = block_scores(
            shaped[0][:, offset : offset + block_rows], shaped[1], table_dist, clip_len, offset
        )
        top_score = jnp.max(scores, axis=-1, keepdims=True)
        raised = jnp.exp(scores - top_score)
        totals = jnp.sum(raised, axis=-1, keepdims=True)
        shares = (raised / totals).astype(jnp.bfloat16)
        outputs.append(
            jnp.einsum(
                "chij,cjhd->cihd", shares, shaped[2], preferred_element_type=jnp.float32
            ).astype(jnp.bfloat16)
        )
        log_totals.append(top_score + jnp.log(totals))
    attended = jnp.concatenate(outputs, axis=1).reshape(CLIP_DEV * L, heads_here * HEAD_DIM)

    def attention_out_rows(row_start, row_count):
        return matmul(attended, weight_out)

    branch = frames_reduce(attention_out_rows, stream.shape[0])
    return (stream + branch, (standard, scale_inv, gathered, shaped, attended, log_totals))


def attention_backward(upstream, gain_vec, weight_in, weight_out, table_dist, clip_len, saved):
    standard, scale_inv, gathered, shaped, attended, log_totals = saved
    heads_here = weight_in.shape[2] // HEAD_DIM
    score_scale = HEAD_DIM ** (-0.5)
    incoming = grads_gather(upstream)
    grad_out = matmul_tn(attended, incoming)
    grad_att = (
        matmul_nt(incoming, weight_out)
        .astype(jnp.bfloat16)
        .reshape(CLIP_DEV, L, heads_here, HEAD_DIM)
    )
    queries, key_rows, values = (shaped[0], shaped[1], shaped[2])
    table_wide = table_dist.astype(jnp.float32)
    grad_keys = jnp.zeros(key_rows.shape, jnp.float32)
    grad_values = jnp.zeros(values.shape, jnp.float32)
    grad_table = jnp.zeros(table_dist.shape, jnp.float32)
    query_parts = []
    block_rows = min(L, 256)
    for number, offset in enumerate(range(0, L, block_rows)):
        query_blk = queries[:, offset : offset + block_rows]
        grad_blk = grad_att[:, offset : offset + block_rows]
        scores, band_table = block_scores(query_blk, key_rows, table_dist, clip_len, offset)
        shares = jnp.exp(scores - log_totals[number])
        grad_values = grad_values + jnp.einsum(
            "chij,cihd->cjhd",
            shares.astype(jnp.bfloat16),
            grad_blk,
            preferred_element_type=jnp.float32,
        )
        grad_shares = jnp.einsum(
            "cihd,cjhd->chij", grad_blk, values, preferred_element_type=jnp.float32
        )
        centred = jnp.sum(shares * grad_shares, axis=-1, keepdims=True)
        grad_scores = (shares * (grad_shares - centred)).astype(jnp.bfloat16)
        grad_query = (
            jnp.einsum("chij,cjhd->cihd", grad_scores, key_rows, preferred_element_type=jnp.float32)
            * score_scale
        )
        grad_keys = (
            grad_keys
            + jnp.einsum(
                "chij,cihd->cjhd", grad_scores, query_blk, preferred_element_type=jnp.float32
            )
            * score_scale
        )
        pulled = jnp.einsum(
            "chij,rij->chir",
            grad_scores.astype(jnp.float32) * score_scale,
            band_table,
            precision=highest,
        )
        grad_query = grad_query + jnp.einsum("chir,rd->cihd", pulled, table_wide, precision=highest)
        grad_table = grad_table + jnp.einsum(
            "chir,cihd->rd", pulled, query_blk.astype(jnp.float32), precision=highest
        )
        query_parts.append(grad_query)
    grad_packed = (
        jnp.stack([jnp.concatenate(query_parts, axis=1), grad_keys, grad_values])
        .astype(jnp.bfloat16)
        .reshape(3, CLIP_DEV * L, heads_here * HEAD_DIM)
    )
    grad_in = jnp.einsum("td,gtc->gdc", gathered, grad_packed, preferred_element_type=jnp.float32)

    def attention_in_rows(row_start, row_count):
        return jnp.einsum("gtc,gdc->td", grad_packed, weight_in, preferred_element_type=jnp.float32)

    grad_normed = grads_reduce(attention_in_rows, upstream.shape[0])
    grad_stream, grad_gain, grad_shift = norm_backward(grad_normed, standard, scale_inv, gain_vec)
    return (upstream + grad_stream, grad_in, grad_out, grad_table, grad_gain, grad_shift)


def conv_forward(
    stream, gain_vec, shift_vec, weight_in, kernel_taps, weight_out, channel_gain, channel_shift
):
    normed, standard, scale_inv = norm_forward(stream, gain_vec, shift_vec)
    gathered = frames_gather(normed)
    halves = jnp.einsum("td,dgc->tgc", gathered, weight_in, preferred_element_type=jnp.float32)
    linear_half = halves[:, 0]
    gate_open = jax.nn.sigmoid(halves[:, 1])
    channels = linear_half.shape[1]
    padded = jnp.pad(
        (linear_half * gate_open).reshape(CLIP_DEV, L, channels), ((0, 0), (KERNEL - 1, 0), (0, 0))
    )
    tap_values = kernel_taps.astype(jnp.float32)
    convolved = tap_values[0] * padded[:, 0:L]
    for offset in range(1, KERNEL):
        convolved = convolved + tap_values[offset] * padded[:, offset : offset + L]
    convolved = convolved.reshape(CLIP_DEV * L, channels)
    channel_mean = lax.psum(jnp.sum(convolved, axis=-1), "tensor")[:, None] / D
    centre = convolved - channel_mean
    channel_var = lax.psum(jnp.sum(centre * centre, axis=-1), "tensor")[:, None] / D
    channel_inv = lax.rsqrt(channel_var + norm_eps)
    channel_unit = centre * channel_inv
    normed_conv = channel_unit * channel_gain + channel_shift
    active = swish(normed_conv).astype(jnp.bfloat16)

    def conv_out_rows(row_start, row_count):
        return matmul(active, weight_out)

    branch = frames_reduce(conv_out_rows, stream.shape[0])
    return (
        stream + branch,
        (
            standard,
            scale_inv,
            gathered,
            linear_half,
            gate_open,
            padded,
            channel_unit,
            channel_inv,
            normed_conv,
            active,
        ),
    )


def conv_backward(upstream, gain_vec, weight_in, kernel_taps, weight_out, channel_gain, saved):
    (
        standard,
        scale_inv,
        gathered,
        linear_half,
        gate_open,
        padded,
        channel_unit,
        channel_inv,
        normed_conv,
        active,
    ) = saved
    channels = linear_half.shape[1]
    incoming = grads_gather(upstream)
    grad_out = matmul_tn(active, incoming)
    grad_mid = matmul_nt(incoming, weight_out) * swish_grad(normed_conv)
    grad_cgain = jnp.sum(grad_mid * channel_unit, axis=0)
    grad_cshift = jnp.sum(grad_mid, axis=0)
    scaled = grad_mid * channel_gain
    sum_scaled, sum_cross = lax.psum(
        (jnp.sum(scaled, axis=-1), jnp.sum(scaled * channel_unit, axis=-1)), "tensor"
    )
    grad_conv = channel_inv * (
        scaled - sum_scaled[:, None] / D - channel_unit * sum_cross[:, None] / D
    )
    grad_grid = grad_conv.reshape(CLIP_DEV, L, channels)
    padded_grad = jnp.pad(grad_grid, ((0, 0), (0, KERNEL - 1), (0, 0)))
    tap_values = kernel_taps.astype(jnp.float32)
    grad_gated = tap_values[0] * padded_grad[:, KERNEL - 1 : KERNEL - 1 + L]
    for offset in range(1, KERNEL):
        grad_gated = (
            grad_gated
            + tap_values[offset] * padded_grad[:, KERNEL - 1 - offset : KERNEL - 1 - offset + L]
        )
    grad_taps = jnp.stack(
        [
            jnp.sum(padded[:, offset : offset + L] * grad_grid, axis=(0, 1))
            for offset in range(KERNEL)
        ]
    )
    grad_gated = grad_gated.reshape(CLIP_DEV * L, channels)
    grad_linear = grad_gated * gate_open
    grad_gate = grad_gated * linear_half * gate_open * (1.0 - gate_open)
    grad_halves = jnp.stack([grad_linear, grad_gate], axis=1).astype(jnp.bfloat16)
    grad_in = jnp.einsum("td,tgc->dgc", gathered, grad_halves, preferred_element_type=jnp.float32)

    def conv_in_rows(row_start, row_count):
        return jnp.einsum("tgc,dgc->td", grad_halves, weight_in, preferred_element_type=jnp.float32)

    grad_normed = grads_reduce(conv_in_rows, upstream.shape[0])
    grad_stream, grad_gain, grad_shift = norm_backward(grad_normed, standard, scale_inv, gain_vec)
    return (
        upstream + grad_stream,
        grad_in,
        grad_taps,
        grad_out,
        grad_gain,
        grad_shift,
        grad_cgain,
        grad_cshift,
    )


def spread_channels(partial_rows, member):
    zero_fill = jnp.zeros(partial_rows.shape[:-1] + (D,), jnp.float32)
    return lax.dynamic_update_slice_in_dim(
        zero_fill, partial_rows, member * partial_rows.shape[-1], partial_rows.ndim - 1
    )


def per_device(
    layer_in,
    norm_gain,
    norm_shift,
    early_up,
    early_down,
    attend_in,
    attend_out,
    position_table,
    pointwise_in,
    depthwise,
    pointwise_out,
    late_up,
    late_down,
    output_grad,
    clip_lengths,
    clip_slots,
    position_rows,
):
    group_index = lax.axis_index("dp")
    member = lax.axis_index("tensor")
    rows_here = layer_in.shape[0]
    channels = depthwise.shape[1]
    slot_ids = group_index * CLIP_DEV + jnp.arange(CLIP_DEV, dtype=jnp.int32)
    clip_len = jnp.sum(
        jnp.where(clip_slots[None, :] == slot_ids[:, None], clip_lengths[None, :], 0), axis=1
    )
    frame_ids = member * rows_here + jnp.arange(rows_here, dtype=jnp.int32)
    frame_len = jnp.sum(
        jnp.where(
            (frame_ids // L)[:, None] == jnp.arange(CLIP_DEV, dtype=jnp.int32)[None, :],
            clip_len[None, :],
            0,
        ),
        axis=1,
    )
    frame_live = frame_ids % L < frame_len
    selector = (position_rows[:, None] == jnp.arange(RELS, dtype=jnp.int32)[None, :]).astype(
        jnp.float32
    )
    table_dist = jnp.dot(selector, position_table.astype(jnp.float32), precision=highest).astype(
        jnp.bfloat16
    )
    channel_gain = lax.dynamic_slice_in_dim(norm_gain[3], member * channels, channels)
    channel_shift = lax.dynamic_slice_in_dim(norm_shift[3], member * channels, channels)
    weights = (
        lax.all_gather(early_up, "dp", axis=0, tiled=True),
        lax.all_gather(early_down, "dp", axis=1, tiled=True),
        lax.all_gather(attend_in, "dp", axis=1, tiled=True),
        lax.all_gather(attend_out, "dp", axis=1, tiled=True),
        lax.all_gather(pointwise_in, "dp", axis=0, tiled=True),
        lax.all_gather(pointwise_out, "dp", axis=1, tiled=True),
        lax.all_gather(late_up, "dp", axis=0, tiled=True),
        lax.all_gather(late_down, "dp", axis=1, tiled=True),
    )
    stream_zero = layer_in.astype(jnp.float32)
    stream_one, saved_early = ffn_forward(
        stream_zero, norm_gain[0], norm_shift[0], weights[0], weights[1]
    )
    stream_two, saved_attend = attention_forward(
        stream_one, norm_gain[1], norm_shift[1], weights[2], weights[3], table_dist, clip_len
    )
    stream_three, saved_conv = conv_forward(
        stream_two,
        norm_gain[2],
        norm_shift[2],
        weights[4],
        depthwise,
        weights[5],
        channel_gain,
        channel_shift,
    )
    stream_four, saved_late = ffn_forward(
        stream_three, norm_gain[4], norm_shift[4], weights[6], weights[7]
    )
    result, final_unit, final_inv = norm_forward(stream_four, norm_gain[5], norm_shift[5])
    back_weights = (
        lax.all_gather(early_up, "dp", axis=0, tiled=True),
        lax.all_gather(early_down, "dp", axis=1, tiled=True),
        lax.all_gather(attend_in, "dp", axis=1, tiled=True),
        lax.all_gather(attend_out, "dp", axis=1, tiled=True),
        lax.all_gather(pointwise_in, "dp", axis=0, tiled=True),
        lax.all_gather(pointwise_out, "dp", axis=1, tiled=True),
        lax.all_gather(late_up, "dp", axis=0, tiled=True),
        lax.all_gather(late_down, "dp", axis=1, tiled=True),
    )
    upstream = jnp.where(frame_live[:, None], output_grad.astype(jnp.float32), 0.0)
    upstream, gain_five, shift_five = norm_backward(upstream, final_unit, final_inv, norm_gain[5])
    upstream, grad_late_up, grad_late_down, gain_four, shift_four = ffn_backward(
        upstream, norm_gain[4], back_weights[6], back_weights[7], saved_late
    )
    (
        upstream,
        grad_point_in,
        grad_taps,
        grad_point_out,
        gain_two,
        shift_two,
        gain_three,
        shift_three,
    ) = conv_backward(
        upstream,
        norm_gain[2],
        back_weights[4],
        depthwise,
        back_weights[5],
        channel_gain,
        saved_conv,
    )
    upstream, grad_att_in, grad_att_out, grad_table_dist, gain_one, shift_one = attention_backward(
        upstream, norm_gain[1], back_weights[2], back_weights[3], table_dist, clip_len, saved_attend
    )
    upstream, grad_early_up, grad_early_down, gain_zero, shift_zero = ffn_backward(
        upstream, norm_gain[0], back_weights[0], back_weights[1], saved_early
    )
    all_sums = (
        lax.psum_scatter(grad_early_up, "dp", scatter_dimension=0, tiled=True),
        lax.psum_scatter(grad_early_down, "dp", scatter_dimension=1, tiled=True),
        lax.psum_scatter(grad_att_in, "dp", scatter_dimension=1, tiled=True),
        lax.psum_scatter(grad_att_out, "dp", scatter_dimension=1, tiled=True),
        lax.psum_scatter(grad_point_in, "dp", scatter_dimension=0, tiled=True),
        lax.psum_scatter(grad_point_out, "dp", scatter_dimension=1, tiled=True),
        lax.psum_scatter(grad_late_up, "dp", scatter_dimension=0, tiled=True),
        lax.psum_scatter(grad_late_down, "dp", scatter_dimension=1, tiled=True),
    )
    late_sums = (all_sums[6], all_sums[7], all_sums[4], all_sums[5])
    early_sums = (all_sums[2], all_sums[3], all_sums[0], all_sums[1])
    gains_part = jnp.stack(
        [gain_zero, gain_one, gain_two, spread_channels(gain_three, member), gain_four, gain_five]
    )
    shifts_part = jnp.stack(
        [
            shift_zero,
            shift_one,
            shift_two,
            spread_channels(shift_three, member),
            shift_four,
            shift_five,
        ]
    )
    table_part = jnp.dot(selector.T, grad_table_dist, precision=highest)
    taps_part = spread_channels(grad_taps, member)
    gains_all, shifts_all, table_all, taps_all = lax.psum(
        (gains_part, shifts_part, table_part, taps_part), ("dp", "tensor")
    )
    return (
        result.astype(jnp.bfloat16),
        upstream,
        gains_all,
        shifts_all,
        early_sums[2],
        early_sums[3],
        early_sums[0],
        early_sums[1],
        table_all,
        late_sums[2],
        taps_all,
        late_sums[3],
        late_sums[0],
        late_sums[1],
    )


def solution(mesh):
    return jax.shard_map(
        per_device,
        mesh=mesh,
        in_specs=(
            P(("dp", "tensor"), None),
            P(),
            P(),
            P("dp", "tensor"),
            P("tensor", "dp"),
            P(None, "dp", "tensor"),
            P("tensor", "dp"),
            P(),
            P("dp", None, "tensor"),
            P(None, "tensor"),
            P("tensor", "dp"),
            P("dp", "tensor"),
            P("tensor", "dp"),
            P(("dp", "tensor"), None),
            P(),
            P(),
            P(),
        ),
        out_specs=(
            P(("dp", "tensor"), None),
            P(("dp", "tensor"), None),
            P(),
            P(),
            P("dp", "tensor"),
            P("tensor", "dp"),
            P(None, "dp", "tensor"),
            P("tensor", "dp"),
            P(),
            P("dp", None, "tensor"),
            P(),
            P("tensor", "dp"),
            P("dp", "tensor"),
            P("tensor", "dp"),
        ),
        check_vma=False,
    )
```

profile of v0, /device:TPU:0, one launch (start us, length us, event | category | flops | bytes accessed | tf_op | source)
XLA Modules:
  0.0 1949.7 jit_solution(17702187678491943438)
XLA Ops:
  15.5 23.9 %all-gather.15.cloned.1.call-done = bf16[1024,1024]{1,0:T(8,128)(2,1)} async-done(((bf16[256,1024]{1,0:T(8,128)(2,1)}), bf16[1024,1024]{1,0:T(8,128)(2,1)}) %all-gather.15.cloned.1.call-update) | async-done | bytes 2097168 | tf_op jit(solution)/shard_map/all_gather | solution.py:65
  39.4 51.2 %all-gather.17.cloned.1.call-done = bf16[1024,1024]{1,0:T(8,128)(2,1)} async-done(((bf16[128,1024]{1,0:T(8,128)(2,1)}), bf16[1024,1024]{1,0:T(8,128)(2,1)}) %all-gather.17.cloned.1.call-update) | async-done | bytes 2097168 | tf_op jit(solution)/shard_map/all_gather | solution.py:402
  97.1 44.5 %all-gather.19.cloned.1.call-done = bf16[1024,1024]{1,0:T(8,128)(2,1)} async-done(((bf16[1024,128]{1,0:T(8,128)(2,1)}), bf16[1024,1024]{1,0:T(8,128)(2,1)}) %all-gather.19.cloned.1.call-update) | async-done | bytes 2097168 | tf_op jit(solution)/shard_map/all_gather | solution.py:403
  148.9 28.8 %reduce-scatter.17.cloned.1.call-done = bf16[256,1024]{1,0:T(8,128)(2,1)} async-done(((bf16[1024,1024]{1,0:T(8,128)(2,1)}), bf16[256,1024]{1,0:T(8,128)(2,1)}) %reduce-scatter.17.cloned.1.call-update) | async-done | bytes 524304 | tf_op jit(solution)/shard_map/reduce_scatter | solution.py:69
  183.1 32.1 %all_gather.61 = bf16[256,1024]{1,0:T(8,128)(2,1)} all-gather(bf16[256,128]{1,0:T(8,128)(2,1)S(1)} %copy-done.53), channel_id=1, replica_groups=mesh['dp'=8,'tensor'=4] {'dp'}, dimensions={1}, use_global_device_ids=true | all-gather | bytes 589824 | tf_op jit(solution)/shard_map/all_gather | solution.py:405
  226.7 23.2 %all-gather.21.cloned.1.call-done = bf16[1024,1024]{1,0:T(8,128)(2,1)} async-done(((bf16[256,1024]{1,0:T(8,128)(2,1)}), bf16[1024,1024]{1,0:T(8,128)(2,1)}) %all-gather.21.cloned.1.call-update) | async-done | bytes 2097168 | tf_op jit(solution)/shard_map/all_gather | solution.py:65
  319.2 30.5 %reduce-scatter.19.cloned.1.call-done = bf16[256,1024]{1,0:T(8,128)(2,1)} async-done(((bf16[1024,1024]{1,0:T(8,128)(2,1)}), bf16[256,1024]{1,0:T(8,128)(2,1)}) %reduce-scatter.19.cloned.1.call-update) | async-done | bytes 524304 | tf_op jit(solution)/shard_map/reduce_scatter | solution.py:69
  354.3 31.5 %all_gather.64 = bf16[256,1024]{1,0:T(8,128)(2,1)} all-gather(bf16[256,128]{1,0:T(8,128)(2,1)S(1)} %copy-done.54), channel_id=1, replica_groups=mesh['dp'=8,'tensor'=4] {'dp'}, dimensions={1}, use_global_device_ids=true | all-gather | bytes 589824 | tf_op jit(solution)/shard_map/all_gather | solution.py:407
  394.6 23.6 %all-gather.25.cloned.1.call-done = bf16[1024,1024]{1,0:T(8,128)(2,1)} async-done(((bf16[256,1024]{1,0:T(8,128)(2,1)}), bf16[1024,1024]{1,0:T(8,128)(2,1)}) %all-gather.25.cloned.1.call-update) | async-done | bytes 2097168 | tf_op jit(solution)/shard_map/all_gather | solution.py:65
  447.2 31.9 %reduce-scatter.21.cloned.1.call-done = bf16[256,1024]{1,0:T(8,128)(2,1)} async-done(((bf16[1024,1024]{1,0:T(8,128)(2,1)}), bf16[256,1024]{1,0:T(8,128)(2,1)}) %reduce-scatter.21.cloned.1.call-update) | async-done | bytes 524304 | tf_op jit(solution)/shard_map/reduce_scatter | solution.py:69
  482.4 47.9 %all-gather.31.cloned.1.call-done = bf16[1024,1024]{1,0:T(8,128)(2,1)} async-done(((bf16[128,1024]{1,0:T(8,128)(2,1)}), bf16[1024,1024]{1,0:T(8,128)(2,1)}) %all-gather.31.cloned.1.call-update) | async-done | bytes 2097168 | tf_op jit(solution)/shard_map/all_gather | solution.py:408
  530.3 23.1 %all-gather.29.cloned.1.call-done = bf16[1024,1024]{1,0:T(8,128)(2,1)} async-done(((bf16[256,1024]{1,0:T(8,128)(2,1)}), bf16[1024,1024]{1,0:T(8,128)(2,1)}) %all-gather.29.cloned.1.call-update) | async-done | bytes 2097168 | tf_op jit(solution)/shard_map/all_gather | solution.py:65
  559.9 45.9 %all-gather.33.cloned.1.call-done = bf16[1024,1024]{1,0:T(8,128)(2,1)} async-done(((bf16[1024,128]{1,0:T(8,128)(2,1)}), bf16[1024,1024]{1,0:T(8,128)(2,1)}) %all-gather.33.cloned.1.call-update) | async-done | bytes 2097168 | tf_op jit(solution)/shard_map/all_gather | solution.py:409
  613.2 28.7 %reduce-scatter.23.cloned.1.call-done = bf16[256,1024]{1,0:T(8,128)(2,1)} async-done(((bf16[1024,1024]{1,0:T(8,128)(2,1)}), bf16[256,1024]{1,0:T(8,128)(2,1)}) %reduce-scatter.23.cloned.1.call-update) | async-done | bytes 524304 | tf_op jit(solution)/shard_map/reduce_scatter | solution.py:69
  647.5 22.5 %all-gather.35.cloned.1.call-done = bf16[1024,1024]{1,0:T(8,128)(2,1)} async-done(((bf16[256,1024]{1,0:T(8,128)(2,1)}), bf16[1024,1024]{1,0:T(8,128)(2,1)}) %all-gather.35.cloned.1.call-update) | async-done | bytes 2097168 | tf_op jit(solution)/shard_map/all_gather | solution.py:78
  681.9 31.3 %reduce-scatter.25.cloned.1.call-done = bf16[256,1024]{1,0:T(8,128)(2,1)} async-done(((bf16[1024,1024]{1,0:T(8,128)(2,1)}), bf16[256,1024]{1,0:T(8,128)(2,1)}) %reduce-scatter.25.cloned.1.call-update) | async-done | bytes 524304 | tf_op jit(solution)/shard_map/reduce_scatter | solution.py:82
  718.5 22.7 %all-gather.37.cloned.1.call-done = bf16[1024,1024]{1,0:T(8,128)(2,1)} async-done(((bf16[256,1024]{1,0:T(8,128)(2,1)}), bf16[1024,1024]{1,0:T(8,128)(2,1)}) %all-gather.37.cloned.1.call-update) | async-done | bytes 2097168 | tf_op jit(solution)/shard_map/all_gather | solution.py:78
  764.3 32.3 %reduce-scatter.27.cloned.1.call-done = bf16[256,1024]{1,0:T(8,128)(2,1)} async-done(((bf16[1024,1024]{1,0:T(8,128)(2,1)}), bf16[256,1024]{1,0:T(8,128)(2,1)}) %reduce-scatter.27.cloned.1.call-update) | async-done | bytes 524304 | tf_op jit(solution)/shard_map/reduce_scatter | solution.py:82
  801.0 22.6 %all-gather.39.cloned.1.call-done = bf16[1024,1024]{1,0:T(8,128)(2,1)} async-done(((bf16[256,1024]{1,0:T(8,128)(2,1)}), bf16[1024,1024]{1,0:T(8,128)(2,1)}) %all-gather.39.cloned.1.call-update) | async-done | bytes 2097168 | tf_op jit(solution)/shard_map/all_gather | solution.py:78
  850.7 21.4 %fusion.66 = f32[2,4,256,73]{3,1,0,2:T(4,128)} fusion(f32[2,4,256,512]{3,2,1,0:T(8,128)S(1)} %get-tuple-element.119, s32[256,512]{1,0:T(8,128)S(1)} %copy-done.44), kind=kOutput, calls=%fused_computation.97 | convolution fusion | flops 928120832 | bytes 5316608 | tf_op jit(solution)/shard_map/chij,rij->chir/dot_general | solution.py:213
  920.6 31.3 %reduce-scatter.29.cloned.1.call-done = bf16[256,1024]{1,0:T(8,128)(2,1)} async-done(((bf16[1024,1024]{1,0:T(8,128)(2,1)}), bf16[256,1024]{1,0:T(8,128)(2,1)}) %reduce-scatter.29.cloned.1.call-update) | async-done | bytes 524304 | tf_op jit(solution)/shard_map/reduce_scatter | solution.py:82
  956.3 22.7 %all-gather.41.cloned.1.call-done = bf16[1024,1024]{1,0:T(8,128)(2,1)} async-done(((bf16[256,1024]{1,0:T(8,128)(2,1)}), bf16[1024,1024]{1,0:T(8,128)(2,1)}) %all-gather.41.cloned.1.call-update) | async-done | bytes 2097168 | tf_op jit(solution)/shard_map/all_gather | solution.py:78
  1052.0 42.2 %reduce-scatter.41.cloned.1.call-done = f32[128,2,256]{2,0,1:T(8,128)} async-done(((f32[1024,2,256]{2,0,1:T(8,128)}), f32[128,2,256]{2,0,1:T(8,128)}) %reduce-scatter.41.cloned.1.call-update) | async-done | bytes 262160 | tf_op jit(solution)/shard_map/reduce_scatter | solution.py:476
  1096.0 75.6 %reduce-scatter.37.cloned.1.call-done = f32[3,128,256]{1,2,0:T(8,128)} async-done(((f32[3,1024,256]{1,2,0:T(8,128)}), f32[3,128,256]{1,2,0:T(8,128)}) %reduce-scatter.37.cloned.1.call-update) | async-done | bytes 393232 | tf_op jit(solution)/shard_map/reduce_scatter | solution.py:474
  1174.9 126.5 %all-reduce.7.cloned.1.call-done = f32[31,1024]{1,0:T(8,128)} async-done(((f32[31,1024]{1,0:T(8,128)}), f32[31,1024]{1,0:T(8,128)}) %all-reduce.7.cloned.1.call-update) | async-done | bytes 126992 | tf_op jit(solution)/shard_map/psum | solution.py:498
  1301.4 91.4 %reduce-scatter.45.cloned.1.call-done = f32[128,1024]{1,0:T(8,128)} async-done(((f32[1024,1024]{1,0:T(8,128)}), f32[128,1024]{1,0:T(8,128)}) %reduce-scatter.45.cloned.1.call-update) | async-done | bytes 524304 | tf_op jit(solution)/shard_map/reduce_scatter | solution.py:478
  1392.8 92.4 %reduce-scatter.47.cloned.1.call-done = f32[1024,128]{1,0:T(8,128)} async-done(((f32[1024,1024]{1,0:T(8,128)}), f32[1024,128]{1,0:T(8,128)}) %reduce-scatter.47.cloned.1.call-update) | async-done | bytes 524304 | tf_op jit(solution)/shard_map/reduce_scatter | solution.py:479
  1485.3 68.3 %reduce-scatter.43.cloned.1.call-done = f32[256,128]{1,0:T(8,128)} async-done(((f32[256,1024]{1,0:T(8,128)}), f32[256,128]{1,0:T(8,128)}) %reduce-scatter.43.cloned.1.call-update) | async-done | bytes 131088 | tf_op jit(solution)/shard_map/reduce_scatter | solution.py:477
  1553.6 67.8 %reduce-scatter.39.cloned.1.call-done = f32[256,128]{1,0:T(8,128)} async-done(((f32[256,1024]{1,0:T(8,128)}), f32[256,128]{1,0:T(8,128)}) %reduce-scatter.39.cloned.1.call-update) | async-done | bytes 131088 | tf_op jit(solution)/shard_map/reduce_scatter | solution.py:475
  1621.4 129.8 %all-reduce.9.cloned.1.call-done = (f32[6,1024]{1,0:T(8,128)}, f32[6,1024]{1,0:T(8,128)}, f32[73,64]{0,1:T(8,128)}) async-done(((f32[6,1024]{1,0:T(8,128)}, f32[6,1024]{1,0:T(8,128)}, f32[73,64]{0,1:T(8,128)}), (f32[6,1024]{1,0:T(8,128)}, f32[6,1024]{1,0:T(8,128)}, f32[73,64]{0,1:T(8,128)})) %all-reduce.9.cloned.1.call-update) | async-done | bytes 67856 | tf_op jit(solution)/shard_map/psum | solution.py:498
  1751.2 93.6 %reduce-scatter.33.cloned.1.call-done = f32[128,1024]{1,0:T(8,128)} async-done(((f32[1024,1024]{1,0:T(8,128)}), f32[128,1024]{1,0:T(8,128)}) %reduce-scatter.33.cloned.1.call-update) | async-done | bytes 524304 | tf_op jit(solution)/shard_map/reduce_scatter | solution.py:472
  1844.7 92.5 %reduce-scatter.35.cloned.1.call-done = f32[1024,128]{1,0:T(8,128)} async-done(((f32[1024,1024]{1,0:T(8,128)}), f32[1024,128]{1,0:T(8,128)}) %reduce-scatter.35.cloned.1.call-update) | async-done | bytes 524304 | tf_op jit(solution)/shard_map/reduce_scatter | solution.py:473
  (512 shorter events, 379.7 us)
Async XLA Ops:
  7.2 32.2 %all-gather.15.cloned.1.call-start = ((), (), s32[]{:S(2)}) async-start(), calls=%async_computation.16 | async-start | bytes 2621440 | tf_op jit(solution)/shard_map/all_gather | solution.py:65
  14.0 76.7 %all-gather.17.cloned.1.call-start = ((), (), s32[]{:S(2)}) async-start(), calls=%async_computation.17 | async-start | bytes 2359296 | tf_op jit(solution)/shard_map/all_gather | solution.py:402
  14.7 126.9 %all-gather.19.cloned.1.call-start = ((), (), s32[]{:S(2)}) async-start(), calls=%async_computation.18 | async-start | bytes 2359296 | tf_op jit(solution)/shard_map/all_gather | solution.py:403
  15.5 162.3 %reduce-scatter.17.cloned.1.call-start = ((), (), s32[]{:S(2)}) async-start(), calls=%async_computation.19 | async-start | bytes 2621440 | tf_op jit(solution)/shard_map/reduce_scatter | solution.py:69
  148.2 78.5 %all-gather.23.cloned.1.call-start = ((), (), s32[]{:S(2)}) async-start(), calls=%async_computation.21 | async-start | bytes 1769472 | tf_op jit(solution)/shard_map/all_gather | solution.py:404
  148.9 101.1 %all-gather.21.cloned.1.call-start = ((), (), s32[]{:S(2)}) async-start(), calls=%async_computation.20 | async-start | bytes 2621440 | tf_op jit(solution)/shard_map/all_gather | solution.py:65
  181.7 168.0 %reduce-scatter.19.cloned.1.call-start = ((), (), s32[]{:S(2)}) async-start(), calls=%async_computation.22 | async-start | bytes 2621440 | tf_op jit(solution)/shard_map/reduce_scatter | solution.py:69
  318.4 76.2 %all-gather.27.cloned.1.call-start = ((), (), s32[]{:S(2)}) async-start(), calls=%async_computation.24 | async-start | bytes 1179648 | tf_op jit(solution)/shard_map/all_gather | solution.py:406
  319.1 99.0 %all-gather.25.cloned.1.call-start = ((), (), s32[]{:S(2)}) async-start(), calls=%async_computation.23 | async-start | bytes 2621440 | tf_op jit(solution)/shard_map/all_gather | solution.py:65
  352.4 126.7 %reduce-scatter.21.cloned.1.call-start = ((), (), s32[]{:S(2)}) async-start(), calls=%async_computation.25 | async-start | bytes 2621440 | tf_op jit(solution)/shard_map/reduce_scatter | solution.py:69
  446.4 83.9 %all-gather.31.cloned.1.call-start = ((), (), s32[]{:S(2)}) async-start(), calls=%async_computation.27 | async-start | bytes 2359296 | tf_op jit(solution)/shard_map/all_gather | solution.py:408
  447.1 106.3 %all-gather.29.cloned.1.call-start = ((), (), s32[]{:S(2)}) async-start(), calls=%async_computation.26 | async-start | bytes 2621440 | tf_op jit(solution)/shard_map/all_gather | solution.py:65
  481.6 124.2 %all-gather.33.cloned.1.call-start = ((), (), s32[]{:S(2)}) async-start(), calls=%async_computation.28 | async-start | bytes 2359296 | tf_op jit(solution)/shard_map/all_gather | solution.py:409
  482.4 159.5 %reduce-scatter.23.cloned.1.call-start = ((), (), s32[]{:S(2)}) async-start(), calls=%async_computation.29 | async-start | bytes 2621440 | tf_op jit(solution)/shard_map/reduce_scatter | solution.py:69
  612.4 57.6 %all-gather.35.cloned.1.call-start = ((), (), s32[]{:S(2)}) async-start(), calls=%async_computation.30 | async-start | bytes 2621440 | tf_op jit(solution)/shard_map/all_gather | solution.py:78
  647.3 65.9 %reduce-scatter.25.cloned.1.call-start = ((), (), s32[]{:S(2)}) async-start(), calls=%async_computation.31 | async-start | bytes 2621440 | tf_op jit(solution)/shard_map/reduce_scatter | solution.py:82
  681.9 59.3 %all-gather.37.cloned.1.call-start = ((), (), s32[]{:S(2)}) async-start(), calls=%async_computation.32 | async-start | bytes 2621440 | tf_op jit(solution)/shard_map/all_gather | solution.py:78
  718.4 78.2 %reduce-scatter.27.cloned.1.call-start = ((), (), s32[]{:S(2)}) async-start(), calls=%async_computation.33 | async-start | bytes 2621440 | tf_op jit(solution)/shard_map/reduce_scatter | solution.py:82
  764.3 59.3 %all-gather.39.cloned.1.call-start = ((), (), s32[]{:S(2)}) async-start(), calls=%async_computation.34 | async-start | bytes 2621440 | tf_op jit(solution)/shard_map/all_gather | solution.py:78
  800.9 151.0 %reduce-scatter.29.cloned.1.call-start = ((), (), s32[]{:S(2)}) async-start(), calls=%async_computation.35 | async-start | bytes 2621440 | tf_op jit(solution)/shard_map/reduce_scatter | solution.py:82
  920.5 58.5 %all-gather.41.cloned.1.call-start = ((), (), s32[]{:S(2)}) async-start(), calls=%async_computation.36 | async-start | bytes 2621440 | tf_op jit(solution)/shard_map/all_gather | solution.py:78
  956.3 78.4 %reduce-scatter.31.cloned.1.call-start = ((), (), s32[]{:S(2)}) async-start(), calls=%async_computation.37 | async-start | bytes 2621440 | tf_op jit(solution)/shard_map/reduce_scatter | solution.py:82
  990.7 103.5 %reduce-scatter.41.cloned.1.call-start = ((), (), s32[]{:S(2)}) async-start(), calls=%async_computation.42 | async-start | bytes 2359296 | tf_op jit(solution)/shard_map/reduce_scatter | solution.py:476
  996.1 175.6 %reduce-scatter.37.cloned.1.call-start = ((), (), s32[]{:S(2)}) async-start(), calls=%async_computation.40 | async-start | bytes 3538944 | tf_op jit(solution)/shard_map/reduce_scatter | solution.py:474
  1002.9 298.5 %all-reduce.7.cloned.1.call-start = ((), (), s32[]{:S(2)}) async-start(), calls=%async_computation.43 | async-start | bytes 262144 | tf_op jit(solution)/shard_map/psum | solution.py:498
  1009.6 383.2 %reduce-scatter.45.cloned.1.call-start = ((), (), s32[]{:S(2)}) async-start(), calls=%async_computation.45 | async-start | bytes 4718592 | tf_op jit(solution)/shard_map/reduce_scatter | solution.py:478
  1016.3 469.0 %reduce-scatter.47.cloned.1.call-start = ((), (), s32[]{:S(2)}) async-start(), calls=%async_computation.46 | async-start | bytes 4718592 | tf_op jit(solution)/shard_map/reduce_scatter | solution.py:479
  1024.5 529.1 %reduce-scatter.43.cloned.1.call-start = ((), (), s32[]{:S(2)}) async-start(), calls=%async_computation.44 | async-start | bytes 1179648 | tf_op jit(solution)/shard_map/reduce_scatter | solution.py:477
  1029.1 592.2 %reduce-scatter.39.cloned.1.call-start = ((), (), s32[]{:S(2)}) async-start(), calls=%async_computation.41 | async-start | bytes 1179648 | tf_op jit(solution)/shard_map/reduce_scatter | solution.py:475
  1032.7 718.5 %all-reduce.9.cloned.1.call-start = ((), (), s32[]{:S(2)}) async-start(), calls=%async_computation.47 | async-start | bytes 196608 | tf_op jit(solution)/shard_map/psum | solution.py:498
  1037.7 807.1 %reduce-scatter.33.cloned.1.call-start = ((), (), s32[]{:S(2)}) async-start(), calls=%async_computation.38 | async-start | bytes 4718592 | tf_op jit(solution)/shard_map/reduce_scatter | solution.py:472
  1044.4 892.9 %reduce-scatter.35.cloned.1.call-start = ((), (), s32[]{:S(2)}) async-start(), calls=%async_computation.39 | async-start | bytes 4718592 | tf_op jit(solution)/shard_map/reduce_scatter | solution.py:473
  (135 other events, 3313.7 us)
Sparse Core Ops, SparseCore 0:
  14.1 25.2 all-gather.14
  41.5 49.0 all-gather.16
  92.7 48.8 all-gather.18
  148.3 29.3 reduce-scatter.16
  179.7 46.9 all-gather.22
  228.7 21.2 all-gather.20
  318.5 31.1 reduce-scatter.18
  352.4 42.1 all-gather.26
  396.7 21.3 all-gather.24
  446.5 32.4 reduce-scatter.20
  481.2 49.0 all-gather.30
  532.3 21.0 all-gather.28
  555.5 50.3 all-gather.32
  612.6 29.3 reduce-scatter.22
  647.4 22.5 all-gather.34
  682.0 31.1 reduce-scatter.24
  718.5 22.5 all-gather.36
  764.4 32.2 reduce-scatter.26
  801.0 22.5 all-gather.38
  920.6 31.1 reduce-scatter.28
  956.4 22.5 all-gather.40
  990.8 31.1 reduce-scatter.30
  1025.6 68.5 reduce-scatter.40
  1097.6 73.9 reduce-scatter.36
  1177.7 123.6 all-reduce.6
  1305.5 87.3 reduce-scatter.44
  1396.9 88.3 reduce-scatter.46
  1489.2 64.3 reduce-scatter.42
  1557.6 63.7 reduce-scatter.38
  1628.4 122.7 all-reduce.8
  1755.4 89.3 reduce-scatter.32
  1848.9 88.2 reduce-scatter.34
where the time goes:
time: 1960 us; the launch traced here: 1950 us
  waiting for transfers between devices  1490 us (76%)
  matrix products  227 us (12%)
  blocking collectives  81.7 us (4%)
  other arithmetic  68.1 us (3%)
  local copies, waits for them, and re-layouts  63 us (3%)
    psum x2, waiting for transfers between devices, per_device(): lax.psum((gains_part, shifts_part, table_part, taps_part), ('dp', 'tensor'))  256 us
    reduce_scatter x4, waiting for transfers between devices, frames_reduce(): lax.psum_scatter(row_term(jnp.int32(0), rows_here * lax.axis_size('tensor...  120 us
    reduce_scatter x4, waiting for transfers between devices, grads_reduce(): lax.psum_scatter(row_term(jnp.int32(0), rows_here * lax.axis_size('tensor...  94.9 us
    all_gather x4, waiting for transfers between devices, frames_gather(): lax.all_gather(normed.astype(jnp.bfloat16), 'tensor', axis=0, tiled=True)  93.8 us
    reduce_scatter x1, waiting for transfers between devices, per_device(): lax.psum_scatter(grad_early_up, 'dp', scatter_dimension=0, tiled=True)  93.6 us
    reduce_scatter x1, waiting for transfers between devices, per_device(): lax.psum_scatter(grad_early_down, 'dp', scatter_dimension=1, tiled=True)  92.5 us
    reduce_scatter x1, waiting for transfers between devices, per_device(): lax.psum_scatter(grad_late_down, 'dp', scatter_dimension=1, tiled=True)  92.4 us
    reduce_scatter x1, waiting for transfers between devices, per_device(): lax.psum_scatter(grad_late_up, 'dp', scatter_dimension=0, tiled=True)  91.4 us
  transfers between devices with their start and end apart: 32, of which 31 were waited for; matrix products, arithmetic and copies ran while one was open for 4% of the time, Pallas kernels for 0%

commit v1 on v0

v1 whole, which is shorter than its diff:
```python
import jax
import jax.numpy as jnp
from jax import lax
from jax.experimental import pallas as pl
from jax.experimental.pallas import tpu as pltpu
from jax.sharding import PartitionSpec as P

D = 1024
HEAD_DIM = 64
KERNEL = 31
REL_LEFT = 64
REL_RIGHT = 8
CLIP_DEV = 2
L = 512
HALF = L // 2
RELS = 73

norm_eps = 1e-05
masked_score = -1e30
highest = lax.Precision.HIGHEST
f32 = jnp.float32
bf16 = jnp.bfloat16

RING = (0, 2, 4, 6, 7, 5, 3, 1)


def mm(a, b):
    return jnp.dot(a, b, preferred_element_type=f32)


def mm_tn(a, b):
    return lax.dot_general(a, b, (((0,), (0,)), ((), ())), preferred_element_type=f32)


def mm_nt(a, b):
    return lax.dot_general(a, b, (((1,), (1,)), ((), ())), preferred_element_type=f32)


def sigmoid_parts(h):
    s = jax.nn.sigmoid(h)
    return s


def swish(h):
    return h * jax.nn.sigmoid(h)


def swish_grad(h):
    s = jax.nn.sigmoid(h)
    return s * (1.0 + h * (1.0 - s))


def to_core(v):
    return lax.ppermute(v, "tensor", [(m, m ^ 1) for m in range(lax.axis_size("tensor"))])


def to_far(v):
    return lax.ppermute(v, "tensor", [(m, m ^ 2) for m in range(lax.axis_size("tensor"))])


def to_right(v):
    n = len(RING)
    return lax.ppermute(v, "dp", [(RING[i], RING[(i + 1) % n]) for i in range(n)])


def to_left(v):
    n = len(RING)
    return lax.ppermute(v, "dp", [(RING[i], RING[(i - 1) % n]) for i in range(n)])


def on_ring():
    return lax.axis_size("dp") == len(RING)


def block_order():
    index = lax.axis_index("dp")
    count = lax.axis_size("dp")
    if not on_ring():
        return jnp.arange(count, dtype=jnp.int32)
    ring = jnp.array(RING, jnp.int32)
    place = jnp.sum(jnp.where(ring == index, jnp.arange(count, dtype=jnp.int32), 0))
    turned = (place + jnp.arange(count, dtype=jnp.int32)) % count
    return jnp.sum(jnp.where(turned[:, None] == jnp.arange(count)[None, :], ring[None, :], 0), axis=1)


def gather_rows(shard):
    if not on_ring():
        return lax.all_gather(shard, "dp", axis=0, tiled=True)
    half = shard.shape[0] // 2
    r1, l1 = to_right(shard), to_left(shard)
    r2, l2 = to_right(r1), to_left(l1)
    r3, l3 = to_right(r2), to_left(l2)
    r4, l4 = to_right(r3[:half]), to_left(l3[half:])
    return jnp.concatenate([shard, l1, l2, l3, r4, l4, r3, r2, r1], axis=0)


def scatter_rows(total):
    count = lax.axis_size("dp")
    rows = total.shape[0] // count
    if not on_ring():
        return lax.psum_scatter(total, "dp", scatter_dimension=0, tiled=True).astype(f32)
    half = rows // 2

    def block(k):
        return total[k * rows : (k + 1) * rows]

    def plus(a, b):
        return (a.astype(f32) + b.astype(f32)).astype(bf16)

    m = to_right(block(4)[:half])
    n = to_left(block(4)[half:])
    m = to_right(jnp.concatenate([plus(block(3)[:half], m), block(3)[half:]], axis=0))
    n = to_left(jnp.concatenate([block(5)[:half], plus(block(5)[half:], n)], axis=0))
    m = to_right(plus(block(2), m))
    n = to_left(plus(block(6), n))
    m = to_right(plus(block(1), m))
    n = to_left(plus(block(7), n))
    return block(0).astype(f32) + m.astype(f32) + n.astype(f32)


def sum_everywhere(values):
    def step(vals, axis, perm):
        return [v + lax.ppermute(v, axis, perm) for v in vals]

    for axis in ("tensor", "dp"):
        count = lax.axis_size(axis)
        bit = 1
        while bit < count:
            values = step(values, axis, [(m, m ^ bit) for m in range(count)])
            bit *= 2
    return values


def gather_frames(mine):
    near = to_core(mine)
    far = to_far(mine)
    return jnp.concatenate([mine, near], axis=0), jnp.concatenate([far, to_core(far)], axis=0)


def reduce_frames(own, other):
    rows = own.shape[0] // 2
    own, other = own.astype(bf16), other.astype(bf16)
    near = to_core(own[rows:])
    near_other = to_core(other[rows:])
    far = to_far((other[:rows].astype(f32) + near_other.astype(f32)).astype(bf16))
    return own[:rows].astype(f32) + near.astype(f32) + far.astype(f32)


def permute_blocks(values, order):
    count = order.shape[0]
    if not on_ring():
        return values
    width = D // count

    def body(order_ref, *refs):
        ins, outs = refs[: len(values)], refs[len(values) :]
        for src, dst in zip(ins, outs):
            for k in range(count):
                at = pl.multiple_of(order_ref[k] * width, width)
                dst[:, k * width : (k + 1) * width] = src[:, pl.ds(at, width)]

    return pl.pallas_call(
        body,
        grid_spec=pltpu.PrefetchScalarGridSpec(
            num_scalar_prefetch=1,
            grid=(),
            in_specs=[pl.BlockSpec(memory_space=pltpu.VMEM) for _ in values],
            out_specs=[pl.BlockSpec(memory_space=pltpu.VMEM) for _ in values],
        ),
        out_shape=[jax.ShapeDtypeStruct(v.shape, v.dtype) for v in values],
    )(order, *values)


def norm_forward(v, gain, shift):
    centre = v - jnp.mean(v, axis=-1, keepdims=True)
    spread = jnp.mean(centre * centre, axis=-1, keepdims=True)
    r = lax.rsqrt(spread + norm_eps)
    unit = centre * r
    return unit * gain + shift, unit, r


def norm_backward(q, unit, r, gain):
    scaled = q * gain
    bracket = (
        scaled
        - jnp.mean(scaled, axis=-1, keepdims=True)
        - unit * jnp.mean(scaled * unit, axis=-1, keepdims=True)
    )
    return r * bracket, jnp.sum(q * unit, axis=0), jnp.sum(q, axis=0)


def ffn_forward(stream, gain, shift, up, down_t):
    normed, unit, r = norm_forward(stream, gain, shift)
    frames = gather_frames(normed.astype(bf16))
    hidden = [mm(x, up) for x in frames]
    active = [swish(h).astype(bf16) for h in hidden]
    branch = reduce_frames(*[mm_nt(a, down_t) for a in active])
    return stream + 0.5 * branch, (unit, r, frames, hidden, active)


def ffn_backward(upstream, gain, up, down_t, saved):
    unit, r, frames, hidden, active = saved
    incoming = gather_frames(upstream.astype(bf16))
    dhidden = [
        (0.5 * mm(g, down_t) * swish_grad(h)).astype(bf16) for g, h in zip(incoming, hidden)
    ]
    dnormed = reduce_frames(*[mm_nt(d, up) for d in dhidden])
    grad_down = (0.5 * sum(mm_tn(g, a) for g, a in zip(incoming, active))).astype(bf16)
    grad_up = sum(mm_tn(x, d) for x, d in zip(frames, dhidden)).astype(bf16)
    dstream, dgain, dshift = norm_backward(dnormed, unit, r, gain)
    return upstream + dstream, grad_up, grad_down, dgain, dshift


def swap_halves(v, low):
    return jnp.where(low == 0, v, jnp.roll(v, HALF, axis=0))


def scores_of(q, k, table, length):
    direct = jnp.einsum("ihd,jhd->hij", q, k, preferred_element_type=f32)
    by_dist = jnp.einsum("ihd,rd->hir", q, table, preferred_element_type=f32)
    at = jnp.arange(L, dtype=jnp.int32)
    distance = jnp.clip(at[None, :] - at[:, None], -REL_LEFT, REL_RIGHT) + REL_LEFT
    band = (distance[None] == jnp.arange(RELS, dtype=jnp.int32)[:, None, None]).astype(f32)
    relative = jnp.einsum("hir,rij->hij", by_dist, band, precision=highest)
    scores = (direct + relative) * HEAD_DIM ** (-0.5)
    return jnp.where((at < length)[None, None, :], scores, masked_score), band


def attend(qkv, table, length, low):
    qkv = swap_halves(qkv, low)
    heads = qkv.shape[1] // (3 * HEAD_DIM)
    q, k, v = jnp.moveaxis(qkv.reshape(L, 3, heads, HEAD_DIM), 1, 0)
    scores, _ = scores_of(q, k, table, length)
    top = jnp.max(scores, axis=-1, keepdims=True)
    raised = jnp.exp(scores - top)
    total = jnp.sum(raised, axis=-1, keepdims=True)
    shares = (raised / total).astype(bf16)
    out = jnp.einsum("hij,jhd->ihd", shares, v, preferred_element_type=f32).astype(bf16)
    return swap_halves(out.reshape(L, heads * HEAD_DIM), low), top + jnp.log(total)


def attend_back(qkv, dout, logs, table, length, low):
    qkv = swap_halves(qkv, low)
    heads = qkv.shape[1] // (3 * HEAD_DIM)
    q, k, v = jnp.moveaxis(qkv.reshape(L, 3, heads, HEAD_DIM), 1, 0)
    dout = swap_halves(dout, low).reshape(L, heads, HEAD_DIM)
    scale = HEAD_DIM ** (-0.5)
    scores, band = scores_of(q, k, table, length)
    shares = jnp.exp(scores - logs)
    dv = jnp.einsum("hij,ihd->jhd", shares.astype(bf16), dout, preferred_element_type=f32)
    dshares = jnp.einsum("ihd,jhd->hij", dout, v, preferred_element_type=f32)
    centre = jnp.sum(shares * dshares, axis=-1, keepdims=True)
    ds = (shares * (dshares - centre)).astype(bf16)
    dq = jnp.einsum("hij,jhd->ihd", ds, k, preferred_element_type=f32) * scale
    dk = jnp.einsum("hij,ihd->jhd", ds, q, preferred_element_type=f32) * scale
    pulled = jnp.einsum("hij,rij->hir", ds.astype(f32) * scale, band, precision=highest)
    dq = dq + jnp.einsum("hir,rd->ihd", pulled, table.astype(f32), precision=highest)
    dtable = jnp.einsum("hir,ihd->rd", pulled, q.astype(f32), precision=highest)
    dqkv = jnp.stack([dq, dk, dv], axis=1).astype(bf16).reshape(L, 3 * heads * HEAD_DIM)
    return swap_halves(dqkv, low), dtable


def attention_forward(stream, gain, shift, w_in, w_out_t, table, lengths, low):
    normed, unit, r = norm_forward(stream, gain, shift)
    frames = gather_frames(normed.astype(bf16))
    qkv = [mm(x, w_in).astype(bf16) for x in frames]
    results = [attend(p, table, n, low) for p, n in zip(qkv, lengths)]
    attended = [a for a, _ in results]
    branch = reduce_frames(*[mm_nt(a, w_out_t) for a in attended])
    return stream + branch, (unit, r, frames, qkv, attended, [s for _, s in results])


def attention_backward(upstream, gain, w_in, w_out_t, table, lengths, low, saved):
    unit, r, frames, qkv, attended, logs = saved
    incoming = gather_frames(upstream.astype(bf16))
    datt = [mm(g, w_out_t).astype(bf16) for g in incoming]
    results = [
        attend_back(p, d, s, table, n, low) for p, d, s, n in zip(qkv, datt, logs, lengths)
    ]
    dqkv = [d for d, _ in results]
    dnormed = reduce_frames(*[mm_nt(d, w_in) for d in dqkv])
    grad_out = sum(mm_tn(g, a) for g, a in zip(incoming, attended)).astype(bf16)
    grad_in = sum(mm_tn(x, d) for x, d in zip(frames, dqkv)).astype(bf16)
    dtable = results[0][1] + results[1][1]
    dstream, dgain, dshift = norm_backward(dnormed, unit, r, gain)
    return upstream + dstream, grad_in, grad_out, dtable, dgain, dshift


def gated_of(halves, low):
    channels = halves.shape[1] // 2
    halves = swap_halves(halves, low)
    linear, opened = halves[:, :channels], jax.nn.sigmoid(halves[:, channels:])
    return linear, opened, jnp.pad(linear * opened, ((KERNEL - 1, 0), (0, 0)))


def convolve(padded, taps):
    out = taps[0] * padded[0:L]
    for k in range(1, KERNEL):
        out = out + taps[k] * padded[k : k + L]
    return out


def across(pairs):
    return to_far(pairs)[::-1]


def channel_stats(convolved):
    count = convolved[0].shape[1]

    def local(rows):
        mean = jnp.mean(rows, axis=-1)
        centre = rows - mean[:, None]
        return jnp.stack([mean, jnp.sum(centre * centre, axis=-1)])

    pairs = jnp.stack([local(rows) for rows in convolved])
    for send in (to_core, across):
        other = send(pairs)
        gap = pairs[:, 0] - other[:, 0]
        pairs = jnp.stack(
            [
                0.5 * (pairs[:, 0] + other[:, 0]),
                pairs[:, 1] + other[:, 1] + 0.5 * count * gap * gap,
            ],
            axis=1,
        )
        count = 2 * count
    return [(p[0][:, None], lax.rsqrt(p[1] / count + norm_eps)[:, None]) for p in pairs]


def conv_forward(stream, gain, shift, w_in, taps, w_out_t, cgain, cshift, low):
    normed, unit, r = norm_forward(stream, gain, shift)
    frames = gather_frames(normed.astype(bf16))
    opened = [gated_of(mm(x, w_in), low) for x in frames]
    convolved = [convolve(padded, taps) for _, _, padded in opened]
    parts = []
    active = []
    for gate, rows, (mean, inverse) in zip(opened, convolved, channel_stats(convolved)):
        cunit = (rows - mean) * inverse
        mid = cunit * cgain + cshift
        active.append(swap_halves(swish(mid).astype(bf16), low))
        parts.append((*gate, cunit, inverse, mid))
    branch = reduce_frames(*[mm_nt(a, w_out_t) for a in active])
    return stream + branch, (unit, r, frames, parts, active)


def conv_backward(upstream, gain, w_in, taps, w_out_t, cgain, low, saved):
    unit, r, frames, parts, active = saved
    incoming = gather_frames(upstream.astype(bf16))
    dhalves = []
    sums = []
    dmids = []
    pairs = []
    for g, (_, _, _, cunit, _, mid) in zip(incoming, parts):
        dmid = swap_halves(mm(g, w_out_t), low) * swish_grad(mid)
        scaled = dmid * cgain
        pairs.append(jnp.stack([jnp.sum(scaled, axis=-1), jnp.sum(scaled * cunit, axis=-1)]))
        dmids.append(dmid)
    pairs = jnp.stack(pairs)
    pairs = pairs + to_core(pairs)
    pairs = (pairs + across(pairs)) / D
    for dmid, pair, (linear, opened, padded, cunit, inverse, mid) in zip(dmids, pairs, parts):
        scaled = dmid * cgain
        dconv = inverse * (scaled - pair[0][:, None] - cunit * pair[1][:, None])
        late = jnp.pad(dconv, ((0, KERNEL - 1), (0, 0)))
        dgated = taps[0] * late[KERNEL - 1 : KERNEL - 1 + L]
        for k in range(1, KERNEL):
            dgated = dgated + taps[k] * late[KERNEL - 1 - k : KERNEL - 1 - k + L]
        dtaps = jnp.stack([jnp.sum(padded[k : k + L] * dconv, axis=0) for k in range(KERNEL)])
        dh = jnp.concatenate(
            [dgated * opened, dgated * linear * opened * (1.0 - opened)], axis=1
        ).astype(bf16)
        dhalves.append(swap_halves(dh, low))
        sums.append((dtaps, jnp.sum(dmid * cunit, axis=0), jnp.sum(dmid, axis=0)))
    dnormed = reduce_frames(*[mm_nt(d, w_in) for d in dhalves])
    grad_out = sum(mm_tn(g, a) for g, a in zip(incoming, active)).astype(bf16)
    grad_in = sum(mm_tn(x, d) for x, d in zip(frames, dhalves)).astype(bf16)
    dtaps, dcgain, dcshift = [a + b for a, b in zip(*sums)]
    dstream, dgain, dshift = norm_backward(dnormed, unit, r, gain)
    return upstream + dstream, grad_in, grad_out, dtaps, dgain, dshift, dcgain, dcshift


def spread_channels(part, member):
    zero = jnp.zeros(part.shape[:-1] + (D,), f32)
    return lax.dynamic_update_slice_in_dim(zero, part, member * part.shape[-1], part.ndim - 1)


def per_device(
    layer_in,
    norm_gain,
    norm_shift,
    early_up,
    early_down,
    attend_in,
    attend_out,
    position_table,
    pointwise_in,
    depthwise,
    pointwise_out,
    late_up,
    late_down,
    output_grad,
    clip_lengths,
    clip_slots,
    position_rows,
):
    group = lax.axis_index("dp")
    member = lax.axis_index("tensor")
    low = member % 2
    high = member // 2
    rows_here = layer_in.shape[0]
    block = early_up.shape[0]
    channels = depthwise.shape[1]

    order = block_order()
    count = order.shape[0]
    inverse_order = jnp.sum(
        jnp.where(
            order[None, :] == jnp.arange(count, dtype=jnp.int32)[:, None],
            jnp.arange(count, dtype=jnp.int32)[None, :],
            0,
        ),
        axis=1,
    )
    stream, cotangent, gains, shifts = permute_blocks(
        [layer_in, output_grad, norm_gain, norm_shift], order
    )

    slots = group * CLIP_DEV + jnp.stack([high, 1 - high])
    lengths = jnp.sum(
        jnp.where(clip_slots[None, :] == slots[:, None], clip_lengths[None, :], 0), axis=1
    )
    lengths = [lengths[0], lengths[1]]
    live = low * rows_here + jnp.arange(rows_here, dtype=jnp.int32) < lengths[0]

    selector = (position_rows[:, None] == jnp.arange(RELS, dtype=jnp.int32)[None, :]).astype(f32)
    table = jnp.dot(selector, position_table.astype(f32), precision=highest).astype(bf16)
    cgain = lax.dynamic_slice_in_dim(norm_gain[3], member * channels, channels)
    cshift = lax.dynamic_slice_in_dim(norm_shift[3], member * channels, channels)
    taps = depthwise.astype(f32)

    pack_attend = jnp.concatenate(
        [jnp.moveaxis(attend_in, 0, 1).reshape(block, -1), attend_out.T], axis=1
    )
    pack_conv = jnp.concatenate([pointwise_in.reshape(block, -1), pointwise_out.T], axis=1)
    wide = attend_in.shape[0] * attend_in.shape[2]
    cwide = 2 * channels

    w_early_up = gather_rows(early_up)
    w_early_down = gather_rows(early_down.T)
    w_attend = gather_rows(pack_attend)
    w_conv = gather_rows(pack_conv)
    w_late_up = gather_rows(late_up)
    w_late_down = gather_rows(late_down.T)
    w_att_in, w_att_out = w_attend[:, :wide], w_attend[:, wide:]
    w_pi, w_po = w_conv[:, :cwide], w_conv[:, cwide:]

    stream0 = stream.astype(f32)
    stream1, saved_early = ffn_forward(stream0, gains[0], shifts[0], w_early_up, w_early_down)
    stream2, saved_attend = attention_forward(
        stream1, gains[1], shifts[1], w_att_in, w_att_out, table, lengths, low
    )
    stream3, saved_conv = conv_forward(
        stream2, gains[2], shifts[2], w_pi, taps, w_po, cgain, cshift, low
    )
    stream4, saved_late = ffn_forward(stream3, gains[4], shifts[4], w_late_up, w_late_down)
    result, unit5, r5 = norm_forward(stream4, gains[5], shifts[5])

    up = jnp.where(live[:, None], cotangent.astype(f32), 0.0)
    up, gain5, shift5 = norm_backward(up, unit5, r5, gains[5])
    up, g_late_up, g_late_down, gain4, shift4 = ffn_backward(
        up, gains[4], w_late_up, w_late_down, saved_late
    )
    g_late_up = scatter_rows(g_late_up)
    g_late_down = scatter_rows(g_late_down)
    up, g_pi, g_po, g_taps, gain2, shift2, gain3, shift3 = conv_backward(
        up, gains[2], w_pi, taps, w_po, cgain, low, saved_conv
    )
    g_conv = scatter_rows(jnp.concatenate([g_pi, g_po], axis=1))
    up, g_in, g_out, g_table, gain1, shift1 = attention_backward(
        up, gains[1], w_att_in, w_att_out, table, lengths, low, saved_attend
    )
    g_attend = scatter_rows(jnp.concatenate([g_in, g_out], axis=1))
    up, g_early_up, g_early_down, gain0, shift0 = ffn_backward(
        up, gains[0], w_early_up, w_early_down, saved_early
    )
    g_early_down = scatter_rows(g_early_down)
    g_early_up = scatter_rows(g_early_up)

    zero_row = jnp.zeros((D,), f32)
    norms = jnp.stack(
        [gain0, gain1, gain2, zero_row, gain4, gain5, shift0, shift1, shift2, zero_row, shift4, shift5]
    )
    result, up, norms = permute_blocks([result.astype(bf16), up, norms], inverse_order)
    side = spread_channels(jnp.concatenate([g_taps, gain3[None], shift3[None]], axis=0), member)
    table_part = jnp.dot(selector.T, g_table, precision=highest)
    norms, side, table_all = sum_everywhere([norms, side, table_part])
    gains_all = jnp.concatenate([norms[0:3], side[KERNEL : KERNEL + 1], norms[4:6]], axis=0)
    shifts_all = jnp.concatenate([norms[6:9], side[KERNEL + 1 :], norms[10:12]], axis=0)

    return (
        result,
        up,
        gains_all,
        shifts_all,
        g_early_up,
        g_early_down.T,
        jnp.moveaxis(g_attend[:, :wide].reshape(block, 3, -1), 1, 0),
        g_attend[:, wide:].T,
        table_all,
        g_conv[:, :cwide].reshape(block, 2, channels),
        side[:KERNEL],
        g_conv[:, cwide:].T,
        g_late_up,
        g_late_down.T,
    )


def solution(mesh):
    return jax.shard_map(
        per_device,
        mesh=mesh,
        in_specs=(
            P(("dp", "tensor"), None),
            P(),
            P(),
            P("dp", "tensor"),
            P("tensor", "dp"),
            P(None, "dp", "tensor"),
            P("tensor", "dp"),
            P(),
            P("dp", None, "tensor"),
            P(None, "tensor"),
            P("tensor", "dp"),
            P("dp", "tensor"),
            P("tensor", "dp"),
            P(("dp", "tensor"), None),
            P(),
            P(),
            P(),
        ),
        out_specs=(
            P(("dp", "tensor"), None),
            P(("dp", "tensor"), None),
            P(),
            P(),
            P("dp", "tensor"),
            P("tensor", "dp"),
            P(None, "dp", "tensor"),
            P("tensor", "dp"),
            P(),
            P("dp", None, "tensor"),
            P(),
            P("tensor", "dp"),
            P("dp", "tensor"),
            P("tensor", "dp"),
        ),
        check_vma=False,
    )
```

time: 1960 us -> 826 us (0.42)
  waiting for transfers between devices: 1490 us -> 191 us
  starting transfers between devices: 1.66 us -> 147 us
  blocking collectives: 81.7 us -> 0 us
  local copies, waits for them, and re-layouts: 63 us -> 116 us
  matrix products: 227 us -> 255 us
  other arithmetic: 68.1 us -> 91.6 us
    reduce_scatter x16 -> x0, waiting for transfers between devices: 839 us -> none  [the longest x4 120 us: frames_reduce(): lax.psum_scatter(row_term(jnp.int32(0), rows_here * lax.axis_size('tensor...]
    all_gather x14 -> x0, waiting for transfers between devices: 393 us -> none  [the longest x4 93.8 us: frames_gather(): lax.all_gather(normed.astype(jnp.bfloat16), 'tensor', axis=0, tiled=True)]
    psum x2 -> x0, waiting for transfers between devices: 256 us -> none  [per_device(): lax.psum((gains_part, shifts_part, table_part, taps_part), ('dp', 'tensor'))]
    ppermute x0 -> x163, waiting for transfers between devices: none -> 191 us  [the longest x18 67 us: to_far(): lax.ppermute(v, 'tensor', [(m, m ^ 2) for m in range(lax.axis_size('tenso...]
    ppermute x0 -> x163, starting transfers between devices: none -> 147 us  [the longest x48 61 us: to_right(): lax.ppermute(v, 'dp', [(RING[i], RING[(i + 1) % n]) for i in range(n)])]
    all_gather x2 -> x0, blocking collectives: 63.6 us -> none  [the longest x1 32.1 us: per_device(): lax.all_gather(attend_out, 'dp', axis=1, tiled=True)]
    dot_general x48 -> x72, matrix products: 227 us -> 255 us  [the longest x2 81.2 us: attend_back(): jnp.einsum('hij,rij->hir', ds.astype(f32) * scale, band, precision=highest)]
  transfers between devices with their start and end apart: 32 -> 163, of which waited for: 31 -> 56; matrix products, arithmetic and copies ran while one was open for 4% -> 53% of each run, Pallas kernels for 0% -> 1%
where the time goes in v1:
time: 826 us; the launch traced here: 814 us
  matrix products  255 us (31%)
  waiting for transfers between devices  191 us (23%)
  starting transfers between devices  147 us (18%)
  local copies, waits for them, and re-layouts  116 us (14%)
  other arithmetic  91.6 us (11%)
    dot_general x2, matrix products, attend_back(): jnp.einsum('hij,rij->hir', ds.astype(f32) * scale, band, precision=highest)  81.2 us
    ppermute x18, waiting for transfers between devices, to_far(): lax.ppermute(v, 'tensor', [(m, m ^ 2) for m in range(lax.axis_size('tenso...  67 us
    dot_general x2, matrix products, scores_of(): relative = jnp.einsum('hir,rij->hij', by_dist, band, precision=highest)  66.5 us
    ppermute x48, starting transfers between devices, to_right(): lax.ppermute(v, 'dp', [(RING[i], RING[(i + 1) % n]) for i in range(n)])  61 us
    ppermute x48, waiting for transfers between devices, to_right(): lax.ppermute(v, 'dp', [(RING[i], RING[(i + 1) % n]) for i in range(n)])  50.7 us
    ppermute x48, starting transfers between devices, to_left(): lax.ppermute(v, 'dp', [(RING[i], RING[(i - 1) % n]) for i in range(n)])  50.2 us
    ppermute x48, waiting for transfers between devices, to_left(): lax.ppermute(v, 'dp', [(RING[i], RING[(i - 1) % n]) for i in range(n)])  38.9 us
    unnamed x570, local copies, waits for them, and re-layouts  38 us
  transfers between devices with their start and end apart: 163, of which 56 were waited for; matrix products, arithmetic and copies ran while one was open for 53% of the time, Pallas kernels for 1%

profile of v1, /device:TPU:0, one launch (start us, length us, event | category | flops | bytes accessed | tf_op | source)
XLA Modules:
  0.0 814.1 jit_solution(9841552379947253624)
XLA Ops:
  25.6 4.2 collective-permute-done.5
  32.7 4.3 collective-permute-done.10
  50.7 6.6 collective-permute-done.16
  86.7 7.5 collective-permute-done.21
  101.2 5.3 collective-permute-done.25
  116.4 4.7 concatenate.196
  126.6 33.3 %fusion.3 = f32[512,512,4]{1,2,0:T(4,128)} fusion(f32[73,512,4]{0,2,1:T(4,128)} %copy.112, s32[512,512]{1,0:T(8,128)} %clamp_add_fusion), kind=kOutput, calls=%fused_computation.4 | convolution fusion | flops 937689088 | bytes 5840896 | tf_op jit(solution)/shard_map/hir,rij->hij/dot_general | solution.py:224
  159.8 5.6 copy.113
  177.2 33.3 %fusion.2 = f32[512,512,4]{1,2,0:T(4,128)} fusion(f32[73,512,4]{0,2,1:T(4,128)} %copy.119, s32[512,512]{1,0:T(8,128)} %clamp_add_fusion), kind=kOutput, calls=%fused_computation.3 | convolution fusion | flops 937689088 | bytes 5840896 | tf_op jit(solution)/shard_map/hir,rij->hij/dot_general | solution.py:224
  210.5 5.4 copy.120
  257.2 8.2 %collective-permute-done.45 = bf16[256,1024]{1,0:T(8,128)(2,1)S(1)} collective-permute-done((bf16[256,1024]{1,0:T(8,128)(2,1)S(1)}, bf16[256,1024]{1,0:T(8,128)(2,1)S(1)}, u32[]{:S(2)}, u32[]{:S(2)}) %collective-permute-start.45) | collective-permute-done | bytes 524320 | tf_op jit(solution)/shard_map/ppermute | solution.py:58
  289.5 4.1 collective-permute-done.57
  319.6 10.2 %collective-permute-done.70 = bf16[256,1024]{1,0:T(8,128)(2,1)} collective-permute-done((bf16[256,1024]{1,0:T(8,128)(2,1)}, bf16[256,1024]{1,0:T(8,128)(2,1)}, u32[]{:S(2)}, u32[]{:S(2)}) %collective-permute-start.70) | collective-permute-done | bytes 524320 | tf_op jit(solution)/shard_map/ppermute | solution.py:58
  332.2 5.0 concatenate.212
  353.0 12.4 %collective-permute-done.73 = bf16[256,1024]{1,0:T(8,128)(2,1)} collective-permute-done((bf16[256,1024]{1,0:T(8,128)(2,1)}, bf16[256,1024]{1,0:T(8,128)(2,1)}, u32[]{:S(2)}, u32[]{:S(2)}) %collective-permute-start.73) | collective-permute-done | bytes 524320 | tf_op jit(solution)/shard_map/ppermute | solution.py:58
  377.1 7.0 collective-permute-done.76
  403.6 4.9 collective-permute-done.156
  416.9 4.6 collective-permute-done.157
  440.6 4.9 collective-permute-done.81
  479.1 5.3 stack.418
  498.2 7.5 collective-permute-done.87
  512.9 6.8 collective-permute-done.107
  537.4 5.4 copy.129
  542.8 40.3 %fusion.24 = f32[4,512,73]{2,0,1:T(4,128)} fusion(f32[4,512,512]{2,0,1:T(4,128)} %copy.129, s32[512,512]{1,0:T(8,128)} %clamp_add_fusion), kind=kOutput, calls=%fused_computation.118 | convolution fusion | flops 937689088 | bytes 5840896 | tf_op jit(solution)/shard_map/hij,rij->hir/dot_general | solution.py:256
  605.6 3.9 convert_multiply_fusion
  609.6 5.5 copy.139
  615.1 40.9 %fusion.25 = f32[4,512,73]{2,0,1:T(4,128)} fusion(f32[4,512,512]{2,0,1:T(4,128)} %copy.139, s32[512,512]{1,0:T(8,128)S(1)} %copy-done.72), kind=kOutput, calls=%fused_computation.119 | convolution fusion | flops 937689088 | bytes 5840896 | tf_op jit(solution)/shard_map/hij,rij->hir/dot_general | solution.py:256
  689.9 4.7 collective-permute-done.109
  726.6 4.9 collective-permute-done.96
  750.2 6.8 collective-permute-done.119
  765.5 4.5 collective-permute-done.123
  796.7 5.6 collective-permute-done.102
  (1217 shorter events, 494.2 us)
Async XLA Ops:
  0.7 21.6 %collective-permute-start.1 = (bf16[128,1024]{1,0:T(8,128)(2,1)}, bf16[128,1024]{1,0:T(8,128)(2,1)S(1)}, u32[]{:S(2)}, u32[]{:S(2)}) collective-permute-start(bf16[128,1024]{1,0:T(8,128)(2,1)} %param.21), channel_id=1, source_target_pairs={{0,4},{8,0},{16,8},{24,16},{28,24},{20,28},{12,20},{4,12},{1,5},{9... | collective-permute-start | bytes 786440 | tf_op jit(solution)/shard_map/ppermute | solution.py:68
  3.9 18.9 %collective-permute-start.9 = (bf16[128,1024]{0,1:T(8,128)(2,1)}, bf16[128,1024]{0,1:T(8,128)(2,1)S(1)}, u32[]{:S(2)}, u32[]{:S(2)}) collective-permute-start(bf16[128,1024]{0,1:T(8,128)(2,1)} %bitcast.391), channel_id=1, source_target_pairs={{0,4},{8,0},{16,8},{24,16},{28,24},{20,28},{12,20},{4,12},{1,5},{9... | collective-permute-start | bytes 786440 | tf_op jit(solution)/shard_map/ppermute | solution.py:68
  5.8 18.5 %collective-permute-start.12 = (bf16[128,1024]{0,1:T(8,128)(2,1)}, bf16[128,1024]{0,1:T(8,128)(2,1)S(1)}, u32[]{:S(2)}, u32[]{:S(2)}) collective-permute-start(bf16[128,1024]{0,1:T(8,128)(2,1)} %bitcast.392), channel_id=1, source_target_pairs={{0,8},{8,16},{16,24},{24,28},{28,20},{20,12},{12,4},{4,0},{1,9},{9... | collective-permute-start | bytes 786440 | tf_op jit(solution)/shard_map/ppermute | solution.py:63
  18.8 21.0 %collective-permute-start.18 = (bf16[256,1024]{1,0:T(8,128)(2,1)}, bf16[256,1024]{1,0:T(8,128)(2,1)}, u32[]{:S(2)}, u32[]{:S(2)}) collective-permute-start(bf16[256,1024]{1,0:T(8,128)(2,1)} %fusion.53), channel_id=1, source_target_pairs={{0,2},{1,3},{2,0},{3,1},{4,6},{5,7},{6,4},{7,5},{8,10},{9,11},{10,... | collective-permute-start | bytes 1572872 | tf_op jit(solution)/shard_map/ppermute | solution.py:58
  39.8 30.1 %collective-permute-start = (bf16[256,1024]{1,0:T(8,128)(2,1)}, bf16[256,1024]{1,0:T(8,128)(2,1)}, u32[]{:S(2)}, u32[]{:S(2)}) collective-permute-start(bf16[256,1024]{1,0:T(8,128)(2,1)} %fusion.53), channel_id=1, source_target_pairs={{0,1},{1,0},{2,3},{3,2},{4,5},{5,4},{6,7},{7,6},{8,9},{9,8},{10,11... | collective-permute-start | bytes 1572872 | tf_op jit(solution)/shard_map/ppermute | solution.py:54
  48.5 34.5 %collective-permute-start.23 = (bf16[128,1024]{0,1:T(8,128)(2,1)S(1)}, bf16[128,1024]{0,1:T(8,128)(2,1)}, u32[]{:S(2)}, u32[]{:S(2)}) collective-permute-start(bf16[128,1024]{0,1:T(8,128)(2,1)S(1)} %pad_maximum_fusion.27), channel_id=1, source_target_pairs={{0,4},{8,0},{16,8},{24,16},{28,24},{20,28},{12,20},{4,12},{1,5},{9... | collective-permute-start | bytes 786440 | tf_op jit(solution)/shard_map/ppermute | solution.py:68
  57.3 27.4 %collective-permute-start.26 = (bf16[128,1024]{0,1:T(8,128)(2,1)S(1)}, bf16[128,1024]{0,1:T(8,128)(2,1)}, u32[]{:S(2)}, u32[]{:S(2)}) collective-permute-start(bf16[128,1024]{0,1:T(8,128)(2,1)S(1)} %pad_maximum_fusion.27), channel_id=1, source_target_pairs={{0,8},{8,16},{16,24},{24,28},{28,20},{20,12},{12,4},{4,0},{1,9},{9... | collective-permute-start | bytes 786440 | tf_op jit(solution)/shard_map/ppermute | solution.py:63
  81.6 28.3 %collective-permute-start.37 = (bf16[128,768]{1,0:T(8,128)(2,1)}, bf16[128,768]{1,0:T(8,128)(2,1)}, u32[]{:S(2)}, u32[]{:S(2)}) collective-permute-start(bf16[128,768]{1,0:T(8,128)(2,1)} %get-tuple-element.275), channel_id=1, source_target_pairs={{0,4},{8,0},{16,8},{24,16},{28,24},{20,28},{12,20},{4,12},{1,5},{9... | collective-permute-start | bytes 589832 | tf_op jit(solution)/shard_map/ppermute | solution.py:68
  83.0 27.4 %collective-permute-start.40 = (bf16[128,768]{1,0:T(8,128)(2,1)}, bf16[128,768]{1,0:T(8,128)(2,1)}, u32[]{:S(2)}, u32[]{:S(2)}) collective-permute-start(bf16[128,768]{1,0:T(8,128)(2,1)} %get-tuple-element.275), channel_id=1, source_target_pairs={{0,8},{8,16},{16,24},{24,28},{28,20},{20,12},{12,4},{4,0},{1,9},{9... | collective-permute-start | bytes 589832 | tf_op jit(solution)/shard_map/ppermute | solution.py:63
  97.0 24.7 %collective-permute-start.22 = (bf16[256,1024]{1,0:T(8,128)(2,1)}, bf16[256,1024]{1,0:T(8,128)(2,1)}, u32[]{:S(2)}, u32[]{:S(2)}) collective-permute-start(bf16[256,1024]{1,0:T(8,128)(2,1)} %add_convert_fusion.14), channel_id=1, source_target_pairs={{0,1},{1,0},{2,3},{3,2},{4,5},{5,4},{6,7},{7,6},{8,9},{9,8},{10,11... | collective-permute-start | bytes 1572872 | tf_op jit(solution)/shard_map/ppermute | solution.py:54
  110.0 125.4 %collective-permute-start.38 = (bf16[128,768]{1,0:T(8,128)(2,1)}, bf16[128,768]{1,0:T(8,128)(2,1)}, u32[]{:S(2)}, u32[]{:S(2)}) collective-permute-start(bf16[128,768]{1,0:T(8,128)(2,1)} %collective-permute-done.37), channel_id=1, source_target_pairs={{0,4},{8,0},{16,8},{24,16},{28,24},{20,28},{12,20},{4,12},{1,5},{9... | collective-permute-start | bytes 589832 | tf_op jit(solution)/shard_map/ppermute | solution.py:68
  110.4 125.6 %collective-permute-start.41 = (bf16[128,768]{1,0:T(8,128)(2,1)}, bf16[128,768]{1,0:T(8,128)(2,1)}, u32[]{:S(2)}, u32[]{:S(2)}) collective-permute-start(bf16[128,768]{1,0:T(8,128)(2,1)} %collective-permute-done.40), channel_id=1, source_target_pairs={{0,8},{8,16},{16,24},{24,28},{28,20},{20,12},{12,4},{4,0},{1,9},{9... | collective-permute-start | bytes 589832 | tf_op jit(solution)/shard_map/ppermute | solution.py:63
  121.1 44.4 %collective-permute-start.32 = (bf16[256,1024]{1,0:T(8,128)(2,1)}, bf16[256,1024]{1,0:T(8,128)(2,1)S(1)}, u32[]{:S(2)}, u32[]{:S(2)}) collective-permute-start(bf16[256,1024]{1,0:T(8,128)(2,1)} %add_convert_fusion.14), channel_id=1, source_target_pairs={{0,2},{1,3},{2,0},{3,1},{4,6},{5,7},{6,4},{7,5},{8,10},{9,11},{10,... | collective-permute-start | bytes 1572872 | tf_op jit(solution)/shard_map/ppermute | solution.py:58
  296.3 19.2 %collective-permute-start.49 = (bf16[256,1024]{1,0:T(8,128)(2,1)S(1)}, bf16[256,1024]{1,0:T(8,128)(2,1)S(1)}, u32[]{:S(2)}, u32[]{:S(2)}) collective-permute-start(bf16[256,1024]{1,0:T(8,128)(2,1)S(1)} %slice.1753), channel_id=1, source_target_pairs={{0,1},{1,0},{2,3},{3,2},{4,5},{5,4},{6,7},{7,6},{8,9},{9,8},{10,11... | collective-permute-start | bytes 1572872 | tf_op jit(solution)/shard_map/ppermute | solution.py:54
  296.6 19.4 %collective-permute-start.51 = (bf16[256,1024]{1,0:T(8,128)(2,1)S(1)}, bf16[256,1024]{1,0:T(8,128)(2,1)S(1)}, u32[]{:S(2)}, u32[]{:S(2)}) collective-permute-start(bf16[256,1024]{1,0:T(8,128)(2,1)S(1)} %add_convert_fusion.11), channel_id=1, source_target_pairs={{0,2},{1,3},{2,0},{3,1},{4,6},{5,7},{6,4},{7,5},{8,10},{9,11},{10,... | collective-permute-start | bytes 1572872 | tf_op jit(solution)/shard_map/ppermute | solution.py:58
  319.3 19.0 %collective-permute-start.52 = (bf16[256,1024]{1,0:T(8,128)(2,1)}, bf16[256,1024]{1,0:T(8,128)(2,1)}, u32[]{:S(2)}, u32[]{:S(2)}) collective-permute-start(bf16[256,1024]{1,0:T(8,128)(2,1)} %add_convert_fusion.10), channel_id=1, source_target_pairs={{0,1},{1,0},{2,3},{3,2},{4,5},{5,4},{6,7},{7,6},{8,9},{9,8},{10,11... | collective-permute-start | bytes 1572872 | tf_op jit(solution)/shard_map/ppermute | solution.py:54
  374.3 58.3 %collective-permute-start.75 = (bf16[256,1024]{1,0:T(8,128)(2,1)S(1)}, bf16[256,1024]{1,0:T(8,128)(2,1)S(1)}, u32[]{:S(2)}, u32[]{:S(2)}) collective-permute-start(bf16[256,1024]{1,0:T(8,128)(2,1)S(1)} %slice.1769), channel_id=1, source_target_pairs={{0,1},{1,0},{2,3},{3,2},{4,5},{5,4},{6,7},{7,6},{8,9},{9,8},{10,11... | collective-permute-start | bytes 1572872 | tf_op jit(solution)/shard_map/ppermute | solution.py:54
  396.6 18.7 %collective-permute-start.160 = (bf16[128,1024]{1,0:T(8,128)(2,1)S(1)}, bf16[128,1024]{1,0:T(8,128)(2,1)S(1)}, u32[]{:S(2)}, u32[]{:S(2)}) collective-permute-start(bf16[128,1024]{1,0:T(8,128)(2,1)S(1)} %pad_maximum_fusion.37), channel_id=1, source_target_pairs={{0,4},{8,0},{16,8},{24,16},{28,24},{20,28},{12,20},{4,12},{1,5},{9... | collective-permute-start | bytes 786440 | tf_op jit(solution)/shard_map/ppermute | solution.py:68
  438.1 71.2 %collective-permute-start.150 = (bf16[128,1024]{1,0:T(8,128)(2,1)}, bf16[128,1024]{1,0:T(8,128)(2,1)}, u32[]{:S(2)}, u32[]{:S(2)}) collective-permute-start(bf16[128,1024]{1,0:T(8,128)(2,1)} %get-tuple-element.198), channel_id=1, source_target_pairs={{0,8},{8,16},{16,24},{24,28},{28,20},{20,12},{12,4},{4,0},{1,9},{9... | collective-permute-start | bytes 786440 | tf_op jit(solution)/shard_map/ppermute | solution.py:63
  473.2 19.9 %collective-permute-start.139 = (bf16[64,768]{0,1:T(8,128)(2,1)}, bf16[64,768]{0,1:T(8,128)(2,1)}, u32[]{:S(2)}, u32[]{:S(2)}) collective-permute-start(bf16[64,768]{0,1:T(8,128)(2,1)} %get-tuple-element.238), channel_id=1, source_target_pairs={{0,8},{8,16},{16,24},{24,28},{28,20},{20,12},{12,4},{4,0},{1,9},{9... | collective-permute-start | bytes 294920 | tf_op jit(solution)/shard_map/ppermute | solution.py:63
  473.6 21.2 %collective-permute-start.143 = (bf16[64,768]{0,1:T(8,128)(2,1)}, bf16[64,768]{0,1:T(8,128)(2,1)}, u32[]{:S(2)}, u32[]{:S(2)}) collective-permute-start(bf16[64,768]{0,1:T(8,128)(2,1)} %get-tuple-element.241), channel_id=1, source_target_pairs={{0,4},{8,0},{16,8},{24,16},{28,24},{20,28},{12,20},{4,12},{1,5},{9... | collective-permute-start | bytes 294920 | tf_op jit(solution)/shard_map/ppermute | solution.py:68
  476.4 21.2 %collective-permute-start.85 = (bf16[256,1024]{1,0:T(8,128)(2,1)}, bf16[256,1024]{1,0:T(8,128)(2,1)S(1)}, u32[]{:S(2)}, u32[]{:S(2)}) collective-permute-start(bf16[256,1024]{1,0:T(8,128)(2,1)} %slice.1783), channel_id=1, source_target_pairs={{0,1},{1,0},{2,3},{3,2},{4,5},{5,4},{6,7},{7,6},{8,9},{9,8},{10,11... | collective-permute-start | bytes 1572872 | tf_op jit(solution)/shard_map/ppermute | solution.py:54
  496.2 23.6 %collective-permute-start.144 = (bf16[128,768]{0,1:T(8,128)(2,1)S(1)}, bf16[128,768]{0,1:T(8,128)(2,1)S(1)}, u32[]{:S(2)}, u32[]{:S(2)}) collective-permute-start(bf16[128,768]{0,1:T(8,128)(2,1)S(1)} %pad_maximum_fusion.41), channel_id=1, source_target_pairs={{0,4},{8,0},{16,8},{24,16},{28,24},{20,28},{12,20},{4,12},{1,5},{9... | collective-permute-start | bytes 589832 | tf_op jit(solution)/shard_map/ppermute | solution.py:68
  508.7 19.0 %collective-permute-start.88 = (bf16[256,1024]{1,0:T(8,128)(2,1)}, bf16[256,1024]{1,0:T(8,128)(2,1)S(1)}, u32[]{:S(2)}, u32[]{:S(2)}) collective-permute-start(bf16[256,1024]{1,0:T(8,128)(2,1)} %get-tuple-element.168), channel_id=1, source_target_pairs={{0,1},{1,0},{2,3},{3,2},{4,5},{5,4},{6,7},{7,6},{8,9},{9,8},{10,11... | collective-permute-start | bytes 1572872 | tf_op jit(solution)/shard_map/ppermute | solution.py:54
  520.7 164.8 %collective-permute-start.141 = (bf16[128,768]{0,1:T(8,128)(2,1)}, bf16[128,768]{0,1:T(8,128)(2,1)}, u32[]{:S(2)}, u32[]{:S(2)}) collective-permute-start(bf16[128,768]{0,1:T(8,128)(2,1)} %get-tuple-element.234), channel_id=1, source_target_pairs={{0,8},{8,16},{16,24},{24,28},{28,20},{20,12},{12,4},{4,0},{1,9},{9... | collective-permute-start | bytes 589832 | tf_op jit(solution)/shard_map/ppermute | solution.py:63
  526.2 65.6 %collective-permute-start.90 = (bf16[256,1024]{1,0:T(8,128)(2,1)}, bf16[256,1024]{1,0:T(8,128)(2,1)}, u32[]{:S(2)}, u32[]{:S(2)}) collective-permute-start(bf16[256,1024]{1,0:T(8,128)(2,1)} %get-tuple-element.168), channel_id=1, source_target_pairs={{0,2},{1,3},{2,0},{3,1},{4,6},{5,7},{6,4},{7,5},{8,10},{9,11},{10,... | collective-permute-start | bytes 1572872 | tf_op jit(solution)/shard_map/ppermute | solution.py:58
  684.1 19.5 %collective-permute-start.89 = (bf16[256,1024]{1,0:T(8,128)(2,1)S(1)}, bf16[256,1024]{1,0:T(8,128)(2,1)S(1)}, u32[]{:S(2)}, u32[]{:S(2)}) collective-permute-start(bf16[256,1024]{1,0:T(8,128)(2,1)S(1)} %slice.1797), channel_id=1, source_target_pairs={{0,1},{1,0},{2,3},{3,2},{4,5},{5,4},{6,7},{7,6},{8,9},{9,8},{10,11... | collective-permute-start | bytes 1572872 | tf_op jit(solution)/shard_map/ppermute | solution.py:54
  715.8 47.6 %collective-permute-start.129 = (bf16[128,1024]{0,1:T(8,128)(2,1)S(1)}, bf16[128,1024]{0,1:T(8,128)(2,1)S(1)}, u32[]{:S(2)}, u32[]{:S(2)}) collective-permute-start(bf16[128,1024]{0,1:T(8,128)(2,1)S(1)} %get-tuple-element.206), channel_id=1, source_target_pairs={{0,8},{8,16},{16,24},{24,28},{28,20},{20,12},{12,4},{4,0},{1,9},{9... | collective-permute-start | bytes 786440 | tf_op jit(solution)/shard_map/ppermute | solution.py:63
  717.9 47.2 %collective-permute-start.133 = (bf16[128,1024]{0,1:T(8,128)(2,1)S(1)}, bf16[128,1024]{0,1:T(8,128)(2,1)S(1)}, u32[]{:S(2)}, u32[]{:S(2)}) collective-permute-start(bf16[128,1024]{0,1:T(8,128)(2,1)S(1)} %get-tuple-element.207), channel_id=1, source_target_pairs={{0,4},{8,0},{16,8},{24,16},{28,24},{20,28},{12,20},{4,12},{1,5},{9... | collective-permute-start | bytes 786440 | tf_op jit(solution)/shard_map/ppermute | solution.py:68
  757.1 20.8 %collective-permute-start.95 = (bf16[256,1024]{1,0:T(8,128)(2,1)S(1)}, bf16[256,1024]{1,0:T(8,128)(2,1)S(1)}, u32[]{:S(2)}, u32[]{:S(2)}) collective-permute-start(bf16[256,1024]{1,0:T(8,128)(2,1)S(1)} %slice.1805), channel_id=1, source_target_pairs={{0,1},{1,0},{2,3},{3,2},{4,5},{5,4},{6,7},{7,6},{8,9},{9,8},{10,11... | collective-permute-start | bytes 1572872 | tf_op jit(solution)/shard_map/ppermute | solution.py:54
  775.6 26.8 %collective-permute-start.121 = (bf16[128,1024]{1,0:T(8,128)(2,1)S(1)}, bf16[128,1024]{1,0:T(8,128)(2,1)S(1)}, u32[]{:S(2)}, u32[]{:S(2)}) collective-permute-start(bf16[128,1024]{1,0:T(8,128)(2,1)S(1)} %get-tuple-element.216), channel_id=1, source_target_pairs={{0,8},{8,16},{16,24},{24,28},{28,20},{20,12},{12,4},{4,0},{1,9},{9... | collective-permute-start | bytes 786440 | tf_op jit(solution)/shard_map/ppermute | solution.py:63
  777.9 30.2 %collective-permute-start.113 = (bf16[128,1024]{1,0:T(8,128)(2,1)S(1)}, bf16[128,1024]{1,0:T(8,128)(2,1)S(1)}, u32[]{:S(2)}, u32[]{:S(2)}) collective-permute-start(bf16[128,1024]{1,0:T(8,128)(2,1)S(1)} %get-tuple-element.224), channel_id=1, source_target_pairs={{0,8},{8,16},{16,24},{24,28},{28,20},{20,12},{12,4},{4,0},{1,9},{9... | collective-permute-start | bytes 786440 | tf_op jit(solution)/shard_map/ppermute | solution.py:63
  (398 other events, 4026.0 us)

commit v2 on v1

v2 whole, which is shorter than its diff:
```python
import jax
import jax.numpy as jnp
from jax import lax
from jax.experimental import pallas as pl
from jax.experimental.pallas import tpu as pltpu
from jax.sharding import PartitionSpec as P

D = 1024
HEAD_DIM = 64
KERNEL = 31
REL_LEFT = 64
REL_RIGHT = 8
CLIP_DEV = 2
L = 512
HALF = L // 2
RELS = 73

norm_eps = 1e-05
masked_score = -1e30
highest = lax.Precision.HIGHEST
f32 = jnp.float32
bf16 = jnp.bfloat16

RING = (0, 2, 4, 6, 7, 5, 3, 1)


def mm(a, b):
    return jnp.dot(a, b, preferred_element_type=f32)


def mm_tn(a, b):
    return lax.dot_general(a, b, (((0,), (0,)), ((), ())), preferred_element_type=f32)


def mm_nt(a, b):
    return lax.dot_general(a, b, (((1,), (1,)), ((), ())), preferred_element_type=f32)


def swish(h):
    return h * jax.nn.sigmoid(h)


def swish_grad(h):
    s = jax.nn.sigmoid(h)
    return s * (1.0 + h * (1.0 - s))


def to_core(v):
    return lax.ppermute(v, "tensor", [(m, m ^ 1) for m in range(lax.axis_size("tensor"))])


def to_far(v):
    return lax.ppermute(v, "tensor", [(m, m ^ 2) for m in range(lax.axis_size("tensor"))])


def to_right(v):
    n = len(RING)
    return lax.ppermute(v, "dp", [(RING[i], RING[(i + 1) % n]) for i in range(n)])


def to_left(v):
    n = len(RING)
    return lax.ppermute(v, "dp", [(RING[i], RING[(i - 1) % n]) for i in range(n)])


def on_ring():
    return lax.axis_size("dp") == len(RING)


def block_order():
    index = lax.axis_index("dp")
    count = lax.axis_size("dp")
    if not on_ring():
        return jnp.arange(count, dtype=jnp.int32)
    ring = jnp.array(RING, jnp.int32)
    place = jnp.sum(jnp.where(ring == index, jnp.arange(count, dtype=jnp.int32), 0))
    turned = (place + jnp.arange(count, dtype=jnp.int32)) % count
    return jnp.sum(jnp.where(turned[:, None] == jnp.arange(count)[None, :], ring[None, :], 0), axis=1)


def after(values, signal):
    return lax.optimization_barrier((values, signal))[0]


def gather_rows(shard):
    if not on_ring():
        return [lax.all_gather(shard, "dp", axis=0, tiled=True)], shard
    half = shard.shape[0] // 2
    r1, l1 = to_right(shard), to_left(shard)
    r2, l2 = to_right(r1), to_left(l1)
    r3, l3 = to_right(r2), to_left(l2)
    r4, l4 = to_right(r3[:half]), to_left(l3[half:])
    return [shard, l1, l2, l3, r4, l4, r3, r2, r1], (r3[:8], l3[:8])


def columns(pieces, start, stop):
    return jnp.concatenate([p[:, start:stop] for p in pieces], axis=0)


def scatter_rows(totals, signal):
    count = lax.axis_size("dp")
    rows = totals[0].shape[0] // count
    if not on_ring():
        total = jnp.concatenate(totals, axis=1)
        return lax.psum_scatter(total, "dp", scatter_dimension=0, tiled=True).astype(f32), signal
    half = rows // 2

    def part(start, stop):
        return jnp.concatenate([t[start:stop] for t in totals], axis=1)

    def block(k):
        return part(k * rows, (k + 1) * rows)

    def plus(a, b):
        return (a.astype(f32) + b.astype(f32)).astype(bf16)

    right, left = part(4 * rows, 4 * rows + half), part(4 * rows + half, 5 * rows)
    if signal is not None:
        right, left = after((right, left), signal)
    m = to_right(right)
    n = to_left(left)
    m = to_right(
        jnp.concatenate(
            [plus(part(3 * rows, 3 * rows + half), m), part(3 * rows + half, 4 * rows)], axis=0
        )
    )
    n = to_left(
        jnp.concatenate(
            [part(5 * rows, 5 * rows + half), plus(part(5 * rows + half, 6 * rows), n)], axis=0
        )
    )
    m = to_right(plus(block(2), m))
    n = to_left(plus(block(6), n))
    free = (m[:8], n[:8])
    m = to_right(plus(block(1), m))
    n = to_left(plus(block(7), n))
    return block(0).astype(f32) + m.astype(f32) + n.astype(f32), free


def sum_everywhere(value):
    for axis in ("tensor", "dp"):
        count = lax.axis_size(axis)
        bit = 1
        while bit < count:
            value = value + lax.ppermute(value, axis, [(m, m ^ bit) for m in range(count)])
            bit *= 2
    return value


def gather_clip(mine):
    return jnp.concatenate([mine, to_core(mine)], axis=0)


def reduce_clip(partial):
    rows = partial.shape[0] // 2
    partial = partial.astype(bf16)
    return partial[:rows].astype(f32) + to_core(partial[rows:]).astype(f32)


def gather_frames(mine):
    near = to_core(mine)
    far = to_far(mine)
    return jnp.concatenate([mine, near], axis=0), jnp.concatenate([far, to_core(far)], axis=0)


def reduce_frames(own, other):
    rows = own.shape[0] // 2
    own, other = own.astype(bf16), other.astype(bf16)
    near = to_core(own[rows:])
    near_other = to_core(other[rows:])
    far = to_far((other[:rows].astype(f32) + near_other.astype(f32)).astype(bf16))
    return own[:rows].astype(f32) + near.astype(f32) + far.astype(f32)


def permute_blocks(values, order):
    count = order.shape[0]
    if not on_ring():
        return values
    width = D // count

    def body(order_ref, *refs):
        ins, outs = refs[: len(values)], refs[len(values) :]
        for src, dst in zip(ins, outs):
            for k in range(count):
                at = pl.multiple_of(order_ref[k] * width, width)
                dst[:, k * width : (k + 1) * width] = src[:, pl.ds(at, width)]

    return pl.pallas_call(
        body,
        grid_spec=pltpu.PrefetchScalarGridSpec(
            num_scalar_prefetch=1,
            grid=(),
            in_specs=[pl.BlockSpec(memory_space=pltpu.VMEM) for _ in values],
            out_specs=[pl.BlockSpec(memory_space=pltpu.VMEM) for _ in values],
        ),
        out_shape=[jax.ShapeDtypeStruct(v.shape, v.dtype) for v in values],
    )(order, *values)


def norm_forward(v, gain, shift):
    centre = v - jnp.mean(v, axis=-1, keepdims=True)
    spread = jnp.mean(centre * centre, axis=-1, keepdims=True)
    r = lax.rsqrt(spread + norm_eps)
    unit = centre * r
    return unit * gain + shift, unit, r


def norm_backward(q, unit, r, gain):
    scaled = q * gain
    bracket = (
        scaled
        - jnp.mean(scaled, axis=-1, keepdims=True)
        - unit * jnp.mean(scaled * unit, axis=-1, keepdims=True)
    )
    return r * bracket, jnp.sum(q * unit, axis=0), jnp.sum(q, axis=0)


def ffn_forward(stream, gain, shift, up, down_t):
    normed, unit, r = norm_forward(stream, gain, shift)
    frames = gather_frames(normed.astype(bf16))
    hidden = [mm(x, up) for x in frames]
    active = [swish(h).astype(bf16) for h in hidden]
    branch = reduce_frames(*[mm_nt(a, down_t) for a in active])
    return stream + 0.5 * branch, (unit, r, frames, hidden, active)


def ffn_backward(upstream, gain, up, down_t, saved):
    unit, r, frames, hidden, active = saved
    incoming = gather_frames(upstream.astype(bf16))
    dhidden = [
        (0.5 * mm(g, down_t) * swish_grad(h)).astype(bf16) for g, h in zip(incoming, hidden)
    ]
    dnormed = reduce_frames(*[mm_nt(d, up) for d in dhidden])
    grad_down = (0.5 * sum(mm_tn(g, a) for g, a in zip(incoming, active))).astype(bf16)
    grad_up = sum(mm_tn(x, d) for x, d in zip(frames, dhidden)).astype(bf16)
    dstream, dgain, dshift = norm_backward(dnormed, unit, r, gain)
    return upstream + dstream, grad_up, grad_down, dgain, dshift


LANES = 128
SCALE = HEAD_DIM ** (-0.5)


def head_lanes(value, upper):
    lane = lax.broadcasted_iota(jnp.int32, value.shape, 1)
    return jnp.where((lane >= HEAD_DIM) == upper, value, jnp.zeros_like(value))


def either(first, second):
    lane = lax.broadcasted_iota(jnp.int32, first.shape, 1)
    return jnp.where(lane < HEAD_DIM, first, second)


def tile_probs(meta_ref, q, k, table):
    low, length = meta_ref[0], meta_ref[1]
    place_i = (lax.broadcasted_iota(jnp.int32, (L, L), 0) + low * HALF) & (L - 1)
    place_j = (lax.broadcasted_iota(jnp.int32, (L, L), 1) + low * HALF) & (L - 1)
    offset = place_j - place_i
    by_row = mm_nt(q, table)
    turned = pltpu.roll(by_row, REL_LEFT, 1, stride=1, stride_axis=0)
    turned = jnp.concatenate([turned] * (L // LANES), axis=1)
    relative = jnp.where(
        offset < -REL_LEFT,
        by_row[:, :1],
        jnp.where(offset >= LANES - REL_LEFT, by_row[:, LANES - 1 :], turned),
    )
    scores = (mm_nt(q, k) + relative) * SCALE
    scores = jnp.where(place_j < length, scores, masked_score)
    raised = jnp.exp(scores - jnp.max(scores, axis=-1, keepdims=True))
    return raised / jnp.sum(raised, axis=-1, keepdims=True), offset


def attend_body(meta_ref, q_ref, k_ref, v_ref, table_ref, out_ref):
    q, k, v, table = q_ref[...], k_ref[...], v_ref[...], table_ref[...]
    outs = []
    for upper in (False, True):
        shares, _ = tile_probs(meta_ref, head_lanes(q, upper), k, table)
        outs.append(mm(shares.astype(bf16), v))
    out_ref[...] = either(*outs).astype(bf16)


def pair_specs(pairs):
    def at(which):
        return pl.BlockSpec((L, LANES), lambda n, meta: (0, which * pairs + n))

    return [at(0), at(1), at(2)]


def attend(qkv, table, meta):
    width = qkv.shape[1] // 3
    pairs = width // LANES
    return pl.pallas_call(
        attend_body,
        grid_spec=pltpu.PrefetchScalarGridSpec(
            num_scalar_prefetch=1,
            grid=(pairs,),
            in_specs=pair_specs(pairs) + [pl.BlockSpec((LANES, LANES), lambda n, meta: (0, 0))],
            out_specs=pl.BlockSpec((L, LANES), lambda n, meta: (0, n)),
        ),
        out_shape=jax.ShapeDtypeStruct((L, width), bf16),
    )(meta, qkv, qkv, qkv, table)


def attend_back_body(
    meta_ref, q_ref, k_ref, v_ref, do_ref, table_ref, dq_ref, dk_ref, dv_ref, dtable_ref
):
    q, k, v, do, table = q_ref[...], k_ref[...], v_ref[...], do_ref[...], table_ref[...]
    lane = lax.broadcasted_iota(jnp.int32, (L, LANES), 1)
    row = lax.broadcasted_iota(jnp.int32, (L, LANES), 0)
    dqs, dks, dvs = [], [], []
    dtable = jnp.zeros((LANES, LANES), f32)
    for upper in (False, True):
        q_one = head_lanes(q, upper)
        shares, offset = tile_probs(meta_ref, q_one, k, table)
        dvs.append(mm_tn(shares.astype(bf16), do))
        dshares = mm_nt(head_lanes(do, upper), v)
        centre = jnp.sum(shares * dshares, axis=-1, keepdims=True)
        ds = (shares * (dshares - centre)).astype(bf16)
        wide = ds.astype(f32)
        before = offset < -REL_LEFT
        beyond = offset >= LANES - REL_LEFT
        left = jnp.sum(jnp.where(before, wide, 0.0), axis=-1, keepdims=True)
        right = jnp.sum(jnp.where(beyond, wide, 0.0), axis=-1, keepdims=True)
        band = jnp.where(before | beyond, 0.0, wide)
        pulled = sum(band[:, n * LANES : (n + 1) * LANES] for n in range(L // LANES))
        pulled = pltpu.roll(pulled, LANES - REL_LEFT, 1)
        bit = 1
        while bit < LANES:
            pulled = jnp.where((row & bit) != 0, pltpu.roll(pulled, LANES - bit, 1), pulled)
            bit *= 2
        pulled = pulled + jnp.where(lane == 0, left, 0.0) + jnp.where(lane == LANES - 1, right, 0.0)
        pulled = pulled.astype(bf16)
        dqs.append(mm(ds, k) + mm(pulled, table))
        dks.append(mm_tn(ds, q))
        dtable = dtable + mm_tn(pulled, q_one)
    dq_ref[...] = (either(*dqs) * SCALE).astype(bf16)
    dk_ref[...] = (either(*dks) * SCALE).astype(bf16)
    dv_ref[...] = either(*dvs).astype(bf16)

    @pl.when(pl.program_id(0) == 0)
    def _():
        dtable_ref[...] = jnp.zeros_like(dtable_ref)

    dtable_ref[...] += dtable * SCALE


def attend_back(qkv, dout, table, meta):
    width = qkv.shape[1] // 3
    pairs = width // LANES
    pair = pl.BlockSpec((L, LANES), lambda n, meta: (0, n))
    square = pl.BlockSpec((LANES, LANES), lambda n, meta: (0, 0))
    part = jax.ShapeDtypeStruct((L, width), bf16)
    return pl.pallas_call(
        attend_back_body,
        grid_spec=pltpu.PrefetchScalarGridSpec(
            num_scalar_prefetch=1,
            grid=(pairs,),
            in_specs=pair_specs(pairs) + [pair, square],
            out_specs=[pair, pair, pair, square],
        ),
        out_shape=[part, part, part, jax.ShapeDtypeStruct((LANES, LANES), f32)],
    )(meta, qkv, qkv, qkv, dout, table)


def attention_forward(stream, gain, shift, w_in, w_out_t, table, meta):
    normed, unit, r = norm_forward(stream, gain, shift)
    frames = gather_clip(normed.astype(bf16))
    qkv = mm(frames, w_in).astype(bf16)
    attended = attend(qkv, table, meta)
    branch = reduce_clip(mm_nt(attended, w_out_t))
    return stream + branch, (unit, r, frames, qkv, attended)


def attention_backward(upstream, gain, w_in, w_out_t, table, meta, saved):
    unit, r, frames, qkv, attended = saved
    incoming = gather_clip(upstream.astype(bf16))
    datt = mm(incoming, w_out_t).astype(bf16)
    dq, dk, dv, dtable = attend_back(qkv, datt, table, meta)
    width = dq.shape[1]
    dnormed = reduce_clip(
        sum(mm_nt(d, w_in[:, n * width : (n + 1) * width]) for n, d in enumerate((dq, dk, dv)))
    )
    grads = [mm_tn(frames, d).astype(bf16) for d in (dq, dk, dv)]
    grads.append(mm_tn(incoming, attended).astype(bf16))
    dstream, dgain, dshift = norm_backward(dnormed, unit, r, gain)
    return upstream + dstream, grads, dtable, dgain, dshift


PAD = 32
CHUNK = 64


def place_rows(dst, value, start, low):
    own = pl.multiple_of(start + low * HALF, 8)
    other = pl.multiple_of(start + (1 - low) * HALF, 8)
    dst[pl.ds(own, HALF), :] = value[:HALF]
    dst[pl.ds(other, HALF), :] = value[HALF:]


def taken_rows(src, start, low):
    own = pl.multiple_of(start + low * HALF, 8)
    other = pl.multiple_of(start + (1 - low) * HALF, 8)
    return src[pl.ds(own, HALF), :], src[pl.ds(other, HALF), :]


def shifted(window, shift):
    size = window.shape[0]
    turned = {}

    def at(first):
        part = first % 8
        if part not in turned:
            turned[part] = window if part == 0 else pltpu.roll(window, size - part, 0)
        base = first - part
        return turned[part][base : base + CHUNK]

    return at


def conv_body(meta_ref, linear_ref, gate_ref, taps_ref, out_ref, padded, placed):
    low = meta_ref[0]
    padded[:PAD, :] = jnp.zeros((PAD, LANES), f32)
    place_rows(padded, linear_ref[...] * jax.nn.sigmoid(gate_ref[...]), PAD, low)
    taps = taps_ref[...]

    def chunk(c, carry):
        base = pl.multiple_of(c * CHUNK, CHUNK)
        at = shifted(padded[pl.ds(base, CHUNK + PAD), :], 0)
        total = taps[0:1] * at(2)
        for k in range(1, KERNEL):
            total = total + taps[k : k + 1] * at(2 + k)
        placed[pl.ds(base, CHUNK), :] = total
        return carry

    lax.fori_loop(0, L // CHUNK, chunk, 0)
    out_ref[:HALF, :], out_ref[HALF:, :] = taken_rows(placed, 0, low)


def conv_back_body(
    meta_ref, dconv_ref, linear_ref, gate_ref, taps_ref, dlin_ref, dgate_ref, dtaps_ref, padded, late, placed
):
    low = meta_ref[0]
    linear, opened = linear_ref[...], jax.nn.sigmoid(gate_ref[...])
    padded[:PAD, :] = jnp.zeros((PAD, LANES), f32)
    place_rows(padded, linear * opened, PAD, low)
    late[L:, :] = jnp.zeros((PAD, LANES), f32)
    place_rows(late, dconv_ref[...], 0, low)
    taps = taps_ref[...]
    dtaps_ref[...] = jnp.zeros_like(dtaps_ref)

    def chunk(c, carry):
        base = pl.multiple_of(c * CHUNK, CHUNK)
        window = late[pl.ds(base, CHUNK + PAD), :]
        ahead = shifted(window, 0)
        back = shifted(padded[pl.ds(base, CHUNK + PAD), :], 0)
        here = window[:CHUNK]
        total = taps[KERNEL - 1 : KERNEL] * here
        for k in range(KERNEL - 1):
            total = total + taps[k : k + 1] * ahead(KERNEL - 1 - k)
        placed[pl.ds(base, CHUNK), :] = total
        for k in range(KERNEL):
            part = (back(2 + k) * here).reshape(CHUNK // 8, 8, LANES)
            dtaps_ref[8 * k : 8 * k + 8, :] += jnp.sum(part, axis=0)
        return carry

    lax.fori_loop(0, L // CHUNK, chunk, 0)
    dgated = jnp.concatenate(taken_rows(placed, 0, low), axis=0)
    dlin_ref[...] = (dgated * opened).astype(bf16)
    dgate_ref[...] = (dgated * linear * opened * (1.0 - opened)).astype(bf16)


def conv_specs(blocks):
    linear = pl.BlockSpec((L, LANES), lambda n, meta: (0, n))
    gate = pl.BlockSpec((L, LANES), lambda n, meta: (0, blocks + n))
    taps = pl.BlockSpec((PAD, LANES), lambda n, meta: (0, n))
    return linear, gate, taps


def conv_gated(halves, taps, meta):
    width = halves.shape[1] // 2
    linear, gate, tap = conv_specs(width // LANES)
    return pl.pallas_call(
        conv_body,
        grid_spec=pltpu.PrefetchScalarGridSpec(
            num_scalar_prefetch=1,
            grid=(width // LANES,),
            in_specs=[linear, gate, tap],
            out_specs=linear,
            scratch_shapes=[pltpu.VMEM((L + PAD, LANES), f32), pltpu.VMEM((L, LANES), f32)],
        ),
        out_shape=jax.ShapeDtypeStruct((L, width), f32),
    )(meta, halves, halves, taps)


def conv_gated_back(dconv, halves, taps, meta):
    width = dconv.shape[1]
    linear, gate, tap = conv_specs(width // LANES)
    long = pltpu.VMEM((L + PAD, LANES), f32)
    return pl.pallas_call(
        conv_back_body,
        grid_spec=pltpu.PrefetchScalarGridSpec(
            num_scalar_prefetch=1,
            grid=(width // LANES,),
            in_specs=[linear, linear, gate, tap],
            out_specs=[linear, linear, pl.BlockSpec((8 * PAD, LANES), lambda n, meta: (0, n))],
            scratch_shapes=[long, long, pltpu.VMEM((L, LANES), f32)],
        ),
        out_shape=[
            jax.ShapeDtypeStruct((L, width), bf16),
            jax.ShapeDtypeStruct((L, width), bf16),
            jax.ShapeDtypeStruct((8 * PAD, width), f32),
        ],
    )(meta, dconv, halves, halves, taps)


def near_rows(pair):
    return jnp.roll(to_core(pair), HALF, axis=-1)


def channel_stats(convolved):
    count = convolved.shape[1]
    mean = jnp.mean(convolved, axis=-1)
    centre = convolved - mean[:, None]
    pair = jnp.stack([mean, jnp.sum(centre * centre, axis=-1)])
    other = near_rows(pair)
    gap = pair[0] - other[0]
    mean = 0.5 * (pair[0] + other[0])
    spread = (pair[1] + other[1] + 0.5 * count * gap * gap) / (2 * count)
    return mean[:, None], lax.rsqrt(spread + norm_eps)[:, None]


def conv_forward(stream, gain, shift, w_in, taps, w_out_t, cgain, cshift, meta):
    normed, unit, r = norm_forward(stream, gain, shift)
    frames = gather_clip(normed.astype(bf16))
    halves = mm(frames, w_in)
    convolved = conv_gated(halves, taps, meta)
    mean, inverse = channel_stats(convolved)
    cunit = (convolved - mean) * inverse
    active = swish(cunit * cgain + cshift).astype(bf16)
    branch = reduce_clip(mm_nt(active, w_out_t))
    return stream + branch, (unit, r, frames, halves, cunit, inverse, active)


def conv_backward(upstream, gain, w_in, taps, w_out_t, cgain, cshift, meta, saved):
    unit, r, frames, halves, cunit, inverse, active = saved
    incoming = gather_clip(upstream.astype(bf16))
    dmid = mm(incoming, w_out_t) * swish_grad(cunit * cgain + cshift)
    scaled = dmid * cgain
    pair = jnp.stack([jnp.sum(scaled, axis=-1), jnp.sum(scaled * cunit, axis=-1)])
    pair = (pair + near_rows(pair)) / D
    dconv = inverse * (scaled - pair[0][:, None] - cunit * pair[1][:, None])
    dlin, dgate, dtaps = conv_gated_back(dconv, halves, taps, meta)
    width = dlin.shape[1]
    dnormed = reduce_clip(mm_nt(dlin, w_in[:, :width]) + mm_nt(dgate, w_in[:, width:]))
    grads = [mm_tn(frames, d).astype(bf16) for d in (dlin, dgate)]
    grads.append(mm_tn(incoming, active).astype(bf16))
    dtaps = jnp.sum(dtaps.reshape(PAD, 8, width), axis=1)[:KERNEL]
    sums = (dtaps, jnp.sum(dmid * cunit, axis=0), jnp.sum(dmid, axis=0))
    dstream, dgain, dshift = norm_backward(dnormed, unit, r, gain)
    return upstream + dstream, grads, sums, dgain, dshift


def spread_channels(part, member):
    zero = jnp.zeros(part.shape[:-1] + (D,), f32)
    return lax.dynamic_update_slice_in_dim(zero, part, member * part.shape[-1], part.ndim - 1)


def per_device(
    layer_in,
    norm_gain,
    norm_shift,
    early_up,
    early_down,
    attend_in,
    attend_out,
    position_table,
    pointwise_in,
    depthwise,
    pointwise_out,
    late_up,
    late_down,
    output_grad,
    clip_lengths,
    clip_slots,
    position_rows,
):
    group = lax.axis_index("dp")
    member = lax.axis_index("tensor")
    low = member % 2
    high = member // 2
    rows_here = layer_in.shape[0]
    block = early_up.shape[0]
    channels = depthwise.shape[1]

    order = block_order()
    count = order.shape[0]
    inverse_order = jnp.sum(
        jnp.where(
            order[None, :] == jnp.arange(count, dtype=jnp.int32)[:, None],
            jnp.arange(count, dtype=jnp.int32)[None, :],
            0,
        ),
        axis=1,
    )
    stream, cotangent, gains, shifts = permute_blocks(
        [layer_in, output_grad, norm_gain, norm_shift], order
    )

    slot = group * CLIP_DEV + high
    length = jnp.sum(jnp.where(clip_slots == slot, clip_lengths, 0))
    live = low * rows_here + jnp.arange(rows_here, dtype=jnp.int32) < length
    meta = jnp.stack([low, length]).astype(jnp.int32)

    selector = (position_rows[:, None] == jnp.arange(RELS, dtype=jnp.int32)[None, :]).astype(f32)
    table = jnp.dot(selector, position_table.astype(f32), precision=highest).astype(bf16)
    table = jnp.concatenate([table, jnp.broadcast_to(table[-1:], (LANES - RELS, HEAD_DIM))], axis=0)
    table = jnp.concatenate([table, table], axis=1)

    far_member = member ^ 2

    def both_members(row):
        return jnp.concatenate(
            [
                lax.dynamic_slice_in_dim(row, at * channels, channels)
                for at in (member, far_member)
            ]
        )

    cgain, cshift = both_members(norm_gain[3]), both_members(norm_shift[3])

    pack_attend = jnp.concatenate(
        [jnp.moveaxis(attend_in, 0, 1).reshape(block, -1), attend_out.T], axis=1
    )
    pack_conv = jnp.concatenate([pointwise_in.reshape(block, -1), pointwise_out.T], axis=1)
    far_attend = to_far(pack_attend)
    far_conv = to_far(pack_conv)
    taps = jnp.concatenate([depthwise, to_far(depthwise)], axis=1).astype(f32)
    taps = jnp.pad(taps, ((0, PAD - KERNEL), (0, 0)))

    def paired(own, far):
        parts = []
        for at in range(0, own.shape[1], channels):
            parts += [own[:, at : at + channels], far[:, at : at + channels]]
        return jnp.concatenate(parts, axis=1)

    both = 2 * channels
    p_early_up, signal = gather_rows(early_up)
    p_early_down, signal = gather_rows(after(early_down.T, signal))
    p_attend, signal = gather_rows(after(paired(pack_attend, far_attend), signal))
    p_conv, signal = gather_rows(after(paired(pack_conv, far_conv), signal))
    p_late, signal = gather_rows(after(jnp.concatenate([late_up, late_down.T], axis=1), signal))
    hidden_cols = early_up.shape[1]
    w_early_up = columns(p_early_up, 0, hidden_cols)
    w_early_down = columns(p_early_down, 0, hidden_cols)
    w_att_in, w_att_out = columns(p_attend, 0, 3 * both), columns(p_attend, 3 * both, 4 * both)
    w_pi, w_po = columns(p_conv, 0, 2 * both), columns(p_conv, 2 * both, 3 * both)
    w_late_up = columns(p_late, 0, hidden_cols)
    w_late_down = columns(p_late, hidden_cols, 2 * hidden_cols)

    stream0 = stream.astype(f32)
    stream1, saved_early = ffn_forward(stream0, gains[0], shifts[0], w_early_up, w_early_down)
    stream2, saved_attend = attention_forward(
        stream1, gains[1], shifts[1], w_att_in, w_att_out, table, meta
    )
    stream3, saved_conv = conv_forward(
        stream2, gains[2], shifts[2], w_pi, taps, w_po, cgain, cshift, meta
    )
    stream4, saved_late = ffn_forward(stream3, gains[4], shifts[4], w_late_up, w_late_down)
    result, unit5, r5 = norm_forward(stream4, gains[5], shifts[5])

    up = jnp.where(live[:, None], cotangent.astype(f32), 0.0)
    up, gain5, shift5 = norm_backward(up, unit5, r5, gains[5])
    up, g_late_up, g_late_down, gain4, shift4 = ffn_backward(
        up, gains[4], w_late_up, w_late_down, saved_late
    )
    g_late, signal = scatter_rows([g_late_up, g_late_down], None)
    up, g_conv, (g_taps, gain3, shift3), gain2, shift2 = conv_backward(
        up, gains[2], w_pi, taps, w_po, cgain, cshift, meta, saved_conv
    )
    g_conv, signal = scatter_rows(g_conv, signal)
    up, g_attend, g_table, gain1, shift1 = attention_backward(
        up, gains[1], w_att_in, w_att_out, table, meta, saved_attend
    )
    g_attend, signal = scatter_rows(g_attend, signal)
    up, g_early_up, g_early_down, gain0, shift0 = ffn_backward(
        up, gains[0], w_early_up, w_early_down, saved_early
    )
    g_early_down, signal = scatter_rows([g_early_down], signal)
    g_early_up, signal = scatter_rows([g_early_up], signal)

    def own_and_far(grad):
        own = [grad[:, at : at + channels] for at in range(0, grad.shape[1], both)]
        far = [grad[:, at + channels : at + both] for at in range(0, grad.shape[1], both)]
        far = to_far(jnp.concatenate(far, axis=1).astype(bf16)).astype(f32)
        return [o + far[:, n * channels : (n + 1) * channels] for n, o in enumerate(own)]

    g_q, g_k, g_v, g_out = own_and_far(g_attend)
    g_linear, g_gate, g_po = own_and_far(g_conv)

    result, norms = permute_blocks(
        [
            result.astype(bf16),
            jnp.stack([gain1, gain2, gain4, gain5, shift1, shift2, shift4, shift5]),
        ],
        inverse_order,
    )
    up, first = permute_blocks([up, jnp.stack([gain0, shift0] + [jnp.zeros((D,), f32)] * 6)], inverse_order)
    side = jnp.concatenate([g_taps, gain3[None], shift3[None]], axis=0)
    side = spread_channels(side[:, :channels], member) + spread_channels(side[:, channels:], far_member)
    g_table = g_table[:, :HEAD_DIM] + g_table[:, HEAD_DIM:]
    g_table = jnp.concatenate(
        [g_table[: RELS - 1], jnp.sum(g_table[RELS - 1 :], axis=0, keepdims=True)], axis=0
    )
    g_table = jnp.dot(selector.T, g_table, precision=highest)
    g_table = jnp.pad(g_table.reshape(-1), (0, 5 * D - RELS * HEAD_DIM)).reshape(5, D)
    sums = sum_everywhere(jnp.concatenate([norms, side, g_table], axis=0))
    first = sum_everywhere(first[:2])
    after_side = 8 + side.shape[0]
    side = sums[8:after_side]
    gains_all = jnp.concatenate([first[:1], sums[0:2], side[KERNEL : KERNEL + 1], sums[2:4]], axis=0)
    shifts_all = jnp.concatenate([first[1:], sums[4:6], side[KERNEL + 1 :], sums[6:8]], axis=0)
    table_all = sums[after_side:].reshape(-1)[: RELS * HEAD_DIM].reshape(RELS, HEAD_DIM)

    return (
        result,
        up,
        gains_all,
        shifts_all,
        g_early_up,
        g_early_down.T,
        jnp.stack([g_q, g_k, g_v]),
        g_out.T,
        table_all,
        jnp.stack([g_linear, g_gate], axis=1),
        side[:KERNEL],
        g_po.T,
        g_late[:, :hidden_cols],
        g_late[:, hidden_cols:].T,
    )


def solution(mesh):
    return jax.shard_map(
        per_device,
        mesh=mesh,
        in_specs=(
            P(("dp", "tensor"), None),
            P(),
            P(),
            P("dp", "tensor"),
            P("tensor", "dp"),
            P(None, "dp", "tensor"),
            P("tensor", "dp"),
            P(),
            P("dp", None, "tensor"),
            P(None, "tensor"),
            P("tensor", "dp"),
            P("dp", "tensor"),
            P("tensor", "dp"),
            P(("dp", "tensor"), None),
            P(),
            P(),
            P(),
        ),
        out_specs=(
            P(("dp", "tensor"), None),
            P(("dp", "tensor"), None),
            P(),
            P(),
            P("dp", "tensor"),
            P("tensor", "dp"),
            P(None, "dp", "tensor"),
            P("tensor", "dp"),
            P(),
            P("dp", None, "tensor"),
            P(),
            P("tensor", "dp"),
            P("dp", "tensor"),
            P("tensor", "dp"),
        ),
        check_vma=False,
    )
```

time: 826 us -> 685 us (0.83)
  matrix products: 255 us -> 83.3 us
  Pallas kernels: 6.71 us -> 68.8 us
  local copies, waits for them, and re-layouts: 116 us -> 155 us
  waiting for transfers between devices: 191 us -> 157 us
  starting transfers between devices: 147 us -> 114 us
    dot_general x23 -> x1, matrix products: 178 us -> 0.92 us  [per_device(): g_table = jnp.dot(selector.T, g_table, precision=highest)]
    pallas_call x0 -> x4, Pallas kernels: none -> 59.9 us  [the longest x1 27.5 us: attend_back(): pl.pallas_call(attend_back_body, grid_spec=pltpu.PrefetchScalarGridSpec(n...]
    slice x37 -> x84, local copies, waits for them, and re-layouts: 6.23 us -> 61.2 us  [the longest x47 43.9 us: columns(): return jnp.concatenate([p[:, start:stop] for p in pieces], axis=0)]
    ppermute x48 -> x40, starting transfers between devices: 61 us -> 28.8 us  [to_right(): lax.ppermute(v, 'dp', [(RING[i], RING[(i + 1) % n]) for i in range(n)])]
    ppermute x18 -> x13, waiting for transfers between devices: 67 us -> 37.9 us  [to_far(): lax.ppermute(v, 'tensor', [(m, m ^ 2) for m in range(lax.axis_size('tenso...]
    concatenate x6 -> x10, local copies, waits for them, and re-layouts: 16.9 us -> 40.7 us  [the longest x8 39.2 us: columns(): return jnp.concatenate([p[:, start:stop] for p in pieces], axis=0)]
    ppermute x48 -> x40, waiting for transfers between devices: 38.9 us -> 61.9 us  [to_left(): lax.ppermute(v, 'dp', [(RING[i], RING[(i - 1) % n]) for i in range(n)])]
    ppermute x15 -> x10, waiting for transfers between devices: 32.1 us -> 18.1 us  [sum_everywhere(): lax.ppermute(value, axis, [(m, m ^ bit) for m in range(count)])]
  transfers between devices with their start and end apart: 163 -> 129, of which waited for: 56 -> 38; matrix products, arithmetic and copies ran while one was open for 53% -> 46% of each run, Pallas kernels for 1% -> 10%
where the time goes in v2:
time: 685 us; the launch traced here: 672 us
  waiting for transfers between devices  157 us (23%)
  local copies, waits for them, and re-layouts  155 us (23%)
  starting transfers between devices  114 us (17%)
  other arithmetic  89.5 us (13%)
  matrix products  83.3 us (12%)
  Pallas kernels  68.8 us (10%)
    ppermute x40, waiting for transfers between devices, to_left(): lax.ppermute(v, 'dp', [(RING[i], RING[(i - 1) % n]) for i in range(n)])  61.9 us
    ppermute x40, starting transfers between devices, to_left(): lax.ppermute(v, 'dp', [(RING[i], RING[(i - 1) % n]) for i in range(n)])  59.9 us
    slice x47, local copies, waits for them, and re-layouts, columns(): return jnp.concatenate([p[:, start:stop] for p in pieces], axis=0)  43.9 us
    concatenate x8, local copies, waits for them, and re-layouts, columns(): return jnp.concatenate([p[:, start:stop] for p in pieces], axis=0)  39.2 us
    ppermute x40, waiting for transfers between devices, to_right(): lax.ppermute(v, 'dp', [(RING[i], RING[(i + 1) % n]) for i in range(n)])  38.8 us
    ppermute x13, waiting for transfers between devices, to_far(): lax.ppermute(v, 'tensor', [(m, m ^ 2) for m in range(lax.axis_size('tenso...  37.9 us
    dot_general x12, matrix products, mm(): return jnp.dot(a, b, preferred_element_type=f32)  32.5 us
    unnamed x384, local copies, waits for them, and re-layouts  32.3 us
  transfers between devices with their start and end apart: 129, of which 38 were waited for; matrix products, arithmetic and copies ran while one was open for 46% of the time, Pallas kernels for 10%

profile of v2, /device:TPU:0, one launch (start us, length us, event | category | flops | bytes accessed | tf_op | source)
XLA Modules:
  0.0 671.7 jit_solution(11390306527126597721)
XLA Ops:
  30.9 5.0 collective-permute-done.13
  57.3 5.9 collective-permute-done.3
  63.9 4.5 collective-permute-done.15
  73.7 4.5 concatenate.251
  100.8 8.1 %collective-permute-done.21 = bf16[256,1024]{1,0:T(8,128)(2,1)S(1)} collective-permute-done((bf16[256,1024]{1,0:T(8,128)(2,1)S(1)}, bf16[256,1024]{1,0:T(8,128)(2,1)S(1)}, u32[]{:S(2)}, u32[]{:S(2)}) %collective-permute-start.21) | collective-permute-done | bytes 524320 | tf_op jit(solution)/shard_map/ppermute | solution.py:53
  131.0 5.9 concatenate.256
  141.5 5.6 convolution_convert_fusion.q_ref.k_ref.v_ref
  147.2 16.1 %shard_map.282 = bf16[512,512]{1,0:T(8,128)(2,1)} custom-call(s32[2]{0:T(128)} %pad_add_fusion.meta_ref, bf16[512,1536]{1,0:T(8,128)(2,1)} %convolution_convert_fusion.q_ref.k_ref.v_ref, bf16[512,1536]{1,0:T(8,128)(2,1)} %convolution_convert_fusion.q_ref.k_ref.v_ref, bf16[512,1536]{1,0:T(8,128)(2,1)} %convolution_convert_fusion.q_ref.k_ref.v_ref, ...), custom_call_target="tpu_custom_call" | custom-call | tf_op jit(solution)/shard_map/pallas_call | solution.py:292
  172.1 6.4 collective-permute-done.36
  184.2 13.4 %collective-permute-done.37 = bf16[128,1536]{0,1:T(8,128)(2,1)S(1)} collective-permute-done((bf16[128,1536]{0,1:T(8,128)(2,1)}, bf16[128,1536]{0,1:T(8,128)(2,1)S(1)}, u32[]{:S(2)}, u32[]{:S(2)}) %collective-permute-start.37) | collective-permute-done | bytes 393248 | tf_op jit(solution)/shard_map/ppermute | solution.py:63
  217.1 4.6 concatenate.263
  221.7 4.6 fusion.40.linear_ref.gate_ref
  226.2 6.3 shard_map.283
  272.3 4.3 collective-permute-done.53
  277.4 3.7 collective-permute-done.56
  282.0 4.6 concatenate.271
  286.6 13.0 %concatenate.272 = bf16[1024,1024]{0,1:T(8,128)(2,1)} concatenate(bf16[128,1024]{0,1:T(8,128)(2,1)S(1)} %copy-done.33, bf16[128,1024]{0,1:T(8,128)(2,1)} %get-tuple-element.288, bf16[128,1024]{0,1:T(8,128)(2,1)} %get-tuple-element.286, bf16[128,1024]{0,1:T(8,128)(2,1)} %get-tuple-element.284, bf16[64,1024]{0,1:T(8,128)(2,1)} %get-tuple-element.282, ...), dimensions={0} | concatenate | bytes 4194304 | tf_op jit(solution)/shard_map/concatenate | solution.py:97
  314.8 12.6 %collective-permute-done.59 = bf16[256,1024]{1,0:T(8,128)(2,1)} collective-permute-done((bf16[256,1024]{1,0:T(8,128)(2,1)}, bf16[256,1024]{1,0:T(8,128)(2,1)}, u32[]{:S(2)}, u32[]{:S(2)}) %collective-permute-start.59) | collective-permute-done | bytes 524320 | tf_op jit(solution)/shard_map/ppermute | solution.py:53
  340.1 7.0 %collective-permute-done.62 = bf16[256,1024]{1,0:T(8,128)(2,1)S(1)} collective-permute-done((bf16[256,1024]{1,0:T(8,128)(2,1)S(1)}, bf16[256,1024]{1,0:T(8,128)(2,1)S(1)}, u32[]{:S(2)}, u32[]{:S(2)}) %collective-permute-start.62) | collective-permute-done | bytes 524320 | tf_op jit(solution)/shard_map/ppermute | solution.py:53
  358.8 5.6 collective-permute-done.125
  368.5 9.4 %collective-permute-done.126 = bf16[128,2048]{1,0:T(8,128)(2,1)S(1)} collective-permute-done((bf16[128,2048]{1,0:T(8,128)(2,1)S(1)}, bf16[128,2048]{1,0:T(8,128)(2,1)S(1)}, u32[]{:S(2)}, u32[]{:S(2)}) %collective-permute-start.126) | collective-permute-done | bytes 524320 | tf_op jit(solution)/shard_map/ppermute | solution.py:63
  383.6 6.9 %collective-permute-done.127 = bf16[128,2048]{1,0:T(8,128)(2,1)S(1)} collective-permute-done((bf16[128,2048]{1,0:T(8,128)(2,1)S(1)}, bf16[128,2048]{1,0:T(8,128)(2,1)S(1)}, u32[]{:S(2)}, u32[]{:S(2)}) %collective-permute-start.127) | collective-permute-done | bytes 524320 | tf_op jit(solution)/shard_map/ppermute | solution.py:63
  399.8 9.9 %shard_map.284 = (bf16[512,512]{1,0:T(8,128)(2,1)}, bf16[512,512]{1,0:T(8,128)(2,1)}, f32[256,512]{1,0:T(8,128)}) custom-call(s32[2]{0:T(128)} %pad_add_fusion.meta_ref, f32[512,512]{1,0:T(8,128)} %subtract_multiply_fusion.dconv_ref, f32[512,1024]{1,0:T(8,128)} %fusion.40.linear_ref.gate_ref, f32[512,1024]{1,0:T(8,128)} %fusion.40.linear_ref.gate_ref, ...), custom_call_target="tpu_custom_call" | custom-call | tf_op jit(solution)/shard_map/pallas_call | solution.py:499
  445.3 8.0 %collective-permute-done.118 = bf16[128,1536]{1,0:T(8,128)(2,1)S(1)} collective-permute-done((bf16[128,1536]{1,0:T(8,128)(2,1)S(1)}, bf16[128,1536]{1,0:T(8,128)(2,1)S(1)}, u32[]{:S(2)}, u32[]{:S(2)}) %collective-permute-start.118) | collective-permute-done | bytes 393248 | tf_op jit(solution)/shard_map/ppermute | solution.py:63
  458.7 27.5 %shard_map.285 = (bf16[512,512]{1,0:T(8,128)(2,1)}, bf16[512,512]{1,0:T(8,128)(2,1)}, bf16[512,512]{1,0:T(8,128)(2,1)}, f32[128,128]{1,0:T(8,128)}) custom-call(s32[2]{0:T(128)} %pad_add_fusion.meta_ref, bf16[512,1536]{1,0:T(8,128)(2,1)} %convolution_convert_fusion.q_ref.k_ref.v_ref, bf16[512,1536]{1,0:T(8,128)(2,1)} %convolution_convert_fusion.q_ref.k_ref.v_ref, ...), custom_call_target="tpu_custom_call" | custom-call | tf_op jit(solution)/shard_map/pallas_call | solution.py:353
  553.6 4.6 fusion.34
  563.2 4.6 fusion.38
  573.2 6.6 collective-permute-done.86
  584.3 3.7 multiply_convert_fusion.2
  621.2 5.6 collective-permute-done.76
  648.0 3.8 collective-permute-done.79
  664.5 3.7 collective-permute-done.102
  (937 shorter events, 431.6 us)
Async XLA Ops:
  0.7 28.0 %collective-permute-start.9 = (bf16[128,1024]{0,1:T(8,128)(2,1)}, bf16[128,1024]{0,1:T(8,128)(2,1)S(1)}, u32[]{:S(2)}, u32[]{:S(2)}) collective-permute-start(bf16[128,1024]{0,1:T(8,128)(2,1)} %bitcast.134), channel_id=1, source_target_pairs={{0,4},{8,0},{16,8},{24,16},{28,24},{20,28},{12,20},{4,12},{1,5},{9... | collective-permute-start | bytes 786440 | tf_op jit(solution)/shard_map/ppermute | solution.py:63
  3.9 24.9 %collective-permute-start.1 = (bf16[128,1024]{1,0:T(8,128)(2,1)}, bf16[128,1024]{1,0:T(8,128)(2,1)S(1)}, u32[]{:S(2)}, u32[]{:S(2)}) collective-permute-start(bf16[128,1024]{1,0:T(8,128)(2,1)} %param.21), channel_id=1, source_target_pairs={{0,4},{8,0},{16,8},{24,16},{28,24},{20,28},{12,20},{4,12},{1,5},{9... | collective-permute-start | bytes 786440 | tf_op jit(solution)/shard_map/ppermute | solution.py:63
  5.8 24.9 %collective-permute-start.4 = (bf16[128,1024]{1,0:T(8,128)(2,1)}, bf16[128,1024]{1,0:T(8,128)(2,1)S(1)}, u32[]{:S(2)}, u32[]{:S(2)}) collective-permute-start(bf16[128,1024]{1,0:T(8,128)(2,1)} %param.21), channel_id=1, source_target_pairs={{0,8},{8,16},{16,24},{24,28},{28,20},{20,12},{12,4},{4,0},{1,9},{9... | collective-permute-start | bytes 786440 | tf_op jit(solution)/shard_map/ppermute | solution.py:58
  43.5 34.8 %collective-permute-start.24 = (bf16[128,2048]{0,1:T(8,128)(2,1)S(1)}, bf16[128,2048]{0,1:T(8,128)(2,1)S(1)}, u32[]{:S(2)}, u32[]{:S(2)}) collective-permute-start(bf16[128,2048]{0,1:T(8,128)(2,1)S(1)} %slice_dynamic-update-slice_fusion.5), channel_id=1, source_target_pairs={{0,4},{8,0},{16,8},{24,16},{28,24},{20,28},{12,20},{4,12},{1,5},{9... | collective-permute-start | bytes 1572872 | tf_op jit(solution)/shard_map/ppermute | solution.py:63
  43.6 35.0 %collective-permute-start.27 = (bf16[128,2048]{0,1:T(8,128)(2,1)S(1)}, bf16[128,2048]{0,1:T(8,128)(2,1)}, u32[]{:S(2)}, u32[]{:S(2)}) collective-permute-start(bf16[128,2048]{0,1:T(8,128)(2,1)S(1)} %slice_dynamic-update-slice_fusion.5), channel_id=1, source_target_pairs={{0,8},{8,16},{16,24},{24,28},{28,20},{20,12},{12,4},{4,0},{1,9},{9... | collective-permute-start | bytes 1572872 | tf_op jit(solution)/shard_map/ppermute | solution.py:58
  72.2 24.4 %collective-permute-start.34 = (bf16[128,768]{0,1:T(8,128)(2,1)}, bf16[128,768]{0,1:T(8,128)(2,1)}, u32[]{:S(2)}, u32[]{:S(2)}) collective-permute-start(bf16[128,768]{0,1:T(8,128)(2,1)} %pad_maximum_fusion.39), channel_id=1, source_target_pairs={{0,2},{1,3},{2,0},{3,1},{4,6},{5,7},{6,4},{7,5},{8,10},{9,11},{10,... | collective-permute-start | bytes 589832 | tf_op jit(solution)/shard_map/ppermute | solution.py:53
  110.7 30.8 %collective-permute-start.22 = (bf16[256,1024]{1,0:T(8,128)(2,1)}, bf16[256,1024]{1,0:T(8,128)(2,1)}, u32[]{:S(2)}, u32[]{:S(2)}) collective-permute-start(bf16[256,1024]{1,0:T(8,128)(2,1)} %add_convert_fusion.18), channel_id=1, source_target_pairs={{0,1},{1,0},{2,3},{3,2},{4,5},{5,4},{6,7},{7,6},{8,9},{9,8},{10,11... | collective-permute-start | bytes 1572872 | tf_op jit(solution)/shard_map/ppermute | solution.py:49
  118.1 48.1 %collective-permute-start.35 = (bf16[128,1536]{0,1:T(8,128)(2,1)}, bf16[128,1536]{0,1:T(8,128)(2,1)}, u32[]{:S(2)}, u32[]{:S(2)}) collective-permute-start(bf16[128,1536]{0,1:T(8,128)(2,1)} %slice_dynamic-update-slice_fusion), channel_id=1, source_target_pairs={{0,4},{8,0},{16,8},{24,16},{28,24},{20,28},{12,20},{4,12},{1,5},{9... | collective-permute-start | bytes 1179656 | tf_op jit(solution)/shard_map/ppermute | solution.py:63
  119.7 48.1 %collective-permute-start.38 = (bf16[128,1536]{0,1:T(8,128)(2,1)}, bf16[128,1536]{0,1:T(8,128)(2,1)}, u32[]{:S(2)}, u32[]{:S(2)}) collective-permute-start(bf16[128,1536]{0,1:T(8,128)(2,1)} %slice_dynamic-update-slice_fusion), channel_id=1, source_target_pairs={{0,8},{8,16},{16,24},{24,28},{28,20},{20,12},{12,4},{4,0},{1,9},{9... | collective-permute-start | bytes 1179656 | tf_op jit(solution)/shard_map/ppermute | solution.py:58
  168.5 38.1 %collective-permute-start.47 = (bf16[128,2048]{0,1:T(8,128)(2,1)S(1)}, bf16[128,2048]{0,1:T(8,128)(2,1)}, u32[]{:S(2)}, u32[]{:S(2)}) collective-permute-start(bf16[128,2048]{0,1:T(8,128)(2,1)S(1)} %pad_maximum_fusion.20), channel_id=1, source_target_pairs={{0,4},{8,0},{16,8},{24,16},{28,24},{20,28},{12,20},{4,12},{1,5},{9... | collective-permute-start | bytes 1572872 | tf_op jit(solution)/shard_map/ppermute | solution.py:63
  170.1 38.1 %collective-permute-start.50 = (bf16[128,2048]{0,1:T(8,128)(2,1)S(1)}, bf16[128,2048]{0,1:T(8,128)(2,1)}, u32[]{:S(2)}, u32[]{:S(2)}) collective-permute-start(bf16[128,2048]{0,1:T(8,128)(2,1)S(1)} %pad_maximum_fusion.20), channel_id=1, source_target_pairs={{0,8},{8,16},{16,24},{24,28},{28,20},{20,12},{12,4},{4,0},{1,9},{9... | collective-permute-start | bytes 1572872 | tf_op jit(solution)/shard_map/ppermute | solution.py:58
  183.4 38.3 %collective-permute-start.33 = (bf16[256,1024]{1,0:T(8,128)(2,1)}, bf16[256,1024]{1,0:T(8,128)(2,1)}, u32[]{:S(2)}, u32[]{:S(2)}) collective-permute-start(bf16[256,1024]{1,0:T(8,128)(2,1)} %add_convert_fusion.17), channel_id=1, source_target_pairs={{0,1},{1,0},{2,3},{3,2},{4,5},{5,4},{6,7},{7,6},{8,9},{9,8},{10,11... | collective-permute-start | bytes 1572872 | tf_op jit(solution)/shard_map/ppermute | solution.py:49
  206.7 37.6 %collective-permute-start.48 = (bf16[128,2048]{0,1:T(8,128)(2,1)}, bf16[128,2048]{0,1:T(8,128)(2,1)}, u32[]{:S(2)}, u32[]{:S(2)}) collective-permute-start(bf16[128,2048]{0,1:T(8,128)(2,1)} %collective-permute-done.47), channel_id=1, source_target_pairs={{0,4},{8,0},{16,8},{24,16},{28,24},{20,28},{12,20},{4,12},{1,5},{9... | collective-permute-start | bytes 1572872 | tf_op jit(solution)/shard_map/ppermute | solution.py:63
  208.3 37.5 %collective-permute-start.51 = (bf16[128,2048]{0,1:T(8,128)(2,1)}, bf16[128,2048]{0,1:T(8,128)(2,1)}, u32[]{:S(2)}, u32[]{:S(2)}) collective-permute-start(bf16[128,2048]{0,1:T(8,128)(2,1)} %collective-permute-done.50), channel_id=1, source_target_pairs={{0,8},{8,16},{16,24},{24,28},{28,20},{20,12},{12,4},{4,0},{1,9},{9... | collective-permute-start | bytes 1572872 | tf_op jit(solution)/shard_map/ppermute | solution.py:58
  272.3 28.4 %collective-permute-start.46 = (bf16[256,1024]{1,0:T(8,128)(2,1)}, bf16[256,1024]{1,0:T(8,128)(2,1)}, u32[]{:S(2)}, u32[]{:S(2)}) collective-permute-start(bf16[256,1024]{1,0:T(8,128)(2,1)} %add_convert_fusion.16), channel_id=1, source_target_pairs={{0,1},{1,0},{2,3},{3,2},{4,5},{5,4},{6,7},{7,6},{8,9},{9,8},{10,11... | collective-permute-start | bytes 1572872 | tf_op jit(solution)/shard_map/ppermute | solution.py:49
  337.4 42.9 %collective-permute-start.61 = (bf16[256,1024]{1,0:T(8,128)(2,1)S(1)}, bf16[256,1024]{1,0:T(8,128)(2,1)S(1)}, u32[]{:S(2)}, u32[]{:S(2)}) collective-permute-start(bf16[256,1024]{1,0:T(8,128)(2,1)S(1)} %slice.1289), channel_id=1, source_target_pairs={{0,1},{1,0},{2,3},{3,2},{4,5},{5,4},{6,7},{7,6},{8,9},{9,8},{10,11... | collective-permute-start | bytes 1572872 | tf_op jit(solution)/shard_map/ppermute | solution.py:49
  391.5 39.5 %collective-permute-start.128 = (bf16[128,2048]{1,0:T(8,128)(2,1)}, bf16[128,2048]{1,0:T(8,128)(2,1)}, u32[]{:S(2)}, u32[]{:S(2)}) collective-permute-start(bf16[128,2048]{1,0:T(8,128)(2,1)} %add_convert_fusion.4), channel_id=1, source_target_pairs={{0,4},{8,0},{16,8},{24,16},{28,24},{20,28},{12,20},{4,12},{1,5},{9... | collective-permute-start | bytes 1572872 | tf_op jit(solution)/shard_map/ppermute | solution.py:63
  394.0 37.0 %collective-permute-start.124 = (bf16[128,2048]{1,0:T(8,128)(2,1)}, bf16[128,2048]{1,0:T(8,128)(2,1)}, u32[]{:S(2)}, u32[]{:S(2)}) collective-permute-start(bf16[128,2048]{1,0:T(8,128)(2,1)} %add_convert_fusion.6), channel_id=1, source_target_pairs={{0,8},{8,16},{16,24},{24,28},{28,20},{20,12},{12,4},{4,0},{1,9},{9... | collective-permute-start | bytes 1572872 | tf_op jit(solution)/shard_map/ppermute | solution.py:58
  454.2 67.8 %collective-permute-start.119 = (bf16[128,1536]{1,0:T(8,128)(2,1)}, bf16[128,1536]{1,0:T(8,128)(2,1)S(1)}, u32[]{:S(2)}, u32[]{:S(2)}) collective-permute-start(bf16[128,1536]{1,0:T(8,128)(2,1)} %add_convert_fusion.20), channel_id=1, source_target_pairs={{0,4},{8,0},{16,8},{24,16},{28,24},{20,28},{12,20},{4,12},{1,5},{9... | collective-permute-start | bytes 1179656 | tf_op jit(solution)/shard_map/ppermute | solution.py:63
  456.6 65.4 %collective-permute-start.115 = (bf16[128,1536]{1,0:T(8,128)(2,1)}, bf16[128,1536]{1,0:T(8,128)(2,1)S(1)}, u32[]{:S(2)}, u32[]{:S(2)}) collective-permute-start(bf16[128,1536]{1,0:T(8,128)(2,1)} %add_convert_fusion.22), channel_id=1, source_target_pairs={{0,8},{8,16},{16,24},{24,28},{28,20},{20,12},{12,4},{4,0},{1,9},{9... | collective-permute-start | bytes 1179656 | tf_op jit(solution)/shard_map/ppermute | solution.py:58
  499.8 26.6 %collective-permute-start.70 = (bf16[256,1024]{1,0:T(8,128)(2,1)}, bf16[256,1024]{1,0:T(8,128)(2,1)S(1)}, u32[]{:S(2)}, u32[]{:S(2)}) collective-permute-start(bf16[256,1024]{1,0:T(8,128)(2,1)} %slice.1304), channel_id=1, source_target_pairs={{0,1},{1,0},{2,3},{3,2},{4,5},{5,4},{6,7},{7,6},{8,9},{9,8},{10,11... | collective-permute-start | bytes 1572872 | tf_op jit(solution)/shard_map/ppermute | solution.py:49
  516.2 25.3 %collective-permute-start.108 = (bf16[128,2048]{1,0:T(8,128)(2,1)}, bf16[128,2048]{1,0:T(8,128)(2,1)}, u32[]{:S(2)}, u32[]{:S(2)}) collective-permute-start(bf16[128,2048]{1,0:T(8,128)(2,1)} %pad_maximum_fusion.21), channel_id=1, source_target_pairs={{0,4},{8,0},{16,8},{24,16},{28,24},{20,28},{12,20},{4,12},{1,5},{9... | collective-permute-start | bytes 1572872 | tf_op jit(solution)/shard_map/ppermute | solution.py:63
  529.2 29.0 %collective-permute-start.73 = (bf16[256,1024]{1,0:T(8,128)(2,1)}, bf16[256,1024]{1,0:T(8,128)(2,1)}, u32[]{:S(2)}, u32[]{:S(2)}) collective-permute-start(bf16[256,1024]{1,0:T(8,128)(2,1)} %get-tuple-element.130), channel_id=1, source_target_pairs={{0,2},{1,3},{2,0},{3,1},{4,6},{5,7},{6,4},{7,5},{8,10},{9,11},{10,... | collective-permute-start | bytes 1572872 | tf_op jit(solution)/shard_map/ppermute | solution.py:53
  542.7 26.3 %collective-permute-start.109 = (bf16[128,2048]{1,0:T(8,128)(2,1)S(1)}, bf16[128,2048]{1,0:T(8,128)(2,1)S(1)}, u32[]{:S(2)}, u32[]{:S(2)}) collective-permute-start(bf16[128,2048]{1,0:T(8,128)(2,1)S(1)} %add_convert_fusion.9), channel_id=1, source_target_pairs={{0,4},{8,0},{16,8},{24,16},{28,24},{20,28},{12,20},{4,12},{1,5},{9... | collective-permute-start | bytes 1572872 | tf_op jit(solution)/shard_map/ppermute | solution.py:63
  545.5 25.8 %collective-permute-start.105 = (bf16[128,2048]{1,0:T(8,128)(2,1)S(1)}, bf16[128,2048]{1,0:T(8,128)(2,1)S(1)}, u32[]{:S(2)}, u32[]{:S(2)}) collective-permute-start(bf16[128,2048]{1,0:T(8,128)(2,1)S(1)} %add_convert_fusion.11), channel_id=1, source_target_pairs={{0,8},{8,16},{16,24},{24,28},{28,20},{20,12},{12,4},{4,0},{1,9},{9... | collective-permute-start | bytes 1572872 | tf_op jit(solution)/shard_map/ppermute | solution.py:58
  553.6 67.4 %collective-permute-start.72 = (bf16[256,1024]{1,0:T(8,128)(2,1)}, bf16[256,1024]{1,0:T(8,128)(2,1)}, u32[]{:S(2)}, u32[]{:S(2)}) collective-permute-start(bf16[256,1024]{1,0:T(8,128)(2,1)} %slice.1306), channel_id=1, source_target_pairs={{0,1},{1,0},{2,3},{3,2},{4,5},{5,4},{6,7},{7,6},{8,9},{9,8},{10,11... | collective-permute-start | bytes 1572872 | tf_op jit(solution)/shard_map/ppermute | solution.py:49
  558.1 24.3 %collective-permute-start.74 = (bf16[256,1024]{1,0:T(8,128)(2,1)}, bf16[256,1024]{1,0:T(8,128)(2,1)}, u32[]{:S(2)}, u32[]{:S(2)}) collective-permute-start(bf16[256,1024]{1,0:T(8,128)(2,1)} %collective-permute-done.73), channel_id=1, source_target_pairs={{0,1},{1,0},{2,3},{3,2},{4,5},{5,4},{6,7},{7,6},{8,9},{9,8},{10,11... | collective-permute-start | bytes 1572872 | tf_op jit(solution)/shard_map/ppermute | solution.py:49
  570.0 34.3 %collective-permute-start.110 = (bf16[128,2048]{1,0:T(8,128)(2,1)}, bf16[128,2048]{1,0:T(8,128)(2,1)}, u32[]{:S(2)}, u32[]{:S(2)}) collective-permute-start(bf16[128,2048]{1,0:T(8,128)(2,1)} %add_convert_fusion.8), channel_id=1, source_target_pairs={{0,4},{8,0},{16,8},{24,16},{28,24},{20,28},{12,20},{4,12},{1,5},{9... | collective-permute-start | bytes 1572872 | tf_op jit(solution)/shard_map/ppermute | solution.py:63
  572.3 33.8 %collective-permute-start.106 = (bf16[128,2048]{1,0:T(8,128)(2,1)}, bf16[128,2048]{1,0:T(8,128)(2,1)}, u32[]{:S(2)}, u32[]{:S(2)}) collective-permute-start(bf16[128,2048]{1,0:T(8,128)(2,1)} %add_convert_fusion.10), channel_id=1, source_target_pairs={{0,8},{8,16},{16,24},{24,28},{28,20},{20,12},{12,4},{4,0},{1,9},{9... | collective-permute-start | bytes 1572872 | tf_op jit(solution)/shard_map/ppermute | solution.py:58
  604.3 31.5 %collective-permute-start.92 = (bf16[128,1024]{1,0:T(8,128)(2,1)}, bf16[128,1024]{1,0:T(8,128)(2,1)}, u32[]{:S(2)}, u32[]{:S(2)}) collective-permute-start(bf16[128,1024]{1,0:T(8,128)(2,1)} %pad_maximum_fusion.30), channel_id=1, source_target_pairs={{0,4},{8,0},{16,8},{24,16},{28,24},{20,28},{12,20},{4,12},{1,5},{9... | collective-permute-start | bytes 786440 | tf_op jit(solution)/shard_map/ppermute | solution.py:63
  617.3 23.6 %collective-permute-start.100 = (bf16[128,1024]{1,0:T(8,128)(2,1)}, bf16[128,1024]{1,0:T(8,128)(2,1)}, u32[]{:S(2)}, u32[]{:S(2)}) collective-permute-start(bf16[128,1024]{1,0:T(8,128)(2,1)} %pad_maximum_fusion.32), channel_id=1, source_target_pairs={{0,4},{8,0},{16,8},{24,16},{28,24},{20,28},{12,20},{4,12},{1,5},{9... | collective-permute-start | bytes 786440 | tf_op jit(solution)/shard_map/ppermute | solution.py:63
  646.0 24.3 %collective-permute-start.90 = (bf16[128,1024]{1,0:T(8,128)(2,1)}, bf16[128,1024]{1,0:T(8,128)(2,1)S(1)}, u32[]{:S(2)}, u32[]{:S(2)}) collective-permute-start(bf16[128,1024]{1,0:T(8,128)(2,1)} %get-tuple-element.174), channel_id=1, source_target_pairs={{0,8},{8,16},{16,24},{24,28},{28,20},{20,12},{12,4},{4,0},{1,9},{9... | collective-permute-start | bytes 786440 | tf_op jit(solution)/shard_map/ppermute | solution.py:58
  (276 other events, 3012.5 us)

commit v3 on v2

--- a/solution.py
+++ b/solution.py
@@ -45,6 +45,12 @@
     return s * (1.0 + h * (1.0 - s))
 
 
+def cost(micros):
+    return pl.CostEstimate(
+        flops=int(micros * 900_000_000), transcendentals=0, bytes_accessed=int(micros * 2_000_000)
+    )
+
+
 def to_core(v):
     return lax.ppermute(v, "tensor", [(m, m ^ 1) for m in range(lax.axis_size("tensor"))])
 
@@ -78,35 +84,30 @@
     return jnp.sum(jnp.where(turned[:, None] == jnp.arange(count)[None, :], ring[None, :], 0), axis=1)
 
 
-def after(values, signal):
-    return lax.optimization_barrier((values, signal))[0]
-
-
 def gather_rows(shard):
     if not on_ring():
-        return [lax.all_gather(shard, "dp", axis=0, tiled=True)], shard
+        return [lax.all_gather(shard, "dp", axis=0, tiled=True)], [(shard,)] * 3
     half = shard.shape[0] // 2
     r1, l1 = to_right(shard), to_left(shard)
     r2, l2 = to_right(r1), to_left(l1)
     r3, l3 = to_right(r2), to_left(l2)
     r4, l4 = to_right(r3[:half]), to_left(l3[half:])
-    return [shard, l1, l2, l3, r4, l4, r3, r2, r1], (r3[:8], l3[:8])
-
-
-def columns(pieces, start, stop):
-    return jnp.concatenate([p[:, start:stop] for p in pieces], axis=0)
-
-
-def scatter_rows(totals, signal):
+    return [shard, l1, l2, l3, r4, l4, r3, r2, r1], [(r1, l1), (r2, l2), (r3, l3)]
+
+
+def scatter_rows(totals, order):
     count = lax.axis_size("dp")
     rows = totals[0].shape[0] // count
     if not on_ring():
         total = jnp.concatenate(totals, axis=1)
-        return lax.psum_scatter(total, "dp", scatter_dimension=0, tiled=True).astype(f32), signal
+        return lax.psum_scatter(total, "dp", scatter_dimension=0, tiled=True).astype(f32)
     half = rows // 2
 
     def part(start, stop):
-        return jnp.concatenate([t[start:stop] for t in totals], axis=1)
+        at = order[start // rows] * rows + start % rows
+        return jnp.concatenate(
+            [lax.dynamic_slice_in_dim(t, at, stop - start) for t in totals], axis=1
+        )
 
     def block(k):
         return part(k * rows, (k + 1) * rows)
@@ -115,8 +116,6 @@
         return (a.astype(f32) + b.astype(f32)).astype(bf16)
 
     right, left = part(4 * rows, 4 * rows + half), part(4 * rows + half, 5 * rows)
-    if signal is not None:
-        right, left = after((right, left), signal)
     m = to_right(right)
     n = to_left(left)
     m = to_right(
@@ -131,20 +130,31 @@
     )
     m = to_right(plus(block(2), m))
     n = to_left(plus(block(6), n))
-    free = (m[:8], n[:8])
     m = to_right(plus(block(1), m))
     n = to_left(plus(block(7), n))
-    return block(0).astype(f32) + m.astype(f32) + n.astype(f32), free
-
-
-def sum_everywhere(value):
-    for axis in ("tensor", "dp"):
-        count = lax.axis_size(axis)
-        bit = 1
-        while bit < count:
-            value = value + lax.ppermute(value, axis, [(m, m ^ bit) for m in range(count)])
-            bit *= 2
-    return value
+    return block(0).astype(f32) + m.astype(f32) + n.astype(f32)
+
+
+def add_across(value, axis, bit):
+    count = lax.axis_size(axis)
+    return value + lax.ppermute(value, axis, [(m, m ^ bit) for m in range(count)])
+
+
+def sum_groups(value):
+    steps = [add_across(value, "tensor", 2)]
+    bit = 1
+    while bit < lax.axis_size("dp"):
+        steps.append(add_across(steps[-1], "dp", bit))
+        bit *= 2
+    return steps
+
+
+def gather_queued(shard):
+    return lax.all_gather(shard, "dp", axis=0, tiled=True)
+
+
+def scatter_queued(total):
+    return lax.psum_scatter(total, "dp", scatter_dimension=0, tiled=True).astype(f32)
 
 
 def gather_clip(mine):
@@ -163,38 +173,66 @@
     return jnp.concatenate([mine, near], axis=0), jnp.concatenate([far, to_core(far)], axis=0)
 
 
-def reduce_frames(own, other):
+def send_other(other):
+    rows = other.shape[0] // 2
+    other = other.astype(bf16)
+    near = to_core(other[rows:])
+    summed = (other[:rows].astype(f32) + near.astype(f32)).astype(bf16)
+    return to_far(summed), summed
+
+
+def reduce_own(own, far):
     rows = own.shape[0] // 2
-    own, other = own.astype(bf16), other.astype(bf16)
-    near = to_core(own[rows:])
-    near_other = to_core(other[rows:])
-    far = to_far((other[:rows].astype(f32) + near_other.astype(f32)).astype(bf16))
-    return own[:rows].astype(f32) + near.astype(f32) + far.astype(f32)
-
-
-def permute_blocks(values, order):
-    count = order.shape[0]
+    own = own.astype(bf16)
+    return own[:rows].astype(f32) + to_core(own[rows:]).astype(f32) + far.astype(f32)
+
+
+ANY = pl.BlockSpec(memory_space=pl.ANY)
+
+
+def after(values, tokens):
+    def body(*refs):
+        pass
+
+    tokens = list(tokens)
+    return pl.pallas_call(
+        body,
+        in_specs=[ANY] * (len(values) + len(tokens)),
+        out_specs=[ANY] * len(values),
+        out_shape=[jax.ShapeDtypeStruct(v.shape, v.dtype) for v in values],
+        input_output_aliases={n: n for n in range(len(values))},
+    )(*values, *tokens)
+
+
+def assemble(pieces, order, spans):
     if not on_ring():
-        return values
-    width = D // count
+        return [pieces[0][:, start:stop] for start, stop in spans]
+    block = pieces[0].shape[0]
+    half = block // 2
+    shapes = [
+        jax.ShapeDtypeStruct((block * order.shape[0], stop - start), pieces[0].dtype)
+        for start, stop in spans
+    ]
+    places = ((0, 0), (1, 0), (2, 0), (3, 0), (4, 0), (4, half), (5, 0), (6, 0), (7, 0))
 
     def body(order_ref, *refs):
-        ins, outs = refs[: len(values)], refs[len(values) :]
-        for src, dst in zip(ins, outs):
-            for k in range(count):
-                at = pl.multiple_of(order_ref[k] * width, width)
-                dst[:, k * width : (k + 1) * width] = src[:, pl.ds(at, width)]
+        ins, outs = refs[: len(pieces)], refs[len(pieces) :]
+        for src, (place, first) in zip(ins, places):
+            to = pl.multiple_of(order_ref[place] * block + first, half)
+            for dst, (start, stop) in zip(outs, spans):
+                dst[pl.ds(to, src.shape[0]), :] = src[:, start:stop]
 
     return pl.pallas_call(
         body,
         grid_spec=pltpu.PrefetchScalarGridSpec(
             num_scalar_prefetch=1,
             grid=(),
-            in_specs=[pl.BlockSpec(memory_space=pltpu.VMEM) for _ in values],
-            out_specs=[pl.BlockSpec(memory_space=pltpu.VMEM) for _ in values],
+            in_specs=[pl.BlockSpec(memory_space=pltpu.VMEM) for _ in pieces],
+            out_specs=[pl.BlockSpec(memory_space=pltpu.VMEM) for _ in spans],
         ),
-        out_shape=[jax.ShapeDtypeStruct(v.shape, v.dtype) for v in values],
-    )(order, *values)
+        out_shape=shapes,
+        cost_estimate=cost(4),
+    )(order, *pieces)
 
 
 def norm_forward(v, gain, shift):
@@ -217,22 +255,40 @@
 
 def ffn_forward(stream, gain, shift, up, down_t):
     normed, unit, r = norm_forward(stream, gain, shift)
-    frames = gather_frames(normed.astype(bf16))
-    hidden = [mm(x, up) for x in frames]
-    active = [swish(h).astype(bf16) for h in hidden]
-    branch = reduce_frames(*[mm_nt(a, down_t) for a in active])
-    return stream + 0.5 * branch, (unit, r, frames, hidden, active)
-
-
-def ffn_backward(upstream, gain, up, down_t, saved):
+    frames, other = gather_frames(normed.astype(bf16))
+
+    def half(x):
+        hidden = mm(x, up)
+        active = swish(hidden).astype(bf16)
+        return hidden, active, mm_nt(active, down_t)
+
+    hidden_other, active_other, part = half(other)
+    far, sent = send_other(part)
+    (frames,) = after([frames], [sent])
+    hidden, active, part = half(frames)
+    branch = reduce_own(part, far)
+    saved = (unit, r, (frames, other), (hidden, hidden_other), (active, active_other))
+    return stream + 0.5 * branch, saved
+
+
+def ffn_backward(upstream, gain, up, down_t, saved, wait):
     unit, r, frames, hidden, active = saved
-    incoming = gather_frames(upstream.astype(bf16))
-    dhidden = [
-        (0.5 * mm(g, down_t) * swish_grad(h)).astype(bf16) for g, h in zip(incoming, hidden)
-    ]
-    dnormed = reduce_frames(*[mm_nt(d, up) for d in dhidden])
-    grad_down = (0.5 * sum(mm_tn(g, a) for g, a in zip(incoming, active))).astype(bf16)
-    grad_up = sum(mm_tn(x, d) for x, d in zip(frames, dhidden)).astype(bf16)
+    incoming, other = gather_frames(upstream.astype(bf16))
+
+    def half(g, h):
+        d = (0.5 * mm(g, down_t) * swish_grad(h)).astype(bf16)
+        return d, mm_nt(d, up)
+
+    d_other, part = half(other, hidden[1])
+    far, sent = send_other(part)
+    (incoming,) = after([incoming], [sent])
+    d_own, part = half(incoming, hidden[0])
+    dnormed = reduce_own(part, far)
+    if wait:
+        *frames, active_own, active_other = after([*frames, *active], [sent])
+        active = active_own, active_other
+    grad_down = (0.5 * (mm_tn(incoming, active[0]) + mm_tn(other, active[1]))).astype(bf16)
+    grad_up = (mm_tn(frames[0], d_own) + mm_tn(frames[1], d_other)).astype(bf16)
     dstream, dgain, dshift = norm_backward(dnormed, unit, r, gain)
     return upstream + dstream, grad_up, grad_down, dgain, dshift
 
@@ -264,14 +320,15 @@
         by_row[:, :1],
         jnp.where(offset >= LANES - REL_LEFT, by_row[:, LANES - 1 :], turned),
     )
-    scores = (mm_nt(q, k) + relative) * SCALE
+    scores = mm_nt(q, k) + relative
     scores = jnp.where(place_j < length, scores, masked_score)
     raised = jnp.exp(scores - jnp.max(scores, axis=-1, keepdims=True))
-    return raised / jnp.sum(raised, axis=-1, keepdims=True), offset
-
-
-def attend_body(meta_ref, q_ref, k_ref, v_ref, table_ref, out_ref):
-    q, k, v, table = q_ref[...], k_ref[...], v_ref[...], table_ref[...]
+    return raised * (1.0 / jnp.sum(raised, axis=-1, keepdims=True)), offset
+
+
+def attend_body(meta_ref, q_ref, k_ref, v_ref, table_ref, *rest):
+    out_ref = rest[-1]
+    q, k, v, table = q_ref[...] * SCALE, k_ref[...], v_ref[...], table_ref[...]
     outs = []
     for upper in (False, True):
         shares, _ = tile_probs(meta_ref, head_lanes(q, upper), k, table)
@@ -279,32 +336,35 @@
     out_ref[...] = either(*outs).astype(bf16)
 
 
-def pair_specs(pairs):
+def pair_specs(pairs, first=0):
     def at(which):
-        return pl.BlockSpec((L, LANES), lambda n, meta: (0, which * pairs + n))
+        return pl.BlockSpec((L, LANES), lambda n, meta: (0, which * pairs + first + n))
 
     return [at(0), at(1), at(2)]
 
 
-def attend(qkv, table, meta):
-    width = qkv.shape[1] // 3
+def attend(qkv, table, meta, part, tokens):
+    width = qkv.shape[1] // 6
     pairs = width // LANES
     return pl.pallas_call(
         attend_body,
         grid_spec=pltpu.PrefetchScalarGridSpec(
             num_scalar_prefetch=1,
             grid=(pairs,),
-            in_specs=pair_specs(pairs) + [pl.BlockSpec((LANES, LANES), lambda n, meta: (0, 0))],
+            in_specs=pair_specs(2 * pairs, part * pairs)
+            + [pl.BlockSpec((LANES, LANES), lambda n, meta: (0, 0))]
+            + [ANY] * len(tokens),
             out_specs=pl.BlockSpec((L, LANES), lambda n, meta: (0, n)),
         ),
         out_shape=jax.ShapeDtypeStruct((L, width), bf16),
-    )(meta, qkv, qkv, qkv, table)
+        cost_estimate=cost(8),
+    )(meta, qkv, qkv, qkv, table, *tokens)
 
 
 def attend_back_body(
     meta_ref, q_ref, k_ref, v_ref, do_ref, table_ref, dq_ref, dk_ref, dv_ref, dtable_ref
 ):
-    q, k, v, do, table = q_ref[...], k_ref[...], v_ref[...], do_ref[...], table_ref[...]
+    q, k, v, do, table = q_ref[...] * SCALE, k_ref[...], v_ref[...], do_ref[...], table_ref[...]
     lane = lax.broadcasted_iota(jnp.int32, (L, LANES), 1)
     row = lax.broadcasted_iota(jnp.int32, (L, LANES), 0)
     dqs, dks, dvs = [], [], []
@@ -334,56 +394,60 @@
         dks.append(mm_tn(ds, q))
         dtable = dtable + mm_tn(pulled, q_one)
     dq_ref[...] = (either(*dqs) * SCALE).astype(bf16)
-    dk_ref[...] = (either(*dks) * SCALE).astype(bf16)
+    dk_ref[...] = either(*dks).astype(bf16)
     dv_ref[...] = either(*dvs).astype(bf16)
 
     @pl.when(pl.program_id(0) == 0)
     def _():
         dtable_ref[...] = jnp.zeros_like(dtable_ref)
 
-    dtable_ref[...] += dtable * SCALE
-
-
-def attend_back(qkv, dout, table, meta):
-    width = qkv.shape[1] // 3
+    dtable_ref[...] += dtable
+
+
+def attend_back(qkv, dout, table, meta, part, tokens):
+    width = qkv.shape[1] // 6
     pairs = width // LANES
     pair = pl.BlockSpec((L, LANES), lambda n, meta: (0, n))
+    pair_in = pl.BlockSpec((L, LANES), lambda n, meta: (0, part * pairs + n))
     square = pl.BlockSpec((LANES, LANES), lambda n, meta: (0, 0))
-    part = jax.ShapeDtypeStruct((L, width), bf16)
+    one = jax.ShapeDtypeStruct((L, width), bf16)
     return pl.pallas_call(
-        attend_back_body,
+        lambda *refs: attend_back_body(*refs[:6], *refs[6 + len(tokens) :]),
         grid_spec=pltpu.PrefetchScalarGridSpec(
             num_scalar_prefetch=1,
             grid=(pairs,),
-            in_specs=pair_specs(pairs) + [pair, square],
+            in_specs=pair_specs(2 * pairs, part * pairs) + [pair_in, square] + [ANY] * len(tokens),
             out_specs=[pair, pair, pair, square],
         ),
-        out_shape=[part, part, part, jax.ShapeDtypeStruct((LANES, LANES), f32)],
-    )(meta, qkv, qkv, qkv, dout, table)
-
-
-def attention_forward(stream, gain, shift, w_in, w_out_t, table, meta):
+        out_shape=[one, one, one, jax.ShapeDtypeStruct((LANES, LANES), f32)],
+        cost_estimate=cost(14),
+    )(meta, qkv, qkv, qkv, dout, table, *tokens)
+
+
+def attention_forward(stream, gain, shift, w_in, w_out_t, table, meta, signals):
     normed, unit, r = norm_forward(stream, gain, shift)
     frames = gather_clip(normed.astype(bf16))
     qkv = mm(frames, w_in).astype(bf16)
-    attended = attend(qkv, table, meta)
+    attended = [attend(qkv, table, meta, n, signals[n]) for n in (0, 1)]
+    attended = jnp.concatenate(attended, axis=1)
     branch = reduce_clip(mm_nt(attended, w_out_t))
     return stream + branch, (unit, r, frames, qkv, attended)
 
 
-def attention_backward(upstream, gain, w_in, w_out_t, table, meta, saved):
+def attention_backward(upstream, gain, w_in, w_out_t, table, meta, saved, signals):
     unit, r, frames, qkv, attended = saved
     incoming = gather_clip(upstream.astype(bf16))
     datt = mm(incoming, w_out_t).astype(bf16)
-    dq, dk, dv, dtable = attend_back(qkv, datt, table, meta)
-    width = dq.shape[1]
-    dnormed = reduce_clip(
-        sum(mm_nt(d, w_in[:, n * width : (n + 1) * width]) for n, d in enumerate((dq, dk, dv)))
-    )
-    grads = [mm_tn(frames, d).astype(bf16) for d in (dq, dk, dv)]
-    grads.append(mm_tn(incoming, attended).astype(bf16))
+    halves = [attend_back(qkv, datt, table, meta, n, signals[n]) for n in (0, 1)]
+    dqkv = jnp.concatenate([halves[n][which] for which in (0, 1, 2) for n in (0, 1)], axis=1)
+    dtable = halves[0][3] + halves[1][3]
+    dnormed = reduce_clip(mm_nt(dqkv, w_in))
     dstream, dgain, dshift = norm_backward(dnormed, unit, r, gain)
-    return upstream + dstream, grads, dtable, dgain, dshift
+    upstream = upstream + dstream
+    sent = upstream.astype(bf16)
+    frames, attended = after([frames, attended], [sent])
+    grads = [mm_tn(frames, dqkv).astype(bf16), mm_tn(incoming, attended).astype(bf16)]
+    return upstream, grads, dtable, dgain, dshift
 
 
 PAD = 32
@@ -417,7 +481,8 @@
     return at
 
 
-def conv_body(meta_ref, linear_ref, gate_ref, taps_ref, out_ref, padded, placed):
+def conv_body(meta_ref, linear_ref, gate_ref, taps_ref, *rest):
+    out_ref, padded, placed = rest[-3:]
     low = meta_ref[0]
     padded[:PAD, :] = jnp.zeros((PAD, LANES), f32)
     place_rows(padded, linear_ref[...] * jax.nn.sigmoid(gate_ref[...]), PAD, low)
@@ -476,7 +541,7 @@
     return linear, gate, taps
 
 
-def conv_gated(halves, taps, meta):
+def conv_gated(halves, taps, meta, tokens):
     width = halves.shape[1] // 2
     linear, gate, tap = conv_specs(width // LANES)
     return pl.pallas_call(
@@ -484,12 +549,13 @@
         grid_spec=pltpu.PrefetchScalarGridSpec(
             num_scalar_prefetch=1,
             grid=(width // LANES,),
-            in_specs=[linear, gate, tap],
+            in_specs=[linear, gate, tap] + [ANY] * len(tokens),
             out_specs=linear,
             scratch_shapes=[pltpu.VMEM((L + PAD, LANES), f32), pltpu.VMEM((L, LANES), f32)],
         ),
         out_shape=jax.ShapeDtypeStruct((L, width), f32),
-    )(meta, halves, halves, taps)
+        cost_estimate=cost(6),
+    )(meta, halves, halves, taps, *tokens)
 
 
 def conv_gated_back(dconv, halves, taps, meta):
@@ -510,6 +576,7 @@
             jax.ShapeDtypeStruct((L, width), bf16),
             jax.ShapeDtypeStruct((8 * PAD, width), f32),
         ],
+        cost_estimate=cost(10),
     )(meta, dconv, halves, halves, taps)
 
 
@@ -529,11 +596,11 @@
     return mean[:, None], lax.rsqrt(spread + norm_eps)[:, None]
 
 
-def conv_forward(stream, gain, shift, w_in, taps, w_out_t, cgain, cshift, meta):
+def conv_forward(stream, gain, shift, w_in, taps, w_out_t, cgain, cshift, meta, signal):
     normed, unit, r = norm_forward(stream, gain, shift)
     frames = gather_clip(normed.astype(bf16))
     halves = mm(frames, w_in)
-    convolved = conv_gated(halves, taps, meta)
+    convolved = conv_gated(halves, taps, meta, signal)
     mean, inverse = channel_stats(convolved)
     cunit = (convolved - mean) * inverse
     active = swish(cunit * cgain + cshift).astype(bf16)
@@ -558,11 +625,6 @@
     sums = (dtaps, jnp.sum(dmid * cunit, axis=0), jnp.sum(dmid, axis=0))
     dstream, dgain, dshift = norm_backward(dnormed, unit, r, gain)
     return upstream + dstream, grads, sums, dgain, dshift
-
-
-def spread_channels(part, member):
-    zero = jnp.zeros(part.shape[:-1] + (D,), f32)
-    return lax.dynamic_update_slice_in_dim(zero, part, member * part.shape[-1], part.ndim - 1)
 
 
 def per_device(
@@ -593,18 +655,7 @@
     channels = depthwise.shape[1]
 
     order = block_order()
-    count = order.shape[0]
-    inverse_order = jnp.sum(
-        jnp.where(
-            order[None, :] == jnp.arange(count, dtype=jnp.int32)[:, None],
-            jnp.arange(count, dtype=jnp.int32)[None, :],
-            0,
-        ),
-        axis=1,
-    )
-    stream, cotangent, gains, shifts = permute_blocks(
-        [layer_in, output_grad, norm_gain, norm_shift], order
-    )
+    gains, shifts = norm_gain, norm_shift
 
     slot = group * CLIP_DEV + high
     length = jnp.sum(jnp.where(clip_slots == slot, clip_lengths, 0))
@@ -633,7 +684,6 @@
     )
     pack_conv = jnp.concatenate([pointwise_in.reshape(block, -1), pointwise_out.T], axis=1)
     far_attend = to_far(pack_attend)
-    far_conv = to_far(pack_conv)
     taps = jnp.concatenate([depthwise, to_far(depthwise)], axis=1).astype(f32)
     taps = jnp.pad(taps, ((0, PAD - KERNEL), (0, 0)))
 
@@ -644,49 +694,60 @@
         return jnp.concatenate(parts, axis=1)
 
     both = 2 * channels
-    p_early_up, signal = gather_rows(early_up)
-    p_early_down, signal = gather_rows(after(early_down.T, signal))
-    p_attend, signal = gather_rows(after(paired(pack_attend, far_attend), signal))
-    p_conv, signal = gather_rows(after(paired(pack_conv, far_conv), signal))
-    p_late, signal = gather_rows(after(jnp.concatenate([late_up, late_down.T], axis=1), signal))
     hidden_cols = early_up.shape[1]
-    w_early_up = columns(p_early_up, 0, hidden_cols)
-    w_early_down = columns(p_early_down, 0, hidden_cols)
-    w_att_in, w_att_out = columns(p_attend, 0, 3 * both), columns(p_attend, 3 * both, 4 * both)
-    w_pi, w_po = columns(p_conv, 0, 2 * both), columns(p_conv, 2 * both, 3 * both)
-    w_late_up = columns(p_late, 0, hidden_cols)
-    w_late_down = columns(p_late, hidden_cols, 2 * hidden_cols)
-
-    stream0 = stream.astype(f32)
+    p_early, signals = gather_rows(jnp.concatenate([early_up, early_down.T], axis=1))
+    p_attend, signals_attend = gather_rows(paired(pack_attend, far_attend))
+    shard_conv, shard_up = after([pack_conv, late_up], signals[2])
+    w_conv = gather_queued(shard_conv)
+    w_late_up = gather_queued(shard_up)
+    p_late_down, signals = gather_rows(after([late_down.T], signals_attend[2])[0])
+    (w_late_down,) = assemble(p_late_down, order, [(0, hidden_cols)])
+    w_early_up, w_early_down = assemble(
+        p_early, order, [(0, hidden_cols), (hidden_cols, 2 * hidden_cols)]
+    )
+    w_att_in, w_att_out = assemble(p_attend, order, [(0, 3 * both), (3 * both, 4 * both)])
+    far_conv = to_far(w_conv)
+    w_conv = paired(w_conv, far_conv)
+    w_pi, w_po = w_conv[:, : 2 * both], w_conv[:, 2 * both :]
+
+    stream0 = layer_in.astype(f32)
     stream1, saved_early = ffn_forward(stream0, gains[0], shifts[0], w_early_up, w_early_down)
     stream2, saved_attend = attention_forward(
-        stream1, gains[1], shifts[1], w_att_in, w_att_out, table, meta
+        stream1, gains[1], shifts[1], w_att_in, w_att_out, table, meta, [signals[0], [*signals[1], far_conv]]
     )
     stream3, saved_conv = conv_forward(
-        stream2, gains[2], shifts[2], w_pi, taps, w_po, cgain, cshift, meta
+        stream2, gains[2], shifts[2], w_pi, taps, w_po, cgain, cshift, meta, [*signals[2], w_late_up]
     )
     stream4, saved_late = ffn_forward(stream3, gains[4], shifts[4], w_late_up, w_late_down)
     result, unit5, r5 = norm_forward(stream4, gains[5], shifts[5])
 
-    up = jnp.where(live[:, None], cotangent.astype(f32), 0.0)
+    up = jnp.where(live[:, None], output_grad.astype(f32), 0.0)
     up, gain5, shift5 = norm_backward(up, unit5, r5, gains[5])
     up, g_late_up, g_late_down, gain4, shift4 = ffn_backward(
-        up, gains[4], w_late_up, w_late_down, saved_late
-    )
-    g_late, signal = scatter_rows([g_late_up, g_late_down], None)
+        up, gains[4], w_late_up, w_late_down, saved_late, True
+    )
+    g_late_up = scatter_queued(g_late_up)
+    g_late_down = scatter_queued(g_late_down)
     up, g_conv, (g_taps, gain3, shift3), gain2, shift2 = conv_backward(
         up, gains[2], w_pi, taps, w_po, cgain, cshift, meta, saved_conv
     )
-    g_conv, signal = scatter_rows(g_conv, signal)
+    norms = jnp.stack([gain2, gain4, gain5, shift2, shift4, shift5]).reshape(-1, both)
+    side = jnp.concatenate([g_taps, gain3[None], shift3[None]], axis=0)
+    side = jnp.where(high == 0, side, jnp.roll(side, channels, axis=1))
+    steps = sum_groups(jnp.concatenate([norms, side], axis=0))
+    own, far = [
+        jnp.concatenate([g[:, at : at + channels] for g in g_conv], axis=1) for at in (0, channels)
+    ]
+    g_conv = scatter_queued((own.astype(f32) + to_far(far).astype(f32)).astype(bf16))
     up, g_attend, g_table, gain1, shift1 = attention_backward(
-        up, gains[1], w_att_in, w_att_out, table, meta, saved_attend
-    )
-    g_attend, signal = scatter_rows(g_attend, signal)
+        up, gains[1], w_att_in, w_att_out, table, meta, saved_attend, [(), [steps[1]]]
+    )
+    g_attend = scatter_rows(g_attend, order)
     up, g_early_up, g_early_down, gain0, shift0 = ffn_backward(
-        up, gains[0], w_early_up, w_early_down, saved_early
-    )
-    g_early_down, signal = scatter_rows([g_early_down], signal)
-    g_early_up, signal = scatter_rows([g_early_up], signal)
+        up, gains[0], w_early_up, w_early_down, saved_early, False
+    )
+    g_early_down = scatter_rows([g_early_down], order)
+    g_early_up = scatter_rows([g_early_up], order)
 
     def own_and_far(grad):
         own = [grad[:, at : at + channels] for at in range(0, grad.shape[1], both)]
@@ -695,31 +756,30 @@
         return [o + far[:, n * channels : (n + 1) * channels] for n, o in enumerate(own)]
 
     g_q, g_k, g_v, g_out = own_and_far(g_attend)
-    g_linear, g_gate, g_po = own_and_far(g_conv)
-
-    result, norms = permute_blocks(
-        [
-            result.astype(bf16),
-            jnp.stack([gain1, gain2, gain4, gain5, shift1, shift2, shift4, shift5]),
-        ],
-        inverse_order,
-    )
-    up, first = permute_blocks([up, jnp.stack([gain0, shift0] + [jnp.zeros((D,), f32)] * 6)], inverse_order)
-    side = jnp.concatenate([g_taps, gain3[None], shift3[None]], axis=0)
-    side = spread_channels(side[:, :channels], member) + spread_channels(side[:, channels:], far_member)
+    g_linear, g_gate, g_po = [g_conv[:, at : at + channels] for at in (0, channels, both)]
+
+    result = result.astype(bf16)
     g_table = g_table[:, :HEAD_DIM] + g_table[:, HEAD_DIM:]
     g_table = jnp.concatenate(
         [g_table[: RELS - 1], jnp.sum(g_table[RELS - 1 :], axis=0, keepdims=True)], axis=0
     )
     g_table = jnp.dot(selector.T, g_table, precision=highest)
     g_table = jnp.pad(g_table.reshape(-1), (0, 5 * D - RELS * HEAD_DIM)).reshape(5, D)
-    sums = sum_everywhere(jnp.concatenate([norms, side, g_table], axis=0))
-    first = sum_everywhere(first[:2])
-    after_side = 8 + side.shape[0]
-    side = sums[8:after_side]
-    gains_all = jnp.concatenate([first[:1], sums[0:2], side[KERNEL : KERNEL + 1], sums[2:4]], axis=0)
-    shifts_all = jnp.concatenate([first[1:], sums[4:6], side[KERNEL + 1 :], sums[6:8]], axis=0)
-    table_all = sums[after_side:].reshape(-1)[: RELS * HEAD_DIM].reshape(RELS, HEAD_DIM)
+    last = sum_groups(jnp.concatenate([jnp.stack([gain0, gain1, shift0, shift1]), g_table], axis=0))
+    last = add_across(last[-1], "tensor", 1)
+    sums, near = steps[-1], to_core(steps[-1])
+    count = norms.shape[0]
+    norms = (sums[:count] + near[:count]).reshape(-1, D)
+    first = jnp.where(low == 0, sums[count:], near[count:])
+    second = jnp.where(low == 0, near[count:], sums[count:])
+    side = jnp.concatenate(
+        [part[:, at : at + channels] for at in (0, channels) for part in (first, second)], axis=1
+    )
+    gains_all = jnp.concatenate(
+        [last[0:2], norms[0:1], side[KERNEL : KERNEL + 1], norms[1:3]], axis=0
+    )
+    shifts_all = jnp.concatenate([last[2:4], norms[3:4], side[KERNEL + 1 :], norms[4:6]], axis=0)
+    table_all = last[4:].reshape(-1)[: RELS * HEAD_DIM].reshape(RELS, HEAD_DIM)
 
     return (
         result,
@@ -734,8 +794,8 @@
         jnp.stack([g_linear, g_gate], axis=1),
         side[:KERNEL],
         g_po.T,
-        g_late[:, :hidden_cols],
-        g_late[:, hidden_cols:].T,
+        g_late_up,
+        g_late_down.T,
     )
 
 

time: 685 us -> 593 us (0.87)
  local copies, waits for them, and re-layouts: 155 us -> 60 us
  starting transfers between devices: 114 us -> 82.2 us
  between operations: 3.96 us -> 22.2 us
  waiting for transfers between devices: 157 us -> 170 us
  Pallas kernels: 68.8 us -> 79.7 us
  other arithmetic: 89.5 us -> 82.1 us
    slice x84 -> x23, local copies, waits for them, and re-layouts: 62 us -> 10.3 us  [the longest x3 4.13 us: per_device(): g[:, at:at + channels]]
    concatenate x8 -> x2, local copies, waits for them, and re-layouts: 39.2 us -> 0.16 us  [the longest x1 0.14 us: per_device(): jnp.concatenate([jnp.stack([gain0, gain1, shift0, shift1]), g_table], axi...]
    ppermute x40 -> x24, starting transfers between devices: 59.9 us -> 29 us  [to_left(): lax.ppermute(v, 'dp', [(RING[i], RING[(i - 1) % n]) for i in range(n)])]
    all_gather x0 -> x2, waiting for transfers between devices: none -> 11.7 us  [gather_queued(): return lax.all_gather(shard, 'dp', axis=0, tiled=True)]
    concatenate x10 -> x13, other arithmetic: 4.49 us -> 14.5 us  [the longest x4 6.28 us: gather_frames(): jnp.concatenate([mine, near], axis=0)]
    ppermute x40 -> x24, waiting for transfers between devices: 61.9 us -> 51.9 us  [to_left(): lax.ppermute(v, 'dp', [(RING[i], RING[(i - 1) % n]) for i in range(n)])]
    dot_general x12, matrix products: 32.5 us -> 41.3 us  [mm(): return jnp.dot(a, b, preferred_element_type=f32)]
    pallas_call x4 -> x13, Pallas kernels: 36.4 us -> 45 us  [the longest x2 31.2 us: attend_back(): pl.pallas_call(lambda *refs: attend_back_body(*refs[:6], *refs[6 + len(to...]
  transfers between devices with their start and end apart: 129 -> 102, of which waited for: 38 -> 40; matrix products, arithmetic and copies ran while one was open for 46% -> 33% of each run, Pallas kernels for 10% -> 13%
where the time goes in v3:
time: 593 us; the launch traced here: 583 us
  waiting for transfers between devices  170 us (29%)
  matrix products  87.3 us (15%)
  starting transfers between devices  82.2 us (14%)
  other arithmetic  82.1 us (14%)
  Pallas kernels  79.7 us (13%)
  local copies, waits for them, and re-layouts  60 us (10%)
  between operations  22.2 us (4%)
    ppermute x24, waiting for transfers between devices, to_left(): lax.ppermute(v, 'dp', [(RING[i], RING[(i - 1) % n]) for i in range(n)])  51.9 us
    ppermute x13, waiting for transfers between devices, to_far(): lax.ppermute(v, 'tensor', [(m, m ^ 2) for m in range(lax.axis_size('tenso...  44.2 us
    dot_general x12, matrix products, mm(): return jnp.dot(a, b, preferred_element_type=f32)  41.3 us
    unnamed x361, local copies, waits for them, and re-layouts  36.9 us
    ppermute x24, waiting for transfers between devices, to_right(): lax.ppermute(v, 'dp', [(RING[i], RING[(i + 1) % n]) for i in range(n)])  34.6 us
    pallas_call x2, Pallas kernels, attend_back(): pl.pallas_call(lambda *refs: attend_back_body(*refs[:6], *refs[6 + len(to...  31.2 us
    ppermute x24, starting transfers between devices, to_left(): lax.ppermute(v, 'dp', [(RING[i], RING[(i - 1) % n]) for i in range(n)])  29 us
    dot_general x13, matrix products, mm_tn(): lax.dot_general(a, b, (((0,), (0,)), ((), ())), preferred_element_type=f32)  24.1 us
  transfers between devices with their start and end apart: 102, of which 40 were waited for; matrix products, arithmetic and copies ran while one was open for 33% of the time, Pallas kernels for 13%

profile of v3, /device:TPU:0, one launch (start us, length us, event | category | flops | bytes accessed | tf_op | source)
XLA Modules:
  0.0 583.2 jit_solution(8637505986505743609)
XLA Ops:
  18.4 5.6 collective-permute-done.15
  30.1 9.4 %collective-permute-done.4.refs_2_ = bf16[128,2048]{1,0:T(8,128)(2,1)} collective-permute-done((bf16[128,2048]{1,0:T(8,128)(2,1)S(1)}, bf16[128,2048]{1,0:T(8,128)(2,1)}, u32[]{:S(2)}, u32[]{:S(2)}) %collective-permute-start.4) | collective-permute-done | bytes 524320 | tf_op jit(solution)/shard_map/ppermute | solution.py:69
  46.1 9.8 %collective-permute-done.8.refs_6_.refs_2_ = bf16[128,2048]{1,0:T(8,128)(2,1)S(1)} collective-permute-done((bf16[128,2048]{1,0:T(8,128)(2,1)}, bf16[128,2048]{1,0:T(8,128)(2,1)S(1)}, u32[]{:S(2)}, u32[]{:S(2)}) %collective-permute-start.8) | collective-permute-done | bytes 524320 | tf_op jit(solution)/shard_map/ppermute | solution.py:64
  59.9 5.9 %collective-permute-done.16.refs_1_ = bf16[128,2048]{1,0:T(8,128)(2,1)} collective-permute-done((bf16[128,2048]{1,0:T(8,128)(2,1)}, bf16[128,2048]{1,0:T(8,128)(2,1)}, u32[]{:S(2)}, u32[]{:S(2)}) %collective-permute-start.16) | collective-permute-done | bytes 524320 | tf_op jit(solution)/shard_map/ppermute | solution.py:69
  70.9 5.1 shard_map.281
  91.0 3.3 fusion.107
  96.7 6.0 %collective-permute-done.18.refs_3_.refs_2_ = bf16[128,2048]{1,0:T(8,128)(2,1)S(1)} collective-permute-done((bf16[128,2048]{1,0:T(8,128)(2,1)}, bf16[128,2048]{1,0:T(8,128)(2,1)S(1)}, u32[]{:S(2)}, u32[]{:S(2)}) %collective-permute-start.18) | collective-permute-done | bytes 524320 | tf_op jit(solution)/shard_map/ppermute | solution.py:69
  114.7 6.7 %collective-permute-done.22.refs_4_ = bf16[64,2048]{1,0:T(8,128)(2,1)S(1)} collective-permute-done((bf16[64,2048]{1,0:T(8,128)(2,1)S(1)}, bf16[64,2048]{1,0:T(8,128)(2,1)S(1)}, u32[]{:S(2)}, u32[]{:S(2)}) %collective-permute-start.22) | collective-permute-done | bytes 262176 | tf_op jit(solution)/shard_map/ppermute | solution.py:64
  122.1 11.7 %all-gather.3.cloned.1.call-done = bf16[1024,768]{1,0:T(8,128)(2,1)} async-done(((bf16[128,768]{1,0:T(8,128)(2,1)}), bf16[1024,768]{1,0:T(8,128)(2,1)}) %all-gather.3.cloned.1.call-update) | async-done | bytes 1572880 | tf_op jit(solution)/shard_map/all_gather | solution.py:153
  139.3 5.1 shard_map.283
  144.4 5.0 convolution_convert_fusion.1.q_ref.k_ref.v_ref.refs_1_.refs_2_.refs_3_
  149.5 9.2 %shard_map.285 = bf16[512,256]{1,0:T(8,128)(2,1)} custom-call(s32[2]{0:T(128)} %pad_add_fusion.meta_ref.refs_0_, bf16[512,1536]{1,0:T(8,128)(2,1)} %convolution_convert_fusion.1.q_ref.k_ref.v_ref.refs_1_.refs_2_.refs_3_, bf16[512,1536]{1,0:T(8,128)(2,1)} %convolution_convert_fusion.1.q_ref.k_ref.v_ref.refs_1_.refs_2_.refs_3_, ...), custom_call_target="tpu_custom_call" | custom-call | flops 7200000000 | bytes 16000000 | tf_op jit(solution)/shard_map/pallas_call | solution.py:349
  158.7 10.5 %collective-permute-done.28.rest_2_ = bf16[1024,768]{1,0:T(8,128)(2,1)S(1)} collective-permute-done((bf16[1024,768]{1,0:T(8,128)(2,1)}, bf16[1024,768]{1,0:T(8,128)(2,1)S(1)}, u32[]{:S(2)}, u32[]{:S(2)}) %collective-permute-start.28) | collective-permute-done | bytes 1572896 | tf_op jit(solution)/shard_map/ppermute | solution.py:59
  170.3 9.2 %shard_map.287 = bf16[512,256]{1,0:T(8,128)(2,1)} custom-call(s32[2]{0:T(128)} %pad_add_fusion.meta_ref.refs_0_, bf16[512,1536]{1,0:T(8,128)(2,1)} %convolution_convert_fusion.1.q_ref.k_ref.v_ref.refs_1_.refs_2_.refs_3_, bf16[512,1536]{1,0:T(8,128)(2,1)} %convolution_convert_fusion.1.q_ref.k_ref.v_ref.refs_1_.refs_2_.refs_3_, ...), custom_call_target="tpu_custom_call" | custom-call | flops 7200000000 | bytes 16000000 | tf_op jit(solution)/shard_map/pallas_call | solution.py:349
  196.5 6.3 %shard_map.288 = f32[512,512]{1,0:T(8,128)} custom-call(s32[2]{0:T(128)} %pad_add_fusion.meta_ref.refs_0_, f32[512,1024]{1,0:T(8,128)} %fusion.linear_ref.gate_ref, f32[512,1024]{1,0:T(8,128)} %fusion.linear_ref.gate_ref, f32[32,512]{1,0:T(8,128)} %fusion.49.taps_ref, bf16[128,1024]{1,0:T(8,128)(2,1)} %copy-done.111, ...), custom_call_target="tpu_custom_call" | custom-call | flops 5400000000 | bytes 12000000 | tf_op jit(solution)/shard_map/pallas_call | solution.py:547
  217.6 9.4 %collective-permute-done.37 = bf16[256,1024]{1,0:T(8,128)(2,1)} collective-permute-done((bf16[256,1024]{1,0:T(8,128)(2,1)S(1)}, bf16[256,1024]{1,0:T(8,128)(2,1)}, u32[]{:S(2)}, u32[]{:S(2)}) %collective-permute-start.37) | collective-permute-done | bytes 524320 | tf_op jit(solution)/shard_map/ppermute | solution.py:59
  227.6 3.6 shard_map.289
  233.9 4.7 multiply_convert_fusion.7
  244.5 4.8 multiply_convert_fusion.6
  252.4 4.9 collective-permute-done.43
  261.9 11.6 %collective-permute-done.45 = bf16[256,1024]{1,0:T(8,128)(2,1)S(1)} collective-permute-done((bf16[256,1024]{1,0:T(8,128)(2,1)S(1)}, bf16[256,1024]{1,0:T(8,128)(2,1)S(1)}, u32[]{:S(2)}, u32[]{:S(2)}) %collective-permute-start.45) | collective-permute-done | bytes 524320 | tf_op jit(solution)/shard_map/ppermute | solution.py:59
  290.1 4.3 multiply_convert_fusion.4
  308.5 3.4 fusion.84
  325.3 10.0 %shard_map.292 = (bf16[512,512]{1,0:T(8,128)(2,1)}, bf16[512,512]{1,0:T(8,128)(2,1)}, f32[256,512]{1,0:T(8,128)}) custom-call(s32[2]{0:T(128)} %pad_add_fusion.meta_ref.refs_0_, f32[512,512]{1,0:T(8,128)} %subtract_multiply_fusion.dconv_ref, f32[512,1024]{1,0:T(8,128)} %fusion.linear_ref.gate_ref, f32[512,1024]{1,0:T(8,128)} %fusion.linear_ref.gate_ref, ...), custom_call_target="tpu_custom_call" | custom-call | flops 8999999488 | bytes 20000000 | tf_op jit(solution)/shard_map/pallas_call | solution.py:565
  372.7 15.4 %shard_map.293 = (bf16[512,256]{1,0:T(8,128)(2,1)}, bf16[512,256]{1,0:T(8,128)(2,1)}, bf16[512,256]{1,0:T(8,128)(2,1)}, f32[128,128]{1,0:T(8,128)}) custom-call(s32[2]{0:T(128)} %pad_add_fusion.meta_ref.refs_0_, bf16[512,1536]{1,0:T(8,128)(2,1)} %convolution_convert_fusion.1.q_ref.k_ref.v_ref.refs_1_.refs_2_.refs_3_, ...), custom_call_target="tpu_custom_call" | custom-call | flops 12600000512 | bytes 28000000 | tf_op jit(solution)/shard_map/pallas_call | solution.py:414
  388.2 15.8 %shard_map.294 = (bf16[512,256]{1,0:T(8,128)(2,1)}, bf16[512,256]{1,0:T(8,128)(2,1)}, bf16[512,256]{1,0:T(8,128)(2,1)}, f32[128,128]{1,0:T(8,128)}) custom-call(s32[2]{0:T(128)} %pad_add_fusion.meta_ref.refs_0_, bf16[512,1536]{1,0:T(8,128)(2,1)} %convolution_convert_fusion.1.q_ref.k_ref.v_ref.refs_1_.refs_2_.refs_3_, ...), custom_call_target="tpu_custom_call" | custom-call | flops 12600000512 | bytes 28000000 | tf_op jit(solution)/shard_map/pallas_call | solution.py:414
  406.2 4.3 convolution_convert_fusion.4
  444.3 15.7 %collective-permute-done.92 = bf16[128,2048]{1,0:T(8,128)(2,1)S(1)} collective-permute-done((bf16[128,2048]{1,0:T(8,128)(2,1)S(1)}, bf16[128,2048]{1,0:T(8,128)(2,1)S(1)}, u32[]{:S(2)}, u32[]{:S(2)}) %collective-permute-start.92) | collective-permute-done | bytes 524320 | tf_op jit(solution)/shard_map/ppermute | solution.py:69
  469.7 5.9 %collective-permute-done.93 = bf16[128,2048]{1,0:T(8,128)(2,1)S(1)} collective-permute-done((bf16[128,2048]{1,0:T(8,128)(2,1)S(1)}, bf16[128,2048]{1,0:T(8,128)(2,1)S(1)}, u32[]{:S(2)}, u32[]{:S(2)}) %collective-permute-start.93) | collective-permute-done | bytes 524320 | tf_op jit(solution)/shard_map/ppermute | solution.py:69
  485.8 4.3 multiply_convert_fusion.2
  533.0 5.9 %collective-permute-done.64 = f32[9,1024]{1,0:T(8,128)S(1)} collective-permute-done((f32[9,1024]{1,0:T(8,128)S(1)}, f32[9,1024]{1,0:T(8,128)S(1)}, u32[]{:S(2)}, u32[]{:S(2)}) %collective-permute-start.64) | collective-permute-done | bytes 36896 | tf_op jit(solution)/shard_map/ppermute | solution.py:140
  557.5 3.4 collective-permute-done.77
  (789 shorter events, 324.8 us)
Async XLA Ops:
  7.2 126.6 %all-gather.3.cloned.1.call-start = ((), (), s32[]{:S(2)}) async-start(), calls=%async_computation.3 | async-start | bytes 1769472 | tf_op jit(solution)/shard_map/all_gather | solution.py:153
  17.6 27.2 %collective-permute-start.1 = (bf16[256,1024]{1,0:T(8,128)(2,1)S(1)}, bf16[256,1024]{1,0:T(8,128)(2,1)}, u32[]{:S(2)}, u32[]{:S(2)}) collective-permute-start(bf16[256,1024]{1,0:T(8,128)(2,1)S(1)} %fusion.15), channel_id=1, source_target_pairs={{0,2},{1,3},{2,0},{3,1},{4,6},{5,7},{6,4},{7,5},{8,10},{9,11},{10,... | collective-permute-start | bytes 1572872 | tf_op jit(solution)/shard_map/ppermute | solution.py:59
  42.8 23.0 %collective-permute-start.16 = (bf16[128,2048]{1,0:T(8,128)(2,1)}, bf16[128,2048]{1,0:T(8,128)(2,1)}, u32[]{:S(2)}, u32[]{:S(2)}) collective-permute-start(bf16[128,2048]{1,0:T(8,128)(2,1)} %slice_dynamic-update-slice_fusion.refs_0_), channel_id=1, source_target_pairs={{0,4},{8,0},{16,8},{24,16},{28,24},{20,28},{12,20},{4,12},{1,5},{9... | collective-permute-start | bytes 1572872 | tf_op jit(solution)/shard_map/ppermute | solution.py:69
  44.2 22.8 %collective-permute-start.19 = (bf16[128,2048]{1,0:T(8,128)(2,1)}, bf16[128,2048]{1,0:T(8,128)(2,1)}, u32[]{:S(2)}, u32[]{:S(2)}) collective-permute-start(bf16[128,2048]{1,0:T(8,128)(2,1)} %slice_dynamic-update-slice_fusion.refs_0_), channel_id=1, source_target_pairs={{0,8},{8,16},{16,24},{24,28},{28,20},{20,12},{12,4},{4,0},{1,9},{9... | collective-permute-start | bytes 1572872 | tf_op jit(solution)/shard_map/ppermute | solution.py:64
  44.8 23.8 %collective-permute-start.2 = (bf16[256,1024]{1,0:T(8,128)(2,1)}, bf16[256,1024]{1,0:T(8,128)(2,1)}, u32[]{:S(2)}, u32[]{:S(2)}) collective-permute-start(bf16[256,1024]{1,0:T(8,128)(2,1)} %collective-permute-done.1), channel_id=1, source_target_pairs={{0,1},{1,0},{2,3},{3,2},{4,5},{5,4},{6,7},{7,6},{8,9},{9,8},{10,11... | collective-permute-start | bytes 1572872 | tf_op jit(solution)/shard_map/ppermute | solution.py:55
  65.8 18.1 %collective-permute-start = (bf16[256,1024]{1,0:T(8,128)(2,1)S(1)}, bf16[256,1024]{1,0:T(8,128)(2,1)}, u32[]{:S(2)}, u32[]{:S(2)}) collective-permute-start(bf16[256,1024]{1,0:T(8,128)(2,1)S(1)} %fusion.15), channel_id=1, source_target_pairs={{0,1},{1,0},{2,3},{3,2},{4,5},{5,4},{6,7},{7,6},{8,9},{9,8},{10,11... | collective-permute-start | bytes 1572872 | tf_op jit(solution)/shard_map/ppermute | solution.py:55
  67.0 19.0 %collective-permute-start.17 = (bf16[128,2048]{1,0:T(8,128)(2,1)}, bf16[128,2048]{1,0:T(8,128)(2,1)}, u32[]{:S(2)}, u32[]{:S(2)}) collective-permute-start(bf16[128,2048]{1,0:T(8,128)(2,1)} %collective-permute-done.16.refs_1_), channel_id=1, source_target_pairs={{0,4},{8,0},{16,8},{24,16},{28,24},{20,28},{12,20},{4,12},{1,5},{9... | collective-permute-start | bytes 1572872 | tf_op jit(solution)/shard_map/ppermute | solution.py:69
  68.6 19.0 %collective-permute-start.20 = (bf16[128,2048]{1,0:T(8,128)(2,1)}, bf16[128,2048]{1,0:T(8,128)(2,1)}, u32[]{:S(2)}, u32[]{:S(2)}) collective-permute-start(bf16[128,2048]{1,0:T(8,128)(2,1)} %collective-permute-done.19.refs_8_), channel_id=1, source_target_pairs={{0,8},{8,16},{16,24},{24,28},{28,20},{20,12},{12,4},{4,0},{1,9},{9... | collective-permute-start | bytes 1572872 | tf_op jit(solution)/shard_map/ppermute | solution.py:64
  88.1 108.5 %all-gather.5.cloned.1.call-start = ((), (), s32[]{:S(2)}) async-start(), calls=%async_computation.4 | async-start | bytes 2359296 | tf_op jit(solution)/shard_map/all_gather | solution.py:153
  89.4 20.6 %collective-permute-start.13 = (bf16[256,1024]{1,0:T(8,128)(2,1)S(1)}, bf16[256,1024]{1,0:T(8,128)(2,1)}, u32[]{:S(2)}, u32[]{:S(2)}) collective-permute-start(bf16[256,1024]{1,0:T(8,128)(2,1)S(1)} %add_convert_fusion.15.refs_1_), channel_id=1, source_target_pairs={{0,2},{1,3},{2,0},{3,1},{4,6},{5,7},{6,4},{7,5},{8,10},{9,11},{10,... | collective-permute-start | bytes 1572872 | tf_op jit(solution)/shard_map/ppermute | solution.py:59
  104.8 31.8 %collective-permute-start.24 = (bf16[128,1024]{1,0:T(8,128)(2,1)}, bf16[128,1024]{1,0:T(8,128)(2,1)}, u32[]{:S(2)}, u32[]{:S(2)}) collective-permute-start(bf16[128,1024]{1,0:T(8,128)(2,1)} %shard_map.284.refs_0_), channel_id=1, source_target_pairs={{0,8},{8,16},{16,24},{24,28},{28,20},{20,12},{12,4},{4,0},{1,9},{9... | collective-permute-start | bytes 786440 | tf_op jit(solution)/shard_map/ppermute | solution.py:64
  106.0 32.8 %collective-permute-start.25 = (bf16[128,1024]{1,0:T(8,128)(2,1)}, bf16[128,1024]{1,0:T(8,128)(2,1)}, u32[]{:S(2)}, u32[]{:S(2)}) collective-permute-start(bf16[128,1024]{1,0:T(8,128)(2,1)} %shard_map.284.refs_0_), channel_id=1, source_target_pairs={{0,4},{8,0},{16,8},{24,16},{28,24},{20,28},{12,20},{4,12},{1,5},{9... | collective-permute-start | bytes 786440 | tf_op jit(solution)/shard_map/ppermute | solution.py:69
  110.0 29.2 %collective-permute-start.23 = (bf16[64,2048]{1,0:T(8,128)(2,1)S(1)}, bf16[64,2048]{1,0:T(8,128)(2,1)}, u32[]{:S(2)}, u32[]{:S(2)}) collective-permute-start(bf16[64,2048]{1,0:T(8,128)(2,1)S(1)} %slice.559), channel_id=1, source_target_pairs={{0,4},{8,0},{16,8},{24,16},{28,24},{20,28},{12,20},{4,12},{1,5},{9... | collective-permute-start | bytes 786440 | tf_op jit(solution)/shard_map/ppermute | solution.py:69
  113.9 30.5 %collective-permute-start.14 = (bf16[256,1024]{1,0:T(8,128)(2,1)S(1)}, bf16[256,1024]{1,0:T(8,128)(2,1)}, u32[]{:S(2)}, u32[]{:S(2)}) collective-permute-start(bf16[256,1024]{1,0:T(8,128)(2,1)S(1)} %add_convert_fusion.14), channel_id=1, source_target_pairs={{0,1},{1,0},{2,3},{3,2},{4,5},{5,4},{6,7},{7,6},{8,9},{9,8},{10,11... | collective-permute-start | bytes 1572872 | tf_op jit(solution)/shard_map/ppermute | solution.py:55
  133.8 35.4 %collective-permute-start.28 = (bf16[1024,768]{1,0:T(8,128)(2,1)}, bf16[1024,768]{1,0:T(8,128)(2,1)S(1)}, u32[]{:S(2)}, u32[]{:S(2)}) collective-permute-start(bf16[1024,768]{1,0:T(8,128)(2,1)} %all-gather.3.cloned.1.call-done), channel_id=1, source_target_pairs={{0,2},{1,3},{2,0},{3,1},{4,6},{5,7},{6,4},{7,5},{8,10},{9,11},{10,... | collective-permute-start | bytes 4718600 | tf_op jit(solution)/shard_map/ppermute | solution.py:59
  136.5 343.5 %reduce-scatter.8.cloned.1.call-start = ((), (), s32[]{:S(2)}) async-start(), calls=%async_computation.6 | async-start | bytes 2359296 | tf_op jit(solution)/shard_map/reduce_scatter | solution.py:157
  136.6 22.1 %collective-permute-start.26 = (bf16[128,1024]{1,0:T(8,128)(2,1)}, bf16[128,1024]{1,0:T(8,128)(2,1)}, u32[]{:S(2)}, u32[]{:S(2)}) collective-permute-start(bf16[128,1024]{1,0:T(8,128)(2,1)} %collective-permute-done.24.rest_0_.refs_8_), channel_id=1, source_target_pairs={{0,8},{8,16},{16,24},{24,28},{28,20},{20,12},{12,4},{4,0},{1,9},{9... | collective-permute-start | bytes 786440 | tf_op jit(solution)/shard_map/ppermute | solution.py:64
  138.8 19.8 %collective-permute-start.27 = (bf16[128,1024]{1,0:T(8,128)(2,1)}, bf16[128,1024]{1,0:T(8,128)(2,1)}, u32[]{:S(2)}, u32[]{:S(2)}) collective-permute-start(bf16[128,1024]{1,0:T(8,128)(2,1)} %collective-permute-done.25.rest_1_.refs_1_), channel_id=1, source_target_pairs={{0,4},{8,0},{16,8},{24,16},{28,24},{20,28},{12,20},{4,12},{1,5},{9... | collective-permute-start | bytes 786440 | tf_op jit(solution)/shard_map/ppermute | solution.py:69
  288.5 193.6 %reduce-scatter.6.cloned.1.call-start = ((), (), s32[]{:S(2)}) async-start(), calls=%async_computation.5 | async-start | bytes 2359296 | tf_op jit(solution)/shard_map/reduce_scatter | solution.py:157
  316.7 256.9 %reduce-scatter.10.cloned.1.call-start = ((), (), s32[]{:S(2)}) async-start(), calls=%async_computation.7 | async-start | bytes 1769472
  353.2 77.0 %collective-permute-start.96 = (bf16[1024,768]{0,1:T(8,128)(2,1)}, bf16[1024,768]{0,1:T(8,128)(2,1)}, u32[]{:S(2)}, u32[]{:S(2)}) collective-permute-start(bf16[1024,768]{0,1:T(8,128)(2,1)} %pad_maximum_fusion), channel_id=1, source_target_pairs={{0,2},{1,3},{2,0},{3,1},{4,6},{5,7},{6,4},{7,5},{8,10},{9,11},{10,... | collective-permute-start | bytes 4718600 | tf_op jit(solution)/shard_map/ppermute | solution.py:59
  418.6 22.5 %collective-permute-start.58 = (bf16[256,1024]{1,0:T(8,128)(2,1)S(1)}, bf16[256,1024]{1,0:T(8,128)(2,1)}, u32[]{:S(2)}, u32[]{:S(2)}) collective-permute-start(bf16[256,1024]{1,0:T(8,128)(2,1)S(1)} %get-tuple-element.142.refs_2_), channel_id=1, source_target_pairs={{0,2},{1,3},{2,0},{3,1},{4,6},{5,7},{6,4},{7,5},{8,10},{9,11},{10,... | collective-permute-start | bytes 1572872 | tf_op jit(solution)/shard_map/ppermute | solution.py:59
  419.3 21.9 %collective-permute-start.57 = (bf16[256,1024]{1,0:T(8,128)(2,1)S(1)}, bf16[256,1024]{1,0:T(8,128)(2,1)}, u32[]{:S(2)}, u32[]{:S(2)}) collective-permute-start(bf16[256,1024]{1,0:T(8,128)(2,1)S(1)} %get-tuple-element.142.refs_2_), channel_id=1, source_target_pairs={{0,1},{1,0},{2,3},{3,2},{4,5},{5,4},{6,7},{7,6},{8,9},{9,8},{10,11... | collective-permute-start | bytes 1572872 | tf_op jit(solution)/shard_map/ppermute | solution.py:55
  437.8 22.2 %collective-permute-start.92 = (bf16[128,2048]{1,0:T(8,128)(2,1)S(1)}, bf16[128,2048]{1,0:T(8,128)(2,1)S(1)}, u32[]{:S(2)}, u32[]{:S(2)}) collective-permute-start(bf16[128,2048]{1,0:T(8,128)(2,1)S(1)} %pad_maximum_fusion.18), channel_id=1, source_target_pairs={{0,4},{8,0},{16,8},{24,16},{28,24},{20,28},{12,20},{4,12},{1,5},{9... | collective-permute-start | bytes 1572872 | tf_op jit(solution)/shard_map/ppermute | solution.py:69
  441.0 21.8 %collective-permute-start.88 = (bf16[128,2048]{1,0:T(8,128)(2,1)S(1)}, bf16[128,2048]{1,0:T(8,128)(2,1)S(1)}, u32[]{:S(2)}, u32[]{:S(2)}) collective-permute-start(bf16[128,2048]{1,0:T(8,128)(2,1)S(1)} %maximum_maximum_fusion), channel_id=1, source_target_pairs={{0,8},{8,16},{16,24},{24,28},{28,20},{20,12},{12,4},{4,0},{1,9},{9... | collective-permute-start | bytes 1572872 | tf_op jit(solution)/shard_map/ppermute | solution.py:64
  441.1 24.4 %collective-permute-start.59 = (bf16[256,1024]{1,0:T(8,128)(2,1)}, bf16[256,1024]{1,0:T(8,128)(2,1)S(1)}, u32[]{:S(2)}, u32[]{:S(2)}) collective-permute-start(bf16[256,1024]{1,0:T(8,128)(2,1)} %collective-permute-done.58), channel_id=1, source_target_pairs={{0,1},{1,0},{2,3},{3,2},{4,5},{5,4},{6,7},{7,6},{8,9},{9,8},{10,11... | collective-permute-start | bytes 1572872 | tf_op jit(solution)/shard_map/ppermute | solution.py:55
  476.5 32.2 %collective-permute-start.94 = (bf16[128,2048]{1,0:T(8,128)(2,1)}, bf16[128,2048]{1,0:T(8,128)(2,1)}, u32[]{:S(2)}, u32[]{:S(2)}) collective-permute-start(bf16[128,2048]{1,0:T(8,128)(2,1)} %add_convert_fusion.4), channel_id=1, source_target_pairs={{0,4},{8,0},{16,8},{24,16},{28,24},{20,28},{12,20},{4,12},{1,5},{9... | collective-permute-start | bytes 1572872 | tf_op jit(solution)/shard_map/ppermute | solution.py:69
  480.0 30.1 %collective-permute-start.90 = (bf16[128,2048]{1,0:T(8,128)(2,1)}, bf16[128,2048]{1,0:T(8,128)(2,1)}, u32[]{:S(2)}, u32[]{:S(2)}) collective-permute-start(bf16[128,2048]{1,0:T(8,128)(2,1)} %add_convert_fusion.6), channel_id=1, source_target_pairs={{0,8},{8,16},{16,24},{24,28},{28,20},{20,12},{12,4},{4,0},{1,9},{9... | collective-permute-start | bytes 1572872 | tf_op jit(solution)/shard_map/ppermute | solution.py:64
  484.8 38.4 %collective-permute-start.62 = (bf16[256,1024]{1,0:T(8,128)(2,1)}, bf16[256,1024]{1,0:T(8,128)(2,1)}, u32[]{:S(2)}, u32[]{:S(2)}) collective-permute-start(bf16[256,1024]{1,0:T(8,128)(2,1)} %add_convert_fusion.8.refs_1_), channel_id=1, source_target_pairs={{0,2},{1,3},{2,0},{3,1},{4,6},{5,7},{6,4},{7,5},{8,10},{9,11},{10,... | collective-permute-start | bytes 1572872 | tf_op jit(solution)/shard_map/ppermute | solution.py:59
  508.6 41.1 %collective-permute-start.76 = (bf16[128,1024]{1,0:T(8,128)(2,1)}, bf16[128,1024]{1,0:T(8,128)(2,1)}, u32[]{:S(2)}, u32[]{:S(2)}) collective-permute-start(bf16[128,1024]{1,0:T(8,128)(2,1)} %pad_maximum_fusion.25), channel_id=1, source_target_pairs={{0,4},{8,0},{16,8},{24,16},{28,24},{20,28},{12,20},{4,12},{1,5},{9... | collective-permute-start | bytes 786440 | tf_op jit(solution)/shard_map/ppermute | solution.py:69
  516.5 26.9 %collective-permute-start.84 = (bf16[128,1024]{1,0:T(8,128)(2,1)}, bf16[128,1024]{1,0:T(8,128)(2,1)}, u32[]{:S(2)}, u32[]{:S(2)}) collective-permute-start(bf16[128,1024]{1,0:T(8,128)(2,1)} %pad_maximum_fusion.27), channel_id=1, source_target_pairs={{0,4},{8,0},{16,8},{24,16},{28,24},{20,28},{12,20},{4,12},{1,5},{9... | collective-permute-start | bytes 786440 | tf_op jit(solution)/shard_map/ppermute | solution.py:69
  523.3 26.5 %collective-permute-start.73 = (bf16[128,1024]{1,0:T(8,128)(2,1)}, bf16[128,1024]{1,0:T(8,128)(2,1)}, u32[]{:S(2)}, u32[]{:S(2)}) collective-permute-start(bf16[128,1024]{1,0:T(8,128)(2,1)} %add_convert_fusion.25), channel_id=1, source_target_pairs={{0,8},{8,16},{16,24},{24,28},{28,20},{20,12},{12,4},{4,0},{1,9},{9... | collective-permute-start | bytes 786440 | tf_op jit(solution)/shard_map/ppermute | solution.py:64
  (234 other events, 1896.3 us)
Sparse Core Ops, SparseCore 0:
  88.2 45.5 all-gather.2
  136.6 48.0 all-gather.4
  288.6 68.4 reduce-scatter.7
  360.5 67.5 reduce-scatter.5
  434.2 70.0 reduce-scatter.9
